TPU v7x, 256 devices: a whole 4x4x8 slice. The times are simulated.
256 devices in a mesh: ctx: 64 (over z, x, core), dp: 4 (over y).
Axes of the slice: x: 4, y: 4, z: 8, core: 2. Of those that a mesh axis runs over, the one named last changes fastest.
Arguments:
- query_policy: bfloat16 [4, 2, 8192, 2048], P('dp', None, 'ctx'), may hold values from -6 to 6
- key_policy: bfloat16 [4, 2, 8192, 512], P('dp', None, 'ctx'), may hold values from -6 to 6
- value_policy: bfloat16 [4, 2, 8192, 512], P('dp', None, 'ctx'), may hold values from -60 to 60
- query_reference: bfloat16 [4, 2, 8192, 2048], P('dp', None, 'ctx'), may hold values from -6 to 6
- key_reference: bfloat16 [4, 2, 8192, 512], P('dp', None, 'ctx'), may hold values from -6 to 6
- value_reference: bfloat16 [4, 2, 8192, 512], P('dp', None, 'ctx'), may hold values from -60 to 60
- readout: bfloat16 [4, 2, 8192, 2048], P('dp', None, 'ctx'), may hold values from -0.0029296875 to 0.0029296875
- response_mask: int32 [4, 2, 8192], P('dp', None, 'ctx'), may hold values from 0 to 1, as said below
Outputs:
- query_gradient_rows: bfloat16 [4, 2, 8192, 2048], P('dp', None, 'ctx')
- key_gradient_rows: bfloat16 [4, 2, 8192, 512], P('dp', None, 'ctx')
- value_gradient_rows: bfloat16 [4, 2, 8192, 512], P('dp', None, 'ctx')
- pair_loss: float32 [], replicated
Inputs may be any that keep to these rules, and one draw needn't show every extreme that they name: `response_mask`: in each pair the mask is 1 exactly from the prompt's end (1 to 2048, the same for both sequences) up to but excluding the sequence's own end (4096 to 8192).
All inputs are finite; a program needn't handle non-finite values.
Results may differ from a plain program's by a relative error of at most 0.018.
Values may be sent and summed in bfloat16 or wider, within the bound.
No kernel may reach another device: no remote copies, remote signals or barrier semaphores. Data moves between devices by JAX's collectives and lax.ppermute only.
A program may use at most 192 MiB of HBM per device.

v0:
```python
import math

import jax
import jax.numpy as jnp
from jax import lax
from jax.sharding import PartitionSpec as P

HEADS = 16
KV_HEADS = 4
D_HEAD = 128


dpo_beta = 0.5
epsilon = 1e-06


def carried_in(x, axis, join, neutral, backward):
    count = lax.axis_size(axis)
    place = lax.axis_index(axis)
    ahead = count - 1 - place if backward else place
    gathered = lax.all_gather(x.astype(jnp.bfloat16), axis)
    state = jnp.zeros_like(x) + jnp.asarray(neutral, x.dtype)

    def one(turn, state):
        source = count - 1 - turn if backward else turn
        return join(state, lax.dynamic_index_in_dim(gathered, source, 0, False).astype(x.dtype))

    return lax.fori_loop(0, ahead, one, state)


def add_states(earlier, following):
    return earlier + following


def causal_mask(block_rows):
    positions = jnp.arange(block_rows)
    return positions[:, None] >= positions[None, :]


def span_state(key_head_rows, value_head_rows):
    return jnp.einsum(
        "asgd,asge->agde", key_head_rows, value_head_rows, preferred_element_type=jnp.float32
    )


def span_forward(query_head_rows, key_head_rows, value_head_rows, carried):
    causal = causal_mask(query_head_rows.shape[1])
    pair_score_rows = jnp.einsum(
        "atgrd,asgd->agrts", query_head_rows, key_head_rows, preferred_element_type=jnp.float32
    )
    pair_score_rows = jnp.where(causal, pair_score_rows, 0.0).astype(jnp.bfloat16)
    carried_low = carried.astype(jnp.bfloat16)
    unnormed_output = jnp.einsum(
        "agrts,asgd->atgrd", pair_score_rows, value_head_rows, preferred_element_type=jnp.float32
    )
    unnormed_output = unnormed_output + jnp.einsum(
        "atgrd,agde->atgre", query_head_rows, carried_low, preferred_element_type=jnp.float32
    )
    inverse = lax.rsqrt(
        jnp.mean(unnormed_output * unnormed_output, axis=-1, keepdims=True) + epsilon
    )
    return (pair_score_rows, carried_low, unnormed_output * inverse, inverse)


def shards(
    query_policy,
    key_policy,
    value_policy,
    query_reference,
    key_reference,
    value_reference,
    readout,
    response_mask,
):
    block_rows = query_policy.shape[2]
    per_group = HEADS // KV_HEADS

    def split_query(array):
        return array.reshape(2, block_rows, KV_HEADS, per_group, D_HEAD)

    def split_shared(array):
        return array.reshape(2, block_rows, KV_HEADS, D_HEAD)

    query_pol = split_query(query_policy)
    key_pol = split_shared(key_policy)
    value_pol = split_shared(value_policy)
    query_ref = split_query(query_reference)
    key_ref = split_shared(key_reference)
    value_ref = split_shared(value_reference)
    states_policy = span_state(key_pol, value_pol)
    states_reference = span_state(key_ref, value_ref)
    carried_policy = carried_in(
        states_policy, "ctx", add_states, jnp.zeros_like(states_policy), False
    )
    carried_reference = carried_in(
        states_reference, "ctx", add_states, jnp.zeros_like(states_reference), False
    )
    scores_policy, carried_policy_low, normed_policy, inverse_policy = span_forward(
        query_pol, key_pol, value_pol, carried_policy
    )
    normed_reference = span_forward(query_ref, key_ref, value_ref, carried_reference)[2]
    read_heads = split_query(readout)
    mask_rows = response_mask.reshape(2, block_rows).astype(jnp.float32)
    policy_tokens = jnp.sum(normed_policy * read_heads, axis=(2, 3, 4))
    reference_tokens = jnp.sum(normed_reference * read_heads, axis=(2, 3, 4))
    sums = jnp.stack(
        [jnp.sum(mask_rows * policy_tokens, axis=1), jnp.sum(mask_rows * reference_tokens, axis=1)]
    )
    totals = lax.psum(sums, "ctx")
    delta = totals[0, 0] - totals[0, 1] - (totals[1, 0] - totals[1, 1])
    pair_loss = lax.psum(jax.nn.softplus(-dpo_beta * delta), "dp") / lax.axis_size("dp")
    scale = math.sqrt(HEADS * D_HEAD * block_rows * lax.axis_size("ctx"))
    pull = dpo_beta * jax.nn.sigmoid(-dpo_beta * delta) * scale
    weights = jnp.stack([-pull, pull])
    upstream = (weights[:, None] * mask_rows)[:, :, None, None, None] * read_heads
    pulled_back_state = upstream - normed_policy * jnp.mean(
        upstream * normed_policy, axis=-1, keepdims=True
    )
    pulled_back_state = (pulled_back_state * inverse_policy).astype(jnp.bfloat16)
    block_grad = jnp.einsum(
        "atgrd,atgre->agde", query_pol, pulled_back_state, preferred_element_type=jnp.float32
    )
    later = carried_in(block_grad, "ctx", add_states, jnp.zeros_like(block_grad), True)
    later_low = later.astype(jnp.bfloat16)
    causal = causal_mask(block_rows)
    score_gradient = jnp.einsum(
        "atgre,asge->agrts", pulled_back_state, value_pol, preferred_element_type=jnp.float32
    )
    score_gradient = jnp.where(causal, score_gradient, 0.0).astype(jnp.bfloat16)
    query_gradient_rows = jnp.einsum(
        "agrts,asgd->atgrd", score_gradient, key_pol, preferred_element_type=jnp.float32
    )
    query_gradient_rows = query_gradient_rows + jnp.einsum(
        "atgre,agde->atgrd",
        pulled_back_state,
        carried_policy_low,
        preferred_element_type=jnp.float32,
    )
    key_gradient_rows = jnp.einsum(
        "agrts,atgrd->asgd", score_gradient, query_pol, preferred_element_type=jnp.float32
    )
    key_gradient_rows = key_gradient_rows + jnp.einsum(
        "asge,agde->asgd", value_pol, later_low, preferred_element_type=jnp.float32
    )
    value_gradient_rows = jnp.einsum(
        "agrts,atgre->asge", scores_policy, pulled_back_state, preferred_element_type=jnp.float32
    )
    value_gradient_rows = value_gradient_rows + jnp.einsum(
        "asgd,agde->asge", key_pol, later_low, preferred_element_type=jnp.float32
    )
    return (
        query_gradient_rows.reshape(1, 2, block_rows, HEADS * D_HEAD).astype(jnp.bfloat16),
        key_gradient_rows.reshape(1, 2, block_rows, KV_HEADS * D_HEAD).astype(jnp.bfloat16),
        value_gradient_rows.reshape(1, 2, block_rows, KV_HEADS * D_HEAD).astype(jnp.bfloat16),
        pair_loss,
    )


def solution(mesh):
    placed = (
        P("dp", None, "ctx", None),
        P("dp", None, "ctx", None),
        P("dp", None, "ctx", None),
        P("dp", None, "ctx", None),
        P("dp", None, "ctx", None),
        P("dp", None, "ctx", None),
        P("dp", None, "ctx", None),
        P("dp", None, "ctx"),
    )
    return jax.shard_map(
        shards,
        mesh=mesh,
        in_specs=placed,
        out_specs=(
            P("dp", None, "ctx", None),
            P("dp", None, "ctx", None),
            P("dp", None, "ctx", None),
            P(),
        ),
        check_vma=False,
    )
```

profile of v0, /device:TPU:1, one launch (start us, length us, event | category | flops | bytes accessed | tf_op | source)
XLA Modules:
  0.0 600.7 jit_solution(8161237302858355317)
XLA Ops:
  8.3 1.1 reshape.127
  13.5 2.0 reshape.129
  15.5 3.0 copy.51
  18.5 1.5 fusion.2
  20.1 95.2 %all-gather.7.cloned.1.call-done = bf16[128,4,128,128]{3,2,1,0:T(8,128)(2,1)} async-done(((bf16[2,4,128,128]{3,2,1,0:T(8,128)(2,1)}), bf16[128,4,128,128]{3,2,1,0:T(8,128)(2,1)}) %all-gather.7.cloned.1.call-update) | async-done | bytes 16777232 | tf_op jit(solution)/shard_map/all_gather | solution.py:21
  115.3 1.1 while.32
  115.4 1.1 convert_add_fusion.6
  116.5 1.8 fusion.18
  118.3 97.1 %all-gather.9.cloned.1.call-done = bf16[128,4,128,128]{3,2,1,0:T(8,128)(2,1)} async-done(((bf16[2,4,128,128]{3,2,1,0:T(8,128)(2,1)}), bf16[128,4,128,128]{3,2,1,0:T(8,128)(2,1)}) %all-gather.9.cloned.1.call-update) | async-done | bytes 16777232 | tf_op jit(solution)/shard_map/all_gather | solution.py:21
  215.4 1.1 while.33
  215.5 1.1 convert_add_fusion.7
  216.6 1.8 fusion.13
  219.7 4.1 multiply_reduce_fusion.2
  223.8 2.8 multiply_reduce_fusion.3
  226.8 188.1 %psum.14 = f32[2,2]{1,0:T(2,128)S(1)} all-reduce(f32[2,2]{1,0:T(2,128)S(1)} %pad_maximum_fusion), channel_id=1, replica_groups=mesh['ctx'=64,'dp'=4] {'ctx'}, use_global_device_ids=true, to_apply=%region_10.11 | all-reduce | flops 4 | bytes 32 | tf_op jit(solution)/shard_map/psum | solution.py:109
  418.3 2.3 multiply_reduce_fusion
  423.8 9.0 %psum.15 = f32[]{:T(128)} all-reduce(f32[]{:T(128)S(6)} %select_n.32), channel_id=1, replica_groups=mesh['ctx'=64,'dp'=4] {'dp'}, use_global_device_ids=true, to_apply=%region_14.15 | all-reduce | flops 1 | bytes 8 | tf_op jit(solution)/shard_map/psum | solution.py:111
  432.7 1.7 fusion.3
  435.0 1.2 copy-done.6
  436.1 1.5 fusion
  437.6 2.4 copy.69
  440.6 2.6 convolution_bitcast_fusion.1
  443.7 78.9 %all-gather.11.cloned.1.call-done = bf16[128,4,128,128]{3,2,1,0:T(8,128)(2,1)} async-done(((bf16[2,4,128,128]{3,2,1,0:T(8,128)(2,1)}), bf16[128,4,128,128]{3,2,1,0:T(8,128)(2,1)}) %all-gather.11.cloned.1.call-update) | async-done | bytes 16777232 | tf_op jit(solution)/shard_map/all_gather | solution.py:21
  522.6 68.1 %while.34 = (s32[]{:T(128)}, f32[2,4,128,128]{3,2,1,0:T(8,128)S(1)}, s32[]{:T(128)}, bf16[64,2,4,128,128]{4,3,2,1,0:T(8,128)(2,1)}, s32[]{:T(128)}, /*index=5*/s32[]{:T(128)}, s32[]{:T(128)}, s32[]{:T(128)}) while((s32[]{:T(128)}, f32[2,4,128,128]{3,2,1,0:T(8,128)S(1)}, s32[]{:T(128)}, bf16[64,2,4,128,128]{4,3,2,1,0:T(8,128)(2,1)}, ...), condition=%wide.region_13.14_spmd, body=%wide.region_12.13_spmd.sunk | while | flops 262150 | bytes 1310855 | solution.py:28
  522.6 1.1 convert_add_fusion.8
  523.8 1.1 convert_add_fusion.8
  524.9 1.1 convert_add_fusion.8
  526.0 1.1 convert_add_fusion.8
  527.1 1.1 convert_add_fusion.8
  528.1 1.1 convert_add_fusion.8
  532.5 1.1 convert_add_fusion.8
  533.6 1.1 convert_add_fusion.8
  534.7 1.1 convert_add_fusion.8
  535.8 1.1 convert_add_fusion.8
  536.9 1.1 convert_add_fusion.8
  538.0 1.1 convert_add_fusion.8
  542.4 1.1 convert_add_fusion.8
  543.5 1.1 convert_add_fusion.8
  544.6 1.1 convert_add_fusion.8
  545.7 1.1 convert_add_fusion.8
  546.8 1.1 convert_add_fusion.8
  547.9 1.1 convert_add_fusion.8
  549.0 1.1 convert_add_fusion.8
  553.4 1.1 convert_add_fusion.8
  554.5 1.1 convert_add_fusion.8
  555.6 1.1 convert_add_fusion.8
  556.7 1.1 convert_add_fusion.8
  557.8 1.1 convert_add_fusion.8
  (109 shorter events, 54.4 us)
Async XLA Ops:
  7.2 3.3 copy-start.16
  7.2 3.4 copy-start.13
  7.2 108.1 %all-gather.7.cloned.1.call-start = ((), (), s32[]{:S(2)}) async-start(), calls=%async_computation | async-start | bytes 17039360 | tf_op jit(solution)/shard_map/all_gather | solution.py:21
  8.3 4.2 copy-start.12
  10.4 205.0 %all-gather.9.cloned.1.call-start = ((), (), s32[]{:S(2)}) async-start(), calls=%async_computation.1 | async-start | bytes 17039360 | tf_op jit(solution)/shard_map/all_gather | solution.py:21
  11.7 510.8 %all-gather.11.cloned.1.call-start = ((), (), s32[]{:S(2)}) async-start(), calls=%async_computation.2 | async-start | bytes 17039360 | tf_op jit(solution)/shard_map/all_gather | solution.py:21
  13.3 103.2 %copy-start.1 = (bf16[2,128,4,4,128]{4,3,2,1,0:T(4,128)(2,1)}, bf16[2,128,4,4,128]{4,3,2,1,0:T(4,128)(2,1)S(1)}, u32[]{:S(2)}) copy-start(bf16[2,128,4,4,128]{4,3,2,1,0:T(4,128)(2,1)S(1)} %reshape.126) | copy-start | bytes 3145732
  13.5 5.1 copy-start.14
  15.5 201.0 %copy-start.4 = (bf16[2,128,4,4,128]{4,3,2,1,0:T(4,128)(2,1)}, bf16[2,128,4,4,128]{4,3,2,1,0:T(4,128)(2,1)S(1)}, u32[]{:S(2)}) copy-start(bf16[2,128,4,4,128]{4,3,2,1,0:T(4,128)(2,1)S(1)} %reshape.129) | copy-start | bytes 3145732
  216.6 1.8 copy-start.7
  216.6 2.6 copy-start.10
  223.8 2.8 copy-start.17
  418.3 2.3 copy-start
  420.6 1.6 copy-start.2
  421.3 1.0 copy-start.5
  422.7 11.8 %copy-start.15 = (bf16[2,128,4,128,1]{1,3,4,2,0:T(8,128)(2,1)S(1)}, bf16[2,128,4,128,1]{1,3,4,2,0:T(8,128)(2,1)}, u32[]{:S(2)}) copy-start(bf16[2,128,4,128,1]{1,3,4,2,0:T(8,128)(2,1)} %copy-done.14) | copy-start | bytes 786436
  434.5 3.1 copy-start.8
  434.5 1.6 copy-start.6
  437.6 5.6 copy-start.3
  440.6 2.6 copy-start.9
  522.6 68.1 %copy-start.11 = (f32[2,4,128,128]{3,2,1,0:T(8,128)S(1)}, f32[2,4,128,128]{3,2,1,0:T(8,128)}, u32[]{:S(2)}) copy-start(f32[2,4,128,128]{3,2,1,0:T(8,128)} %convolution_bitcast_fusion.1) | copy-start | bytes 1572868
Sparse Core Ops, SparseCore 0:
  11.4 103.9 all-gather.6
  118.7 96.7 all-gather.8
  423.7 98.8 all-gather.10
where the time goes:
time: 605 us; the launch traced here: 601 us
  waiting for transfers between devices  271 us (45%)
  blocking collectives  197 us (33%)
  other arithmetic  74.6 us (12%)
  matrix products  19.5 us (3%)
  between operations  18.7 us (3%)
  local copies, waits for them, and re-layouts  17.8 us (3%)
    all_gather x3, waiting for transfers between devices, carried_in(): gathered = lax.all_gather(x.astype(jnp.bfloat16), axis)  271 us
    psum x1, blocking collectives, shards(): totals = lax.psum(sums, 'ctx')  188 us
    add x64, other arithmetic, add_states(): return earlier + following  68.5 us
  transfers between devices with their start and end apart: 3, of which 3 were waited for; matrix products, arithmetic and copies ran while one was open for 4% of the time, Pallas kernels for 0%

commit v1 on v0

v1 whole, which is shorter than its diff:
```python
import math

import jax
import jax.numpy as jnp
from jax import lax
from jax.experimental import pallas as pl
from jax.experimental.pallas import tpu as pltpu
from jax.sharding import Mesh, PartitionSpec as P

HEADS = 16
KV_HEADS = 4
GROUP = HEADS // KV_HEADS
D = 128
T = 128
DPO_BETA = 0.5
EPS = 1e-06
CHIPS = 32
F32 = jnp.float32
BF16 = jnp.bfloat16
SWAP = [(0, 1), (1, 0)]
SCALAR_ROWS = 8
VMEM_LIMIT = 20 * 1024 * 1024
SMALL_VMEM = 8 * 1024 * 1024


def far(*arrays):
    return tuple(pltpu.with_memory_space_constraint(x, pltpu.HBM) for x in arrays)


def near(*arrays):
    return tuple(pltpu.with_memory_space_constraint(x, pltpu.VMEM) for x in arrays)


def dot(a, b, ca, cb):
    return lax.dot_general(a, b, (((ca,), (cb,)), ((), ())), preferred_element_type=F32)


def states_kernel(core_ref, kp_ref, vp_ref, kr_ref, vr_ref, kp2_ref, vp2_ref, kr2_ref, vr2_ref, total_ref, first_ref):
    core = core_ref[0]
    sets = (
        ((kp_ref, vp_ref), (kp2_ref, vp2_ref)),
        ((kr_ref, vr_ref), (kr2_ref, vr2_ref)),
    )
    rows = 2 * KV_HEADS * D // CHIPS
    for model, (mine, theirs) in enumerate(sets):
        for g in range(KV_HEADS):
            span = slice(g * D, (g + 1) * D)
            own = dot(mine[0][0, core, :, span], mine[1][0, core, :, span], 0, 0)
            other = dot(theirs[0][0, core, :, span], theirs[1][0, core, :, span], 0, 0)
            first_ref[model, g] = jnp.where(core == 0, own, other)
            total = (own + other).astype(BF16)
            for j in range(D // rows):
                total_ref[(model * KV_HEADS + g) * (D // rows) + j] = total[j * rows : (j + 1) * rows]


def block_states(core, kp, vp, kr, vr, kp2, vp2, kr2, vr2):
    return pl.pallas_call(
        states_kernel,
        out_shape=(
            pltpu.VMEM((CHIPS, 2 * KV_HEADS * D // CHIPS, D), BF16),
            pltpu.HBM((2, KV_HEADS, D, D), F32),
        ),
        in_specs=[pl.BlockSpec(memory_space=pltpu.SMEM)] + [pl.BlockSpec(memory_space=pltpu.VMEM)] * 8,
        out_specs=(pl.BlockSpec(memory_space=pltpu.VMEM),) * 2,
        name="block_states",
        cost_estimate=pl.CostEstimate(flops=16 * 2 * D * D * T, bytes_accessed=2 << 20, transcendentals=0),
        compiler_params=pltpu.CompilerParams(vmem_limit_bytes=SMALL_VMEM),
    )(core, *far(kp, vp, kr, vr), *near(kp2, vp2, kr2, vr2))


def prefix_kernel(x_ref, o_ref):
    total = jnp.zeros(x_ref.shape[1:], F32)
    for chip in range(CHIPS):
        o_ref[chip] = total.astype(BF16)
        total = total + x_ref[chip].astype(F32)


def exclusive_prefix(x):
    return pl.pallas_call(
        prefix_kernel,
        out_shape=pltpu.VMEM(x.shape, BF16),
        in_specs=[pl.BlockSpec(memory_space=pltpu.VMEM)],
        out_specs=pl.BlockSpec(memory_space=pltpu.VMEM),
        name="exclusive_prefix",
        cost_estimate=pl.CostEstimate(flops=x.size, bytes_accessed=4 * x.size, transcendentals=0),
        compiler_params=pltpu.CompilerParams(vmem_limit_bytes=SMALL_VMEM),
    )(*near(x))


def suffix_kernel(x_ref, o_ref, delta_ref):
    rows = o_ref.shape[1]
    total = jnp.zeros((rows, D), F32)
    pieces = jnp.zeros((SCALAR_ROWS, D), F32)
    for chip in range(CHIPS - 1, -1, -1):
        o_ref[chip] = total.astype(BF16)
        total = total + x_ref[chip, 0:rows].astype(F32)
        pieces = pieces + x_ref[chip, rows : rows + SCALAR_ROWS].astype(F32)
    delta_ref[...] = jnp.broadcast_to(jnp.sum(pieces, axis=0, keepdims=True), (SCALAR_ROWS, D))


def exclusive_suffix(x):
    rows = x.shape[1] - SCALAR_ROWS
    return pl.pallas_call(
        suffix_kernel,
        out_shape=(
            pltpu.VMEM((CHIPS, rows, D), BF16),
            pltpu.VMEM((SCALAR_ROWS, D), F32),
        ),
        in_specs=[pl.BlockSpec(memory_space=pltpu.VMEM)],
        out_specs=(pl.BlockSpec(memory_space=pltpu.VMEM),) * 2,
        name="exclusive_suffix",
        cost_estimate=pl.CostEstimate(flops=x.size, bytes_accessed=4 * x.size, transcendentals=0),
        compiler_params=pltpu.CompilerParams(vmem_limit_bytes=SMALL_VMEM),
    )(*near(x))


def rows_of(x):
    return jnp.concatenate([x[:, r * D : (r + 1) * D] for r in range(GROUP)], axis=0)


def causal_rows():
    row = lax.broadcasted_iota(jnp.int32, (T, T), 0)
    column = lax.broadcasted_iota(jnp.int32, (T, T), 1)
    return jnp.concatenate([row >= column] * GROUP, axis=0)


def seq_spec(width):
    return pl.BlockSpec((1, 1, T, width), lambda g, c: (0, c[0], 0, g))


def flat_spec(width):
    return pl.BlockSpec((T, width), lambda g, c: (0, g))


def stack_spec(count, width):
    return pl.BlockSpec((count, T, width), lambda g, c: (0, 0, g))


SCORES = pl.BlockSpec((4, 1, GROUP * T, T), lambda g, c: (0, g, 0, 0))
PULLED = pl.BlockSpec((2, 1, GROUP * T, D), lambda g, c: (0, g, 0, 0))
ARBITRARY = pltpu.CompilerParams(dimension_semantics=("arbitrary",), vmem_limit_bytes=VMEM_LIMIT)


def scores_kernel(core_ref, qp_ref, qr_ref, kp_ref, kr_ref, qp2_ref, qr2_ref, kp2_ref, kr2_ref, s_ref):
    causal = causal_rows()
    pairs = (
        (qp_ref[0, 0], kp_ref[0, 0]),
        (qp2_ref[0, 0], kp2_ref[0, 0]),
        (qr_ref[0, 0], kr_ref[0, 0]),
        (qr2_ref[0, 0], kr2_ref[0, 0]),
    )
    for i, (query, key) in enumerate(pairs):
        s_ref[i, 0] = jnp.where(causal, dot(rows_of(query), key, 1, 1), 0.0).astype(BF16)


def block_scores(core, qp, qr, kp, kr, qp2, qr2, kp2, kr2):
    wide, narrow = GROUP * D, D
    return pl.pallas_call(
        scores_kernel,
        grid_spec=pltpu.PrefetchScalarGridSpec(
            num_scalar_prefetch=1,
            grid=(KV_HEADS,),
            in_specs=[
                seq_spec(wide),
                seq_spec(wide),
                seq_spec(narrow),
                seq_spec(narrow),
                seq_spec(wide),
                seq_spec(wide),
                seq_spec(narrow),
                seq_spec(narrow),
            ],
            out_specs=SCORES,
        ),
        out_shape=pltpu.HBM((4, KV_HEADS, GROUP * T, T), BF16),
        name="block_scores",
        cost_estimate=pl.CostEstimate(flops=64 * 2 * D * D * T, bytes_accessed=5 << 20, transcendentals=0),
        compiler_params=ARBITRARY,
    )(core, *far(qp, qr, kp, kr, qp2, qr2, kp2, kr2))


def forward_kernel(
    core_ref,
    qp_ref,
    qr_ref,
    vp_ref,
    vr_ref,
    read_ref,
    qp2_ref,
    qr2_ref,
    read2_ref,
    vp2_ref,
    vr2_ref,
    mask_ref,
    mask2_ref,
    s_ref,
    before_ref,
    first_ref,
    pulled_ref,
    total_ref,
    second_ref,
    carried_ref,
    acc_ref,
):
    core = core_ref[0]
    g = pl.program_id(0)
    ones = jnp.ones((D, D), BF16)

    def row_mean(x):
        return dot(x.astype(BF16), ones, 1, 0) * (1.0 / D)

    def carried_of(model):
        before = before_ref[model, 0].astype(F32)
        after = before + first_ref[model, 0]
        own = jnp.where(core == 0, before, after).astype(BF16)
        other = jnp.where(core == 0, after, before).astype(BF16)
        return own, other

    def forward(scores, query, value, carried):
        raw = dot(jnp.concatenate([scores, query], axis=1), jnp.concatenate([value, carried], axis=0), 1, 0)
        inverse = lax.rsqrt(row_mean(raw * raw) + EPS)
        return raw * inverse, inverse

    carried_policy = carried_of(0)
    carried_reference = carried_of(1)
    row = lax.broadcasted_iota(jnp.int32, (T, T), 0)
    column = lax.broadcasted_iota(jnp.int32, (T, T), 1)

    def masked(read, mask):
        mask = mask[0, pl.ds(core, 1), :].astype(F32)
        kept = jnp.sum(jnp.where(row == column, mask, 0.0), axis=1, keepdims=True)
        kept = jnp.broadcast_to(kept, (T, D))
        return jnp.concatenate([read[:, r * D : (r + 1) * D].astype(F32) * kept for r in range(GROUP)], axis=0)

    queries = rows_of(qp_ref[0, 0]), rows_of(qp2_ref[0, 0])
    queries_ref = rows_of(qr_ref[0, 0]), rows_of(qr2_ref[0, 0])
    values = vp_ref[0, 0], vp2_ref[0, 0]
    values_ref = vr_ref[0, 0], vr2_ref[0, 0]
    reads = masked(read_ref[0, 0], mask_ref), masked(read2_ref[0, 0], mask2_ref)
    tokens = jnp.zeros((1, D), F32)
    grads = []
    for i in range(2):
        read = reads[i]
        normed, inverse = forward(s_ref[i, 0], queries[i], values[i], carried_policy[i])
        normed_ref = forward(s_ref[2 + i, 0], queries_ref[i], values_ref[i], carried_reference[i])[0]
        reading = read * normed
        tokens = tokens + jnp.sum(reading - read * normed_ref, axis=0, keepdims=True)
        pulled = (inverse * (read - normed * row_mean(reading))).astype(BF16)
        pulled_ref[i, 0] = pulled
        carried_ref[i, 0] = carried_policy[i]
        grads.append(dot(queries[i], pulled, 0, 0))

    @pl.when(g == 0)
    def _():
        acc_ref[...] = jnp.zeros_like(acc_ref)

    acc_ref[0:1, :] = acc_ref[0:1, :] + tokens
    chunks = CHIPS // KV_HEADS
    total = (grads[0] + grads[1]).astype(BF16)
    rows = D // chunks
    for j in range(chunks):
        total_ref[g * chunks + j, 0:rows, :] = total[j * rows : (j + 1) * rows]
    second_ref[0] = jnp.where(core == 0, grads[1], grads[0])

    @pl.when(g == KV_HEADS - 1)
    def _():
        part = jnp.broadcast_to(jnp.sum(acc_ref[0:1, :], axis=1, keepdims=True), (SCALAR_ROWS, D))
        high = part.astype(BF16).astype(F32)
        middle = (part - high).astype(BF16).astype(F32)
        low = part - high - middle
        place = lax.broadcasted_iota(jnp.int32, (SCALAR_ROWS, D), 0)
        pieces = jnp.where(
            place == 0, high, jnp.where(place == 1, middle, jnp.where(place == 2, low, 0.0))
        ).astype(BF16)
        for chip in range(CHIPS):
            total_ref[chip, rows : rows + SCALAR_ROWS, :] = pieces


def forward_pass(core, qp, qr, vp, vr, read, qp2, qr2, read2, vp2, vr2, mask, mask2, scores, before, first):
    wide, narrow = GROUP * D, D
    state = pl.BlockSpec((2, 1, D, D), lambda g, c: (0, g, 0, 0))
    whole = pl.BlockSpec((1, 2, T), lambda g, c: (0, 0, 0))
    rows = KV_HEADS * D // CHIPS + SCALAR_ROWS
    return pl.pallas_call(
        forward_kernel,
        grid_spec=pltpu.PrefetchScalarGridSpec(
            num_scalar_prefetch=1,
            grid=(KV_HEADS,),
            in_specs=[
                seq_spec(wide),
                seq_spec(wide),
                seq_spec(narrow),
                seq_spec(narrow),
                seq_spec(wide),
                seq_spec(wide),
                seq_spec(wide),
                seq_spec(wide),
                seq_spec(narrow),
                seq_spec(narrow),
                whole,
                whole,
                SCORES,
                state,
                state,
            ],
            out_specs=(
                PULLED,
                pl.BlockSpec((CHIPS, rows, D), lambda g, c: (0, 0, 0)),
                pl.BlockSpec((1, D, D), lambda g, c: (g, 0, 0)),
                state,
            ),
            scratch_shapes=[pltpu.VMEM((8, D), F32)],
        ),
        out_shape=(
            pltpu.HBM((2, KV_HEADS, GROUP * T, D), BF16),
            pltpu.VMEM((CHIPS, rows, D), BF16),
            pltpu.HBM((KV_HEADS, D, D), F32),
            pltpu.HBM((2, KV_HEADS, D, D), BF16),
        ),
        name="forward_pass",
        cost_estimate=pl.CostEstimate(flops=192 * 2 * D * D * T, bytes_accessed=8 << 20, transcendentals=65536),
        compiler_params=ARBITRARY,
    )(core, *far(qp, qr, vp, vr, read, qp2, qr2, read2, vp2, vr2, mask, mask2, scores), *near(before), *far(first))


def backward_kernel(
    core_ref,
    qp_ref,
    kp_ref,
    vp_ref,
    qp2_ref,
    kp2_ref,
    vp2_ref,
    s_ref,
    pulled_ref,
    carried_ref,
    qg_ref,
    kv_ref,
    qg2_ref,
    kvg2_ref,
):
    causal = causal_rows()
    blocks = (
        (qp_ref[0, 0], kp_ref[0, 0], vp_ref[0, 0], qg_ref, kv_ref),
        (qp2_ref[0, 0], kp2_ref[0, 0], vp2_ref[0, 0], qg2_ref, kvg2_ref),
    )
    for i, (query, key, value, q_out, kv_out) in enumerate(blocks):
        pulled = pulled_ref[i, 0]
        dscore = jnp.where(causal, dot(pulled, value, 1, 1), 0.0).astype(BF16)
        query_grad = (dot(dscore, key, 1, 0) + dot(pulled, carried_ref[i, 0], 1, 1)).astype(BF16)
        for r in range(GROUP):
            q_out[:, r * D : (r + 1) * D] = query_grad[r * T : (r + 1) * T]
        kv_out[0] = dot(dscore, rows_of(query), 0, 0)
        kv_out[1] = dot(s_ref[i, 0], pulled, 0, 0)


def backward_pass(core, qp, kp, vp, qp2, kp2, vp2, scores, pulled, carried):
    wide, narrow = GROUP * D, D
    query_shape = pltpu.HBM((T, HEADS * D), BF16)
    pair_shape = pltpu.HBM((2, T, KV_HEADS * D), F32)
    return pl.pallas_call(
        backward_kernel,
        grid_spec=pltpu.PrefetchScalarGridSpec(
            num_scalar_prefetch=1,
            grid=(KV_HEADS,),
            in_specs=[
                seq_spec(wide),
                seq_spec(narrow),
                seq_spec(narrow),
                seq_spec(wide),
                seq_spec(narrow),
                seq_spec(narrow),
                pl.BlockSpec((2, 1, GROUP * T, T), lambda g, c: (0, g, 0, 0)),
                PULLED,
                pl.BlockSpec((2, 1, D, D), lambda g, c: (0, g, 0, 0)),
            ],
            out_specs=(flat_spec(wide), stack_spec(2, narrow), flat_spec(wide), stack_spec(2, narrow)),
        ),
        out_shape=(query_shape, pair_shape, query_shape, pair_shape),
        name="backward_pass",
        cost_estimate=pl.CostEstimate(flops=160 * 2 * D * D * T, bytes_accessed=6 << 20, transcendentals=0),
        compiler_params=ARBITRARY,
    )(core, *far(qp, kp, vp, qp2, kp2, vp2, scores, pulled, carried))


def weight_of(seq, weight_ref):
    return jnp.where(seq == 0, -weight_ref[0:1, 0:1], weight_ref[0:1, 0:1])


def scale_kernel(core_ref, own_ref, other_ref, weight_ref, o_ref):
    core = core_ref[0]
    for turn, ref in ((0, own_ref), (1, other_ref)):
        seq = lax.rem(core + turn, 2)
        o_ref[0, seq] = (ref[...].astype(F32) * weight_of(seq, weight_ref)).astype(BF16)


def scaled_queries(core, own, other, weight):
    part = pl.BlockSpec((T, GROUP * D), lambda g, c: (0, g))
    return pl.pallas_call(
        scale_kernel,
        grid_spec=pltpu.PrefetchScalarGridSpec(
            num_scalar_prefetch=1,
            grid=(KV_HEADS,),
            in_specs=[part, part, pl.BlockSpec((SCALAR_ROWS, D), lambda g, c: (0, 0))],
            out_specs=pl.BlockSpec((1, 2, T, GROUP * D), lambda g, c: (0, 0, 0, g)),
        ),
        out_shape=pltpu.HBM((1, 2, T, HEADS * D), BF16),
        name="scaled_queries",
        cost_estimate=pl.CostEstimate(flops=2 * T * HEADS * D, bytes_accessed=2 << 20, transcendentals=0),
        compiler_params=ARBITRARY,
    )(core, *far(own, other), weight)


def final_kernel(
    core_ref,
    kp_ref,
    vp_ref,
    pair_ref,
    pair2_ref,
    weight_ref,
    after_ref,
    after2_ref,
    second_ref,
    second2_ref,
    ko_ref,
    vo_ref,
):
    core = core_ref[0]
    for turn, after, second, grads_ref in (
        (0, after_ref, second_ref, pair_ref),
        (1, after2_ref, second2_ref, pair2_ref),
    ):
        seq = lax.rem(core + turn, 2)
        weight = weight_of(seq, weight_ref)
        for g in range(KV_HEADS):
            span = slice(g * D, (g + 1) * D)
            later = after[g].astype(F32)
            later = jnp.where(core == 0, later + second[g], later).astype(BF16)
            key_grad = grads_ref[0, :, span] + dot(vp_ref[0, seq, :, span], later, 1, 1)
            value_grad = grads_ref[1, :, span] + dot(kp_ref[0, seq, :, span], later, 1, 0)
            ko_ref[0, seq, :, span] = (weight * key_grad).astype(BF16)
            vo_ref[0, seq, :, span] = (weight * value_grad).astype(BF16)


def final_pass(core, kp, vp, pair, pair2, weight, after, after2, second, second2):
    shape = pltpu.HBM((1, 2, T, KV_HEADS * D), BF16)
    return pl.pallas_call(
        final_kernel,
        out_shape=(shape, shape),
        in_specs=[pl.BlockSpec(memory_space=pltpu.SMEM)] + [pl.BlockSpec(memory_space=pltpu.VMEM)] * 9,
        out_specs=(pl.BlockSpec(memory_space=pltpu.VMEM),) * 2,
        name="final_pass",
        cost_estimate=pl.CostEstimate(flops=16 * 2 * D * D * T, bytes_accessed=3 << 20, transcendentals=0),
        compiler_params=pltpu.CompilerParams(vmem_limit_bytes=SMALL_VMEM),
    )(core, *near(kp, vp, pair, pair2), weight, *near(after, after2, second, second2))


def swap(x):
    return lax.ppermute(x, "core", SWAP)


def exchange(x):
    return lax.all_to_all(x, "chip", 0, 0, tiled=True)


def shards(qp, kp, vp, qr, kr, vr, read, mask):
    core_id = lax.axis_index("core")
    core = core_id.astype(jnp.int32).reshape(1)
    first_core = core_id == 0
    kv2 = tuple(swap(x) for x in (kp, vp, kr, vr))
    kv2, wide = lax.optimization_barrier((kv2, (qp, qr, read, mask)))
    kp2, vp2, kr2, vr2 = kv2
    qp2, qr2, read2, mask2 = (swap(x) for x in wide)
    total, first = block_states(core, kp, vp, kr, vr, *kv2)
    spread = exchange(total)
    scores = block_scores(core, qp, qr, kp, kr, qp2, qr2, kp2, kr2)
    before = exchange(exclusive_prefix(spread)).reshape(2, KV_HEADS, D, D)
    pulled, payload, second, carried = forward_pass(
        core, qp, qr, vp, vr, read, qp2, qr2, read2, vp2, vr2, mask, mask2, scores, before, first
    )
    arrived = exchange(payload)
    second2 = swap(second)
    grads = backward_pass(core, qp, kp, vp, qp2, kp2, vp2, scores, pulled, carried)
    arrived, grads = lax.optimization_barrier((arrived, grads))
    qg, pair, qg2, pair2 = grads
    qg2, pair2 = swap(qg2), swap(pair2)
    after, mine = exclusive_suffix(arrived)
    after = exchange(after).reshape(KV_HEADS, D, D)

    theirs = swap(mine)
    delta = jnp.where(first_core, mine - theirs, theirs - mine)
    loss = jax.nn.softplus(-DPO_BETA * delta)
    pairs = lax.axis_size("dp")
    one, two, three = (lax.ppermute(loss, "dp", [(i, i ^ k) for i in range(pairs)]) for k in (1, 2, 3))
    pair_loss = ((loss + one) + (two + three)) / pairs
    scale = math.sqrt(HEADS * D * T * lax.axis_size("chip") * 2)
    weight = DPO_BETA * jax.nn.sigmoid(-DPO_BETA * delta) * scale
    query_rows = scaled_queries(core, qg, qg2, weight)
    after, query_rows, pair_loss, pair2, second2 = lax.optimization_barrier(
        (after, query_rows, pair_loss[0, 0], pair2, second2)
    )
    key_rows, value_rows = final_pass(core, kp, vp, pair, pair2, weight, after, swap(after), second, second2)
    return query_rows, key_rows, value_rows, pair_loss


def solution(mesh):
    devices = mesh.devices
    split = Mesh(devices.reshape(devices.shape[0] // 2, 2, devices.shape[1]), ("chip", "core", "dp"))
    placed = P("dp", None, ("chip", "core"), None)
    return jax.shard_map(
        shards,
        mesh=split,
        in_specs=(placed,) * 7 + (P("dp", None, ("chip", "core")),),
        out_specs=(placed, placed, placed, P()),
        check_vma=False,
    )
```

time: 605 us -> 96.9 us (0.16)
  waiting for transfers between devices: 271 us -> 13.6 us
  blocking collectives: 197 us -> 20.9 us
  other arithmetic: 74.6 us -> 0.02 us
  starting transfers between devices: 0.12 us -> 31.5 us
  Pallas kernels: 0 us -> 27.2 us
  matrix products: 19.5 us -> 0 us
  between operations: 18.7 us -> 0.8 us
  local copies, waits for them, and re-layouts: 17.8 us -> 2.29 us
    all_gather x3 -> x0, waiting for transfers between devices: 271 us -> none  [carried_in(): gathered = lax.all_gather(x.astype(jnp.bfloat16), axis)]
    psum x2 -> x0, blocking collectives: 197 us -> none  [the longest x1 188 us: shards(): totals = lax.psum(sums, 'ctx')]
    add x64 -> x0, other arithmetic: 68.5 us -> none  [add_states(): return earlier + following]
    pallas_call x0 -> x8, Pallas kernels: none -> 27.2 us  [the longest x1 8.56 us: forward_pass(): pl.pallas_call(forward_kernel, grid_spec=pltpu.PrefetchScalarGridSpec(num...]
    all_to_all x0 -> x1, blocking collectives: none -> 20.9 us  [exchange(): return lax.all_to_all(x, 'chip', 0, 0, tiled=True)]
    dot_general x15 -> x0, matrix products: 19.5 us -> none  [the longest x2 4.6 us: span_forward(): jnp.einsum('agrts,asgd->atgrd', pair_score_rows, value_head_rows, preferr...]
    ppermute x0 -> x16, starting transfers between devices: none -> 16.4 us  [the longest x13 11.1 us: swap(): return lax.ppermute(x, 'core', SWAP)]
    all_to_all x0 -> x3, starting transfers between devices: none -> 15.1 us  [exchange(): return lax.all_to_all(x, 'chip', 0, 0, tiled=True)]
  transfers between devices with their start and end apart: 3 -> 19, of which waited for: 3 -> 9; matrix products, arithmetic and copies ran while one was open for 4% -> 1% of each run, Pallas kernels for 0% -> 18%
where the time goes in v1:
time: 96.9 us; the launch traced here: 96.3 us
  starting transfers between devices  31.5 us (33%)
  Pallas kernels  27.2 us (28%)
  blocking collectives  20.9 us (22%)
  waiting for transfers between devices  13.6 us (14%)
  local copies, waits for them, and re-layouts  2.29 us (2%)
    all_to_all x1, blocking collectives, exchange(): return lax.all_to_all(x, 'chip', 0, 0, tiled=True)  20.9 us
    all_to_all x3, starting transfers between devices, exchange(): return lax.all_to_all(x, 'chip', 0, 0, tiled=True)  15.1 us
    ppermute x13, starting transfers between devices, swap(): return lax.ppermute(x, 'core', SWAP)  11.1 us
    pallas_call x1, Pallas kernels, forward_pass(): pl.pallas_call(forward_kernel, grid_spec=pltpu.PrefetchScalarGridSpec(num...  8.56 us
    all_to_all x3, waiting for transfers between devices, exchange(): return lax.all_to_all(x, 'chip', 0, 0, tiled=True)  8.04 us
    pallas_call x1, Pallas kernels, backward_pass(): pl.pallas_call(backward_kernel, grid_spec=pltpu.PrefetchScalarGridSpec(nu...  5.71 us
    ppermute x3, starting transfers between devices, shards(): lax.ppermute(loss, 'dp', [(i, i ^ k) for i in range(pairs)])  5.27 us
    pallas_call x1, Pallas kernels, block_scores(): pl.pallas_call(scores_kernel, grid_spec=pltpu.PrefetchScalarGridSpec(num_...  4.47 us
  transfers between devices with their start and end apart: 19, of which 9 were waited for; matrix products, arithmetic and copies ran while one was open for 1% of the time, Pallas kernels for 18%

profile of v1, /device:TPU:1, one launch (start us, length us, event | category | flops | bytes accessed | tf_op | source)
XLA Modules:
  0.0 96.3 jit_solution(170695214241928419)
XLA Ops:
  0.6 0.0 copy-start.10
  0.6 3.3 %collective-permute-start = (bf16[1,2,128,512]{3,2,1,0:T(8,128)(2,1)}, bf16[1,2,128,512]{3,2,1,0:T(8,128)(2,1)S(1)}, u32[]{:S(2)}, u32[]{:S(2)}) collective-permute-start(bf16[1,2,128,512]{3,2,1,0:T(8,128)(2,1)} %kp_ref.7), channel_id=1, source_target_pairs={{0,4},{4,0},{1,5},{5,1},{2,6},{6,2},{3,7},{7,3},{8,12},{12,8},{9,1... | collective-permute-start | bytes 786440 | tf_op jit(solution)/shard_map/ppermute | solution.py:459
  4.0 0.1 collective-permute-start.1
  4.1 0.4 collective-permute-start.2
  4.5 0.1 collective-permute-start.3
  4.6 0.8 collective-permute-done.kp2_ref
  5.3 0.4 collective-permute-done.1.vp2_ref
  5.7 0.4 collective-permute-done.2.kr2_ref
  6.1 0.4 collective-permute-done.3.vr2_ref
  6.5 0.4 collective-permute-start.4
  6.8 0.1 collective-permute-start.5
  7.0 0.4 collective-permute-start.6
  7.4 2.3 %block_states.1 = (bf16[32,32,128]{2,1,0:T(8,128)(2,1)S(1)}, f32[2,4,128,128]{3,2,1,0:T(8,128)}) custom-call(s32[1]{0:T(128)} %bitcast.core_ref, bf16[1,2,128,512]{3,2,1,0:T(8,128)(2,1)} %kp_ref.7, bf16[1,2,128,512]{3,2,1,0:T(8,128)(2,1)} %vp_ref.7, bf16[1,2,128,512]{3,2,1,0:T(8,128)(2,1)} %kr_ref.3, bf16[1,2,128,512]{3,2,1,0:T(8,128)(2,1)} %vr_ref.3, ...), custom_call_target="tpu_custom_call" | custom-call | flops 67108864 | bytes 2097152 | tf_op jit(solution)/shard_map/block_states/pallas_call | solution.py:57
  9.7 20.9 %all_to_all.20.x_ref = bf16[32,32,128]{2,1,0:T(8,128)(2,1)S(1)} all-to-all(bf16[32,32,128]{2,1,0:T(8,128)(2,1)S(1)} %get-tuple-element.44), channel_id=1, replica_groups=mesh['chip'=32,'core'=2,'dp'=4] {'chip'}, dimensions={0} | all-to-all | bytes 524288 | tf_op jit(solution)/shard_map/all_to_all | solution.py:463
  30.6 0.7 exclusive_prefix.1
  31.3 4.3 %all-to-all-start.1 = ((bf16[32,32,128]{2,1,0:T(8,128)(2,1)}), bf16[32,32,128]{2,1,0:T(8,128)(2,1)S(1)}, u32[]{:S(2)}, u32[]{:S(2)}) async-start(bf16[32,32,128]{2,1,0:T(8,128)(2,1)} %exclusive_prefix.1), calls=%async_computation.1 | async-start | bytes 524288 | tf_op jit(solution)/shard_map/all_to_all | solution.py:463
  35.7 1.8 %collective-permute-start.7 = (s32[1,2,128]{2,1,0:T(2,128)S(1)}, s32[1,2,128]{2,1,0:T(2,128)S(1)}, u32[]{:S(2)}, u32[]{:S(2)}) collective-permute-start(s32[1,2,128]{2,1,0:T(2,128)S(1)} %copy-done.10), channel_id=1, source_target_pairs={{0,4},{4,0},{1,5},{5,1},{2,6},{6,2},{3,7},{7,3},{8,12},{12,8},{9,1... | collective-permute-start | bytes 3080 | tf_op jit(solution)/shard_map/ppermute | solution.py:459
  37.5 0.0 collective-permute-done.4.qp2_ref
  37.5 0.0 collective-permute-done.5.qr2_ref
  37.5 0.9 copy-done.8
  38.4 4.5 %block_scores.1.s_ref = bf16[4,4,512,128]{3,2,1,0:T(8,128)(2,1)} custom-call(s32[1]{0:T(128)} %bitcast.core_ref, bf16[1,2,128,2048]{3,2,1,0:T(8,128)(2,1)} %qp_ref.5, bf16[1,2,128,2048]{3,2,1,0:T(8,128)(2,1)} %qr_ref.3, bf16[1,2,128,512]{3,2,1,0:T(8,128)(2,1)} %kp_ref.7, bf16[1,2,128,512]{3,2,1,0:T(8,128)(2,1)} %kr_ref.3, ...), custom_call_target="tpu_custom_call" | custom-call | flops 268435456 | bytes 5242880 | tf_op jit(solution)/shard_map/block_scores/pallas_call | solution.py:158
  42.9 0.0 collective-permute-done.7.mask2_ref
  42.9 3.2 %all-to-all-done.1 = bf16[32,32,128]{2,1,0:T(8,128)(2,1)S(1)} async-done(((bf16[32,32,128]{2,1,0:T(8,128)(2,1)}), bf16[32,32,128]{2,1,0:T(8,128)(2,1)S(1)}, u32[]{:S(2)}, u32[]{:S(2)}) %all-to-all-start.1) | async-done | bytes 262176 | tf_op jit(solution)/shard_map/all_to_all | solution.py:463
  46.1 8.6 %forward_pass.1 = (bf16[2,4,512,128]{3,2,1,0:T(8,128)(2,1)}, bf16[32,24,128]{2,1,0:T(8,128)(2,1)}, f32[4,128,128]{2,1,0:T(8,128)}, bf16[2,4,128,128]{3,2,1,0:T(8,128)(2,1)}) custom-call(s32[1]{0:T(128)} %bitcast.core_ref, bf16[1,2,128,2048]{3,2,1,0:T(8,128)(2,1)} %qp_ref.5, bf16[1,2,128,2048]{3,2,1,0:T(8,128)(2,1)} %qr_ref.3, ...), custom_call_target="tpu_custom_call" | custom-call | flops 805306368 | bytes 8388608 | tf_op jit(solution)/shard_map/forward_pass/pallas_call | solution.py:284
  54.7 6.9 %all-to-all-start.2 = ((bf16[32,24,128]{2,1,0:T(8,128)(2,1)}), bf16[32,24,128]{2,1,0:T(8,128)(2,1)S(1)}, u32[]{:S(2)}, u32[]{:S(2)}) async-start(bf16[32,24,128]{2,1,0:T(8,128)(2,1)} %get-tuple-element.46), calls=%async_computation.2 | async-start | bytes 393216 | tf_op jit(solution)/shard_map/all_to_all | solution.py:463
  61.6 5.7 %backward_pass.1 = (bf16[128,2048]{1,0:T(8,128)(2,1)}, f32[2,128,512]{2,1,0:T(8,128)}, bf16[128,2048]{1,0:T(8,128)(2,1)}, f32[2,128,512]{2,1,0:T(8,128)}) custom-call(s32[1]{0:T(128)} %bitcast.core_ref, bf16[1,2,128,2048]{3,2,1,0:T(8,128)(2,1)} %qp_ref.5, bf16[1,2,128,512]{3,2,1,0:T(8,128)(2,1)} %kp_ref.7, bf16[1,2,128,512]{3,2,1,0:T(8,128)(2,1)} %vp_ref.7, ...), custom_call_target="tpu_custom_call" | custom-call | flops 671088640 | bytes 6291456 | tf_op jit(solution)/shard_map/backward_pass/pallas_call | solution.py:361
  67.3 0.0 copy-start.1
  67.3 4.9 %all-to-all-done.2.x_ref = bf16[32,24,128]{2,1,0:T(8,128)(2,1)S(1)} async-done(((bf16[32,24,128]{2,1,0:T(8,128)(2,1)}), bf16[32,24,128]{2,1,0:T(8,128)(2,1)S(1)}, u32[]{:S(2)}, u32[]{:S(2)}) %all-to-all-start.2) | async-done | bytes 196640 | tf_op jit(solution)/shard_map/all_to_all | solution.py:463
  72.2 2.0 %collective-permute-start.8 = (bf16[128,2048]{1,0:T(8,128)(2,1)}, bf16[128,2048]{1,0:T(8,128)(2,1)S(1)}, u32[]{:S(2)}, u32[]{:S(2)}) collective-permute-start(bf16[128,2048]{1,0:T(8,128)(2,1)} %get-tuple-element.56), channel_id=1, source_target_pairs={{0,4},{4,0},{1,5},{5,1},{2,6},{6,2},{3,7},{7,3},{8,12},{12,8},{9,1... | collective-permute-start | bytes 1572872 | tf_op jit(solution)/shard_map/ppermute | solution.py:459
  74.2 0.0 collective-permute-start.13
  74.2 0.7 exclusive_suffix.1
  74.9 0.5 collective-permute-start.9
  75.4 0.0 collective-permute-start.14
  75.4 3.9 %all-to-all-start.3 = ((bf16[32,16,128]{2,1,0:T(8,128)(2,1)}), bf16[32,16,128]{2,1,0:T(8,128)(2,1)S(1)}, u32[]{:S(2)}, u32[]{:S(2)}) async-start(bf16[32,16,128]{2,1,0:T(8,128)(2,1)} %get-tuple-element.54), calls=%async_computation.3 | async-start | bytes 262144 | tf_op jit(solution)/shard_map/all_to_all | solution.py:463
  79.3 1.4 %collective-permute-start.10 = (f32[8,128]{1,0:T(8,128)S(1)}, f32[8,128]{1,0:T(8,128)S(1)}, u32[]{:S(2)}, u32[]{:S(2)}) collective-permute-start(f32[8,128]{1,0:T(8,128)S(1)} %get-tuple-element.68), channel_id=1, source_target_pairs={{0,1},{1,0},{2,3},{3,2},{4,5},{5,4},{6,7},{7,6},{8,9},{9,8},{10,11... | collective-permute-start | bytes 12296 | tf_op jit(solution)/shard_map/ppermute | solution.py:494
  80.7 2.6 %collective-permute-start.11 = (f32[8,128]{1,0:T(8,128)S(1)}, f32[8,128]{1,0:T(8,128)S(1)}, u32[]{:S(2)}, u32[]{:S(2)}) collective-permute-start(f32[8,128]{1,0:T(8,128)S(1)} %get-tuple-element.68), channel_id=1, source_target_pairs={{0,2},{1,3},{2,0},{3,1},{4,6},{5,7},{6,4},{7,5},{8,10},{9,11},{10,... | collective-permute-start | bytes 12296 | tf_op jit(solution)/shard_map/ppermute | solution.py:494
  83.3 1.3 %collective-permute-start.12 = (f32[8,128]{1,0:T(8,128)S(1)}, f32[8,128]{1,0:T(8,128)S(1)}, u32[]{:S(2)}, u32[]{:S(2)}) collective-permute-start(f32[8,128]{1,0:T(8,128)S(1)} %get-tuple-element.68), channel_id=1, source_target_pairs={{0,3},{1,2},{2,1},{3,0},{4,7},{5,6},{6,5},{7,4},{8,11},{9,10},{10,... | collective-permute-start | bytes 12296 | tf_op jit(solution)/shard_map/ppermute | solution.py:494
  84.6 0.1 collective-permute-done.11
  84.7 2.6 %collective-permute-done.12 = f32[8,128]{1,0:T(8,128)S(1)} collective-permute-done((f32[8,128]{1,0:T(8,128)S(1)}, f32[8,128]{1,0:T(8,128)S(1)}, u32[]{:S(2)}, u32[]{:S(2)}) %collective-permute-start.12) | collective-permute-done | bytes 4128 | tf_op jit(solution)/shard_map/ppermute | solution.py:494
  87.3 0.5 slice.3
  87.8 0.0 collective-permute-done.8.other_ref
  87.8 0.8 copy-done.9
  88.6 3.5 %scaled_queries.1 = bf16[1,2,128,2048]{3,2,1,0:T(8,128)(2,1)} custom-call(s32[1]{0:T(128)} %bitcast.core_ref, bf16[128,2048]{1,0:T(8,128)(2,1)} %get-tuple-element.55.own_ref, bf16[128,2048]{1,0:T(8,128)(2,1)} %copy-done.9, f32[8,128]{1,0:T(8,128)S(1)} %get-tuple-element.69.weight_ref), custom_call_target="tpu_custom_call" | custom-call | flops 524288 | bytes 2097152 | tf_op jit(solution)/shard_map/scaled_queries/pallas_call | solution.py:399
  92.1 0.0 all-to-all-done.3
  92.2 0.0 collective-permute-done.13.pair2_ref
  92.2 2.0 %collective-permute-start.15 = (bf16[4,128,128]{2,1,0:T(8,128)(2,1)S(1)}, bf16[4,128,128]{2,1,0:T(8,128)(2,1)S(1)}, u32[]{:S(2)}, u32[]{:S(2)}) collective-permute-start(bf16[4,128,128]{2,1,0:T(8,128)(2,1)S(1)} %bitcast.5), channel_id=1, source_target_pairs={{0,4},{4,0},{1,5},{5,1},{2,6},{6,2},{3,7},{7,3},{8,12},{12,8},{9,1... | collective-permute-start | bytes 393224 | tf_op jit(solution)/shard_map/ppermute | solution.py:459
  94.2 1.0 %collective-permute-done.15.after2_ref = bf16[4,128,128]{2,1,0:T(8,128)(2,1)S(1)} collective-permute-done((bf16[4,128,128]{2,1,0:T(8,128)(2,1)S(1)}, bf16[4,128,128]{2,1,0:T(8,128)(2,1)S(1)}, u32[]{:S(2)}, u32[]{:S(2)}) %collective-permute-start.15) | collective-permute-done | bytes 131104 | tf_op jit(solution)/shard_map/ppermute | solution.py:459
  95.2 1.2 %final_pass.1 = (bf16[1,2,128,512]{3,2,1,0:T(8,128)(2,1)}, bf16[1,2,128,512]{3,2,1,0:T(8,128)(2,1)}) custom-call(s32[1]{0:T(128)} %bitcast.core_ref, bf16[1,2,128,512]{3,2,1,0:T(8,128)(2,1)S(1)} %copy-done.1, bf16[1,2,128,512]{3,2,1,0:T(8,128)(2,1)S(1)} %copy-done, f32[2,128,512]{2,1,0:T(8,128)S(1)} %copy-done.6, ...), custom_call_target="tpu_custom_call" | custom-call | flops 67108864 | bytes 3145728 | tf_op jit(solution)/shard_map/final_pass/pallas_call | solution.py:447
  (26 shorter events, 0.1 us)
Async XLA Ops:
  0.6 35.1 %copy-start.10 = (s32[1,2,128]{2,1,0:T(2,128)S(1)}, s32[1,2,128]{2,1,0:T(2,128)}, u32[]{:S(2)}) copy-start(s32[1,2,128]{2,1,0:T(2,128)} %mask_ref.1) | copy-start | bytes 3076
  0.6 4.7 %collective-permute-start = (bf16[1,2,128,512]{3,2,1,0:T(8,128)(2,1)}, bf16[1,2,128,512]{3,2,1,0:T(8,128)(2,1)S(1)}, u32[]{:S(2)}, u32[]{:S(2)}) collective-permute-start(bf16[1,2,128,512]{3,2,1,0:T(8,128)(2,1)} %kp_ref.7), channel_id=1, source_target_pairs={{0,4},{4,0},{1,5},{5,1},{2,6},{6,2},{3,7},{7,3},{8,12},{12,8},{9,1... | collective-permute-start | bytes 786440 | tf_op jit(solution)/shard_map/ppermute | solution.py:459
  4.0 1.7 %collective-permute-start.1 = (bf16[1,2,128,512]{3,2,1,0:T(8,128)(2,1)}, bf16[1,2,128,512]{3,2,1,0:T(8,128)(2,1)S(1)}, u32[]{:S(2)}, u32[]{:S(2)}) collective-permute-start(bf16[1,2,128,512]{3,2,1,0:T(8,128)(2,1)} %vp_ref.7), channel_id=1, source_target_pairs={{0,4},{4,0},{1,5},{5,1},{2,6},{6,2},{3,7},{7,3},{8,12},{12,8},{9,1... | collective-permute-start | bytes 786440 | tf_op jit(solution)/shard_map/ppermute | solution.py:459
  4.1 2.0 %collective-permute-start.2 = (bf16[1,2,128,512]{3,2,1,0:T(8,128)(2,1)}, bf16[1,2,128,512]{3,2,1,0:T(8,128)(2,1)S(1)}, u32[]{:S(2)}, u32[]{:S(2)}) collective-permute-start(bf16[1,2,128,512]{3,2,1,0:T(8,128)(2,1)} %kr_ref.3), channel_id=1, source_target_pairs={{0,4},{4,0},{1,5},{5,1},{2,6},{6,2},{3,7},{7,3},{8,12},{12,8},{9,1... | collective-permute-start | bytes 786440 | tf_op jit(solution)/shard_map/ppermute | solution.py:459
  4.5 2.0 %collective-permute-start.3 = (bf16[1,2,128,512]{3,2,1,0:T(8,128)(2,1)}, bf16[1,2,128,512]{3,2,1,0:T(8,128)(2,1)S(1)}, u32[]{:S(2)}, u32[]{:S(2)}) collective-permute-start(bf16[1,2,128,512]{3,2,1,0:T(8,128)(2,1)} %vr_ref.3), channel_id=1, source_target_pairs={{0,4},{4,0},{1,5},{5,1},{2,6},{6,2},{3,7},{7,3},{8,12},{12,8},{9,1... | collective-permute-start | bytes 786440 | tf_op jit(solution)/shard_map/ppermute | solution.py:459
  5.3 32.1 %copy-start.3 = (bf16[1,2,128,512]{3,2,1,0:T(8,128)(2,1)}, bf16[1,2,128,512]{3,2,1,0:T(8,128)(2,1)S(1)}, u32[]{:S(2)}) copy-start(bf16[1,2,128,512]{3,2,1,0:T(8,128)(2,1)S(1)} %collective-permute-done.kp2_ref) | copy-start | bytes 786436
  5.7 37.2 %copy-start.2 = (bf16[1,2,128,512]{3,2,1,0:T(8,128)(2,1)}, bf16[1,2,128,512]{3,2,1,0:T(8,128)(2,1)S(1)}, u32[]{:S(2)}) copy-start(bf16[1,2,128,512]{3,2,1,0:T(8,128)(2,1)S(1)} %collective-permute-done.1.vp2_ref) | copy-start | bytes 786436
  6.1 31.4 %copy-start.5 = (bf16[1,2,128,512]{3,2,1,0:T(8,128)(2,1)}, bf16[1,2,128,512]{3,2,1,0:T(8,128)(2,1)S(1)}, u32[]{:S(2)}) copy-start(bf16[1,2,128,512]{3,2,1,0:T(8,128)(2,1)S(1)} %collective-permute-done.2.kr2_ref) | copy-start | bytes 786436
  6.5 36.4 %copy-start.4 = (bf16[1,2,128,512]{3,2,1,0:T(8,128)(2,1)}, bf16[1,2,128,512]{3,2,1,0:T(8,128)(2,1)S(1)}, u32[]{:S(2)}) copy-start(bf16[1,2,128,512]{3,2,1,0:T(8,128)(2,1)S(1)} %collective-permute-done.3.vr2_ref) | copy-start | bytes 786436
  6.5 31.0 %collective-permute-start.4 = (bf16[1,2,128,2048]{3,2,1,0:T(8,128)(2,1)}, bf16[1,2,128,2048]{3,2,1,0:T(8,128)(2,1)S(1)}, u32[]{:S(2)}, u32[]{:S(2)}) collective-permute-start(bf16[1,2,128,2048]{3,2,1,0:T(8,128)(2,1)} %qp_ref.5), channel_id=1, source_target_pairs={{0,4},{4,0},{1,5},{5,1},{2,6},{6,2},{3,7},{7,3},{8,12},{12,8},{9,1... | collective-permute-start | bytes 3145736 | tf_op jit(solution)/shard_map/ppermute | solution.py:459
  6.8 30.6 %collective-permute-start.5 = (bf16[1,2,128,2048]{3,2,1,0:T(8,128)(2,1)}, bf16[1,2,128,2048]{3,2,1,0:T(8,128)(2,1)}, u32[]{:S(2)}, u32[]{:S(2)}) collective-permute-start(bf16[1,2,128,2048]{3,2,1,0:T(8,128)(2,1)} %qr_ref.3), channel_id=1, source_target_pairs={{0,4},{4,0},{1,5},{5,1},{2,6},{6,2},{3,7},{7,3},{8,12},{12,8},{9,1... | collective-permute-start | bytes 3145736 | tf_op jit(solution)/shard_map/ppermute | solution.py:459
  7.0 39.1 %collective-permute-start.6 = (bf16[1,2,128,2048]{3,2,1,0:T(8,128)(2,1)}, bf16[1,2,128,2048]{3,2,1,0:T(8,128)(2,1)}, u32[]{:S(2)}, u32[]{:S(2)}) collective-permute-start(bf16[1,2,128,2048]{3,2,1,0:T(8,128)(2,1)} %read_ref.1), channel_id=1, source_target_pairs={{0,4},{4,0},{1,5},{5,1},{2,6},{6,2},{3,7},{7,3},{8,12},{12,8},{9,1... | collective-permute-start | bytes 3145736 | tf_op jit(solution)/shard_map/ppermute | solution.py:459
  31.3 14.8 %all-to-all-start.1 = ((bf16[32,32,128]{2,1,0:T(8,128)(2,1)}), bf16[32,32,128]{2,1,0:T(8,128)(2,1)S(1)}, u32[]{:S(2)}, u32[]{:S(2)}) async-start(bf16[32,32,128]{2,1,0:T(8,128)(2,1)} %exclusive_prefix.1), calls=%async_computation.1 | async-start | bytes 524288 | tf_op jit(solution)/shard_map/all_to_all | solution.py:463
  35.7 7.2 %collective-permute-start.7 = (s32[1,2,128]{2,1,0:T(2,128)S(1)}, s32[1,2,128]{2,1,0:T(2,128)S(1)}, u32[]{:S(2)}, u32[]{:S(2)}) collective-permute-start(s32[1,2,128]{2,1,0:T(2,128)S(1)} %copy-done.10), channel_id=1, source_target_pairs={{0,4},{4,0},{1,5},{5,1},{2,6},{6,2},{3,7},{7,3},{8,12},{12,8},{9,1... | collective-permute-start | bytes 3080 | tf_op jit(solution)/shard_map/ppermute | solution.py:459
  37.5 1.0 %copy-start.8 = (bf16[1,2,128,2048]{3,2,1,0:T(8,128)(2,1)}, bf16[1,2,128,2048]{3,2,1,0:T(8,128)(2,1)S(1)}, u32[]{:S(2)}) copy-start(bf16[1,2,128,2048]{3,2,1,0:T(8,128)(2,1)S(1)} %collective-permute-done.4.qp2_ref) | copy-start | bytes 3145732
  42.9 3.2 %copy-start.11 = (s32[1,2,128]{2,1,0:T(2,128)}, s32[1,2,128]{2,1,0:T(2,128)S(1)}, u32[]{:S(2)}) copy-start(s32[1,2,128]{2,1,0:T(2,128)S(1)} %collective-permute-done.7.mask2_ref) | copy-start | bytes 3076
  54.7 17.5 %all-to-all-start.2 = ((bf16[32,24,128]{2,1,0:T(8,128)(2,1)}), bf16[32,24,128]{2,1,0:T(8,128)(2,1)S(1)}, u32[]{:S(2)}, u32[]{:S(2)}) async-start(bf16[32,24,128]{2,1,0:T(8,128)(2,1)} %get-tuple-element.46), calls=%async_computation.2 | async-start | bytes 393216 | tf_op jit(solution)/shard_map/all_to_all | solution.py:463
  61.6 13.8 %copy-start.7 = (f32[4,128,128]{2,1,0:T(8,128)S(1)}, f32[4,128,128]{2,1,0:T(8,128)}, u32[]{:S(2)}) copy-start(f32[4,128,128]{2,1,0:T(8,128)} %get-tuple-element.59.second_ref) | copy-start | bytes 786436
  67.3 27.8 %copy-start = (bf16[1,2,128,512]{3,2,1,0:T(8,128)(2,1)S(1)}, bf16[1,2,128,512]{3,2,1,0:T(8,128)(2,1)}, u32[]{:S(2)}) copy-start(bf16[1,2,128,512]{3,2,1,0:T(8,128)(2,1)} %vp_ref.7) | copy-start | bytes 786436
  67.3 27.8 %copy-start.1 = (bf16[1,2,128,512]{3,2,1,0:T(8,128)(2,1)S(1)}, bf16[1,2,128,512]{3,2,1,0:T(8,128)(2,1)}, u32[]{:S(2)}) copy-start(bf16[1,2,128,512]{3,2,1,0:T(8,128)(2,1)} %kp_ref.7) | copy-start | bytes 786436
  67.3 27.8 %copy-start.6 = (f32[2,128,512]{2,1,0:T(8,128)S(1)}, f32[2,128,512]{2,1,0:T(8,128)}, u32[]{:S(2)}) copy-start(f32[2,128,512]{2,1,0:T(8,128)} %get-tuple-element.61.pair_ref) | copy-start | bytes 1572868
  72.2 15.6 %collective-permute-start.8 = (bf16[128,2048]{1,0:T(8,128)(2,1)}, bf16[128,2048]{1,0:T(8,128)(2,1)S(1)}, u32[]{:S(2)}, u32[]{:S(2)}) collective-permute-start(bf16[128,2048]{1,0:T(8,128)(2,1)} %get-tuple-element.56), channel_id=1, source_target_pairs={{0,4},{4,0},{1,5},{5,1},{2,6},{6,2},{3,7},{7,3},{8,12},{12,8},{9,1... | collective-permute-start | bytes 1572872 | tf_op jit(solution)/shard_map/ppermute | solution.py:459
  74.2 18.0 %collective-permute-start.13 = (f32[2,128,512]{2,1,0:T(8,128)}, f32[2,128,512]{2,1,0:T(8,128)S(1)}, u32[]{:S(2)}, u32[]{:S(2)}) collective-permute-start(f32[2,128,512]{2,1,0:T(8,128)} %get-tuple-element.58), channel_id=1, source_target_pairs={{0,4},{4,0},{1,5},{5,1},{2,6},{6,2},{3,7},{7,3},{8,12},{12,8},{9,1... | collective-permute-start | bytes 1572872 | tf_op jit(solution)/shard_map/ppermute | solution.py:459
  74.9 4.4 %collective-permute-start.9 = (f32[8,128]{1,0:T(8,128)S(1)}, f32[8,128]{1,0:T(8,128)S(1)}, u32[]{:S(2)}, u32[]{:S(2)}) collective-permute-start(f32[8,128]{1,0:T(8,128)S(1)} %get-tuple-element.57), channel_id=1, source_target_pairs={{0,4},{4,0},{1,5},{5,1},{2,6},{6,2},{3,7},{7,3},{8,12},{12,8},{9,1... | collective-permute-start | bytes 12296 | tf_op jit(solution)/shard_map/ppermute | solution.py:459
  75.4 16.7 %collective-permute-start.14 = (f32[4,128,128]{2,1,0:T(8,128)S(1)}, f32[4,128,128]{2,1,0:T(8,128)S(1)}, u32[]{:S(2)}, u32[]{:S(2)}) collective-permute-start(f32[4,128,128]{2,1,0:T(8,128)S(1)} %copy-done.7), channel_id=1, source_target_pairs={{0,4},{4,0},{1,5},{5,1},{2,6},{6,2},{3,7},{7,3},{8,12},{12,8},{9,1... | collective-permute-start | bytes 786440 | tf_op jit(solution)/shard_map/ppermute | solution.py:459
  75.4 16.7 %all-to-all-start.3 = ((bf16[32,16,128]{2,1,0:T(8,128)(2,1)}), bf16[32,16,128]{2,1,0:T(8,128)(2,1)S(1)}, u32[]{:S(2)}, u32[]{:S(2)}) async-start(bf16[32,16,128]{2,1,0:T(8,128)(2,1)} %get-tuple-element.54), calls=%async_computation.3 | async-start | bytes 262144 | tf_op jit(solution)/shard_map/all_to_all | solution.py:463
  79.3 4.0 %collective-permute-start.10 = (f32[8,128]{1,0:T(8,128)S(1)}, f32[8,128]{1,0:T(8,128)S(1)}, u32[]{:S(2)}, u32[]{:S(2)}) collective-permute-start(f32[8,128]{1,0:T(8,128)S(1)} %get-tuple-element.68), channel_id=1, source_target_pairs={{0,1},{1,0},{2,3},{3,2},{4,5},{5,4},{6,7},{7,6},{8,9},{9,8},{10,11... | collective-permute-start | bytes 12296 | tf_op jit(solution)/shard_map/ppermute | solution.py:494
  80.7 4.0 %collective-permute-start.11 = (f32[8,128]{1,0:T(8,128)S(1)}, f32[8,128]{1,0:T(8,128)S(1)}, u32[]{:S(2)}, u32[]{:S(2)}) collective-permute-start(f32[8,128]{1,0:T(8,128)S(1)} %get-tuple-element.68), channel_id=1, source_target_pairs={{0,2},{1,3},{2,0},{3,1},{4,6},{5,7},{6,4},{7,5},{8,10},{9,11},{10,... | collective-permute-start | bytes 12296 | tf_op jit(solution)/shard_map/ppermute | solution.py:494
  83.3 4.0 %collective-permute-start.12 = (f32[8,128]{1,0:T(8,128)S(1)}, f32[8,128]{1,0:T(8,128)S(1)}, u32[]{:S(2)}, u32[]{:S(2)}) collective-permute-start(f32[8,128]{1,0:T(8,128)S(1)} %get-tuple-element.68), channel_id=1, source_target_pairs={{0,3},{1,2},{2,1},{3,0},{4,7},{5,6},{6,5},{7,4},{8,11},{9,10},{10,... | collective-permute-start | bytes 12296 | tf_op jit(solution)/shard_map/ppermute | solution.py:494
  87.8 0.8 copy-start.9
  92.2 3.0 %collective-permute-start.15 = (bf16[4,128,128]{2,1,0:T(8,128)(2,1)S(1)}, bf16[4,128,128]{2,1,0:T(8,128)(2,1)S(1)}, u32[]{:S(2)}, u32[]{:S(2)}) collective-permute-start(bf16[4,128,128]{2,1,0:T(8,128)(2,1)S(1)} %bitcast.5), channel_id=1, source_target_pairs={{0,4},{4,0},{1,5},{5,1},{2,6},{6,2},{3,7},{7,3},{8,12},{12,8},{9,1... | collective-permute-start | bytes 393224 | tf_op jit(solution)/shard_map/ppermute | solution.py:459

commit v2 on v1

v2 whole, which is shorter than its diff:
```python
import math

import jax
import jax.numpy as jnp
from jax import lax
from jax.experimental import pallas as pl
from jax.experimental.pallas import tpu as pltpu
from jax.sharding import Mesh, PartitionSpec as P

HEADS = 16
KV_HEADS = 4
GROUP = HEADS // KV_HEADS
D = 128
T = 128
DPO_BETA = 0.5
EPS = 1e-06
CHIPS = 32
F32 = jnp.float32
BF16 = jnp.bfloat16
SWAP = [(0, 1), (1, 0)]
SCALAR_ROWS = 8
UNROLL = 2
VMEM_LIMIT = 20 * 1024 * 1024
SMALL_VMEM = 8 * 1024 * 1024


WIDE = GROUP * D
IN_HBM = pl.BlockSpec(memory_space=pltpu.HBM)


def out_vmem(count):
    return (pl.BlockSpec(memory_space=pltpu.VMEM),) * count


def far(*arrays):
    return tuple(pltpu.with_memory_space_constraint(x, pltpu.HBM) for x in arrays)


def near(*arrays):
    return tuple(pltpu.with_memory_space_constraint(x, pltpu.VMEM) for x in arrays)


def dot(a, b, ca, cb):
    return lax.dot_general(a, b, (((ca,), (cb,)), ((), ())), preferred_element_type=F32)


def staged(moves, sems):
    copies = [pltpu.make_async_copy(a, b, sems.at[i]) for i, (a, b) in enumerate(moves)]
    for copy in copies:
        copy.start()
    return copies


def own_states_kernel(*refs):
    own_hbm, mask_hbm, mine_ref, mask_ref, own, sems = refs[:4], refs[4], refs[5], refs[6], refs[7:11], refs[11]
    core = lax.axis_index("core")
    moves = [(a.at[0, core], b) for a, b in zip(own_hbm, own)] + [(mask_hbm, mask_ref)]
    for copy in staged(moves, sems):
        copy.wait()
    for model in range(2):
        for g in range(KV_HEADS):
            span = slice(g * D, (g + 1) * D)
            mine_ref[model, g] = dot(own[2 * model][:, span], own[2 * model + 1][:, span], 0, 0)


def own_states(*arrays):
    return pl.pallas_call(
        own_states_kernel,
        out_shape=(pltpu.VMEM((2, KV_HEADS, D, D), F32), pltpu.VMEM((1, 2, T), jnp.int32)),
        in_specs=[IN_HBM] * 5,
        out_specs=out_vmem(2),
        scratch_shapes=[pltpu.VMEM((T, KV_HEADS * D), BF16)] * 4 + [pltpu.SemaphoreType.DMA((5,))],
        name="own_states",
        cost_estimate=pl.CostEstimate(flops=8 * 2 * D * D * T, bytes_accessed=1 << 20, transcendentals=0),
        compiler_params=pltpu.CompilerParams(vmem_limit_bytes=SMALL_VMEM),
    )(*far(*arrays))


def chip_states_kernel(mine_ref, kp2_ref, vp2_ref, kr2_ref, vr2_ref, total_ref):
    core = lax.axis_index("core")
    rows = 2 * KV_HEADS * D // CHIPS
    for model, (k_ref, v_ref) in enumerate(((kp2_ref, vp2_ref), (kr2_ref, vr2_ref))):
        for g in range(KV_HEADS):
            span = slice(g * D, (g + 1) * D)
            total = mine_ref[model, g] + dot(k_ref[0, core, :, span], v_ref[0, core, :, span], 0, 0)
            total = total.astype(BF16)
            for j in range(D // rows):
                total_ref[(model * KV_HEADS + g) * (D // rows) + j] = total[j * rows : (j + 1) * rows]


def chip_states(*arrays):
    return pl.pallas_call(
        chip_states_kernel,
        out_shape=pltpu.VMEM((CHIPS, 2 * KV_HEADS * D // CHIPS, D), BF16),
        in_specs=[pl.BlockSpec(memory_space=pltpu.VMEM)] * 5,
        out_specs=pl.BlockSpec(memory_space=pltpu.VMEM),
        name="chip_states",
        cost_estimate=pl.CostEstimate(flops=8 * 2 * D * D * T, bytes_accessed=1 << 20, transcendentals=0),
        compiler_params=pltpu.CompilerParams(vmem_limit_bytes=SMALL_VMEM),
    )(*near(*arrays))


def prefix_kernel(x_ref, o_ref):
    total = jnp.zeros(x_ref.shape[1:], F32)
    for chip in range(CHIPS):
        o_ref[chip] = total.astype(BF16)
        total = total + x_ref[chip].astype(F32)


def exclusive_prefix(x):
    return pl.pallas_call(
        prefix_kernel,
        out_shape=pltpu.VMEM(x.shape, BF16),
        in_specs=[pl.BlockSpec(memory_space=pltpu.VMEM)],
        out_specs=pl.BlockSpec(memory_space=pltpu.VMEM),
        name="exclusive_prefix",
        cost_estimate=pl.CostEstimate(flops=x.size, bytes_accessed=4 * x.size, transcendentals=0),
        compiler_params=pltpu.CompilerParams(vmem_limit_bytes=SMALL_VMEM),
    )(*near(x))


def suffix_kernel(x_ref, o_ref, score_ref):
    rows = o_ref.shape[1]
    total = jnp.zeros((rows, D), F32)
    pieces = jnp.zeros((SCALAR_ROWS, D), F32)
    for chip in range(CHIPS - 1, -1, -1):
        o_ref[chip] = total.astype(BF16)
        total = total + x_ref[chip, 0:rows].astype(F32)
        pieces = pieces + x_ref[chip, rows : rows + SCALAR_ROWS].astype(F32)
    score = jnp.broadcast_to(jnp.sum(pieces, axis=0, keepdims=True), (SCALAR_ROWS, D))
    score_ref[...] = jnp.where(lax.axis_index("core") == 0, score, -score)


def exclusive_suffix(x):
    rows = x.shape[1] - SCALAR_ROWS
    return pl.pallas_call(
        suffix_kernel,
        out_shape=(
            pltpu.HBM((CHIPS, rows, D), BF16),
            pltpu.VMEM((SCALAR_ROWS, D), F32),
        ),
        in_specs=[pl.BlockSpec(memory_space=pltpu.VMEM)],
        out_specs=(pl.BlockSpec(memory_space=pltpu.VMEM),) * 2,
        name="exclusive_suffix",
        cost_estimate=pl.CostEstimate(flops=x.size, bytes_accessed=4 * x.size, transcendentals=0),
        compiler_params=pltpu.CompilerParams(vmem_limit_bytes=SMALL_VMEM),
    )(*near(x))


def rows_of(x):
    return jnp.concatenate([x[:, r * D : (r + 1) * D] for r in range(GROUP)], axis=0)


def causal_rows():
    row = lax.broadcasted_iota(jnp.int32, (T, T), 0)
    column = lax.broadcasted_iota(jnp.int32, (T, T), 1)
    return jnp.concatenate([row >= column] * GROUP, axis=0)


def at(g, width):
    return pl.ds(pl.multiple_of(g * width, width), width)


def each_group(body):
    lax.fori_loop(0, KV_HEADS, lambda g, _: (body(g), 0)[1], 0, unroll=UNROLL)


def in_vmem(count):
    return [pl.BlockSpec(memory_space=pltpu.VMEM)] * count


PARAMS = pltpu.CompilerParams(vmem_limit_bytes=VMEM_LIMIT)


def forward_kernel(*refs):
    blocks = (refs[:8], refs[8:16])
    before_ref = refs[16]
    pulled_out, total_ref, second_out, carried_out = refs[17:21]
    pulled_ref, second_ref, carried_ref, acc_ref, out_sems = refs[21:]
    core = lax.axis_index("core")
    causal = causal_rows()
    row = lax.broadcasted_iota(jnp.int32, (T, T), 0)
    column = lax.broadcasted_iota(jnp.int32, (T, T), 1)
    kept = []
    for block in blocks:
        mask = block[7][0, pl.ds(core, 1), :].astype(F32)
        mask = jnp.sum(jnp.where(row == column, mask, 0.0), axis=1, keepdims=True)
        kept.append(jnp.broadcast_to(mask, (T, D)))

    def masked(read, mask):
        return jnp.concatenate([read[:, r * D : (r + 1) * D].astype(F32) * mask for r in range(GROUP)], axis=0)

    def row_mean(x):
        return jnp.sum(x, axis=1, keepdims=True) * (1.0 / D)

    def carried_of(model, g, states):
        before = before_ref[model, g].astype(F32)
        after = before + jnp.where(core == 0, states[0], states[1])
        own = jnp.where(core == 0, before, after).astype(BF16)
        other = jnp.where(core == 0, after, before).astype(BF16)
        return own, other

    def forward(scores, query, value, carried):
        raw = dot(jnp.concatenate([scores, query], axis=1), jnp.concatenate([value, carried], axis=0), 1, 0)
        inverse = lax.rsqrt(row_mean(raw * raw) + EPS)
        return raw * inverse, inverse

    acc_ref[...] = jnp.zeros_like(acc_ref)
    chunks = CHIPS // KV_HEADS
    rows = D // chunks

    def copies(g):
        return (
            pltpu.make_async_copy(pulled_ref.at[:, g], pulled_out.at[:, g], out_sems.at[0, g]),
            pltpu.make_async_copy(second_ref.at[g], second_out.at[g], out_sems.at[1, g]),
            pltpu.make_async_copy(carried_ref.at[:, g], carried_out.at[:, g], out_sems.at[2, g]),
        )

    def group(g):
        queries, keys, values, scores, carried = [], [], [], [], []
        for model in range(2):
            queries.append([rows_of(b[model][0, core, :, at(g, WIDE)]) for b in blocks])
            keys.append([b[3 + 2 * model][0, core, :, at(g, D)] for b in blocks])
            values.append([b[4 + 2 * model][0, core, :, at(g, D)] for b in blocks])
            states = [dot(k, v, 0, 0) for k, v in zip(keys[model], values[model])]
            carried.append(carried_of(model, g, states))
            scores.append(
                [jnp.where(causal, dot(q, k, 1, 1), 0.0).astype(BF16) for q, k in zip(queries[model], keys[model])]
            )
        tokens = jnp.zeros((1, D), F32)
        grads = []
        for i in range(2):
            query = queries[0][i]
            read = masked(blocks[i][2][0, core, :, at(g, WIDE)], kept[i])
            normed, inverse = forward(scores[0][i], query, values[0][i], carried[0][i])
            normed_ref = forward(scores[1][i], queries[1][i], values[1][i], carried[1][i])[0]
            reading = read * normed
            tokens = tokens + jnp.sum(reading - read * normed_ref, axis=0, keepdims=True)
            pulled = (inverse * (read - normed * row_mean(reading))).astype(BF16)
            pulled_ref[i, g] = pulled
            carried_ref[i, g] = carried[0][i]
            grads.append(dot(query, pulled, 0, 0))
        acc_ref[0:1, :] = acc_ref[0:1, :] + tokens
        total = (grads[0] + grads[1]).astype(BF16)
        for j in range(chunks):
            total_ref[g * chunks + j, 0:rows, :] = total[j * rows : (j + 1) * rows]
        second_ref[g] = jnp.where(core == 0, grads[1], grads[0])
        for copy in copies(g):
            copy.start()

    each_group(group)
    part = jnp.broadcast_to(jnp.sum(acc_ref[0:1, :], axis=1, keepdims=True), (SCALAR_ROWS, D))
    high = part.astype(BF16).astype(F32)
    middle = (part - high).astype(BF16).astype(F32)
    low = part - high - middle
    place = lax.broadcasted_iota(jnp.int32, (SCALAR_ROWS, D), 0)
    pieces = jnp.where(place == 0, high, jnp.where(place == 1, middle, jnp.where(place == 2, low, 0.0))).astype(BF16)
    for chip in range(CHIPS):
        total_ref[chip, rows : rows + SCALAR_ROWS, :] = pieces
    for g in range(KV_HEADS):
        for copy in copies(g):
            copy.wait()


def forward_pass(*arrays):
    rows = KV_HEADS * D // CHIPS + SCALAR_ROWS
    in_vmem = pl.BlockSpec(memory_space=pltpu.VMEM)
    return pl.pallas_call(
        forward_kernel,
        in_specs=[in_vmem] * 17,
        out_specs=(IN_HBM, in_vmem, IN_HBM, IN_HBM),
        out_shape=(
            pltpu.HBM((2, KV_HEADS, GROUP * T, D), BF16),
            pltpu.HBM((CHIPS, rows, D), BF16),
            pltpu.HBM((KV_HEADS, D, D), F32),
            pltpu.HBM((2, KV_HEADS, D, D), BF16),
        ),
        scratch_shapes=[
            pltpu.VMEM((2, KV_HEADS, GROUP * T, D), BF16),
            pltpu.VMEM((KV_HEADS, D, D), F32),
            pltpu.VMEM((2, KV_HEADS, D, D), BF16),
            pltpu.VMEM((8, D), F32),
            pltpu.SemaphoreType.DMA((3, KV_HEADS)),
        ],
        name="forward_pass",
        cost_estimate=pl.CostEstimate(flops=192 * 2 * D * D * T, bytes_accessed=8 << 20, transcendentals=65536),
        compiler_params=PARAMS,
    )(*near(*arrays))


def backward_kernel(*refs):
    (qp_hbm, kp_hbm, vp_hbm, qp2_hbm, kp2_hbm, vp2_hbm, pulled_hbm, carried_hbm) = refs[:8]
    qg_ref, kv_ref, qg2_ref, kvg2_ref = refs[8:12]
    qp_ref, kp_ref, vp_ref, qp2_ref, kp2_ref, vp2_ref, pulled_ref, carried_ref, sems = refs[12:]
    core = lax.axis_index("core")
    causal = causal_rows()
    moves = [
        (qp_hbm.at[0, core], qp_ref),
        (kp_hbm.at[0, core], kp_ref),
        (vp_hbm.at[0, core], vp_ref),
        (pulled_hbm, pulled_ref),
        (qp2_hbm.at[0, core], qp2_ref),
        (kp2_hbm.at[0, core], kp2_ref),
        (vp2_hbm.at[0, core], vp2_ref),
        (carried_hbm, carried_ref),
    ]
    for copy in staged(moves, sems):
        copy.wait()
    blocks = ((qp_ref, kp_ref, vp_ref, qg_ref, kv_ref), (qp2_ref, kp2_ref, vp2_ref, qg2_ref, kvg2_ref))

    def group(g):
        for i, (q_ref, k_ref, v_ref, q_out, kv_out) in enumerate(blocks):
            query, key, value = rows_of(q_ref[:, at(g, WIDE)]), k_ref[:, at(g, D)], v_ref[:, at(g, D)]
            pulled = pulled_ref[i, g]
            dscore = jnp.where(causal, dot(pulled, value, 1, 1), 0.0).astype(BF16)
            query_grad = (dot(dscore, key, 1, 0) + dot(pulled, carried_ref[i, g], 1, 1)).astype(BF16)
            q_out[:, at(g, WIDE)] = jnp.concatenate([query_grad[r * T : (r + 1) * T] for r in range(GROUP)], axis=1)
            kv_out[0, :, at(g, D)] = dot(dscore, query, 0, 0)
            scores = jnp.where(causal, dot(query, key, 1, 1), 0.0).astype(BF16)
            kv_out[1, :, at(g, D)] = dot(scores, pulled, 0, 0)

    each_group(group)


def backward_pass(*arrays):
    query_shape = pltpu.HBM((T, HEADS * D), BF16)
    pair_shape = pltpu.HBM((2, T, KV_HEADS * D), F32)
    wide, narrow = pltpu.VMEM((T, HEADS * D), BF16), pltpu.VMEM((T, KV_HEADS * D), BF16)
    return pl.pallas_call(
        backward_kernel,
        in_specs=[IN_HBM] * 8,
        out_specs=out_vmem(4),
        out_shape=(query_shape, pair_shape, query_shape, pair_shape),
        scratch_shapes=[
            wide,
            narrow,
            narrow,
            wide,
            narrow,
            narrow,
            pltpu.VMEM((2, KV_HEADS, GROUP * T, D), BF16),
            pltpu.VMEM((2, KV_HEADS, D, D), BF16),
            pltpu.SemaphoreType.DMA((8,)),
        ],
        name="backward_pass",
        cost_estimate=pl.CostEstimate(flops=160 * 2 * D * D * T, bytes_accessed=6 << 20, transcendentals=0),
        compiler_params=PARAMS,
    )(*far(*arrays))


def weight_of(seq, weight_ref):
    return jnp.where(seq == 0, -weight_ref[0:1, 0:1], weight_ref[0:1, 0:1])


def scale_kernel(own_ref, other_ref, weight_ref, o_ref):
    core = lax.axis_index("core")
    for turn, ref in ((0, own_ref), (1, other_ref)):
        seq = lax.rem(core + turn, 2)
        o_ref[0, seq] = (ref[...].astype(F32) * weight_of(seq, weight_ref)).astype(BF16)


def scaled_queries(*arrays):
    return pl.pallas_call(
        scale_kernel,
        in_specs=in_vmem(3),
        out_specs=out_vmem(1)[0],
        out_shape=pltpu.HBM((1, 2, T, HEADS * D), BF16),
        name="scaled_queries",
        cost_estimate=pl.CostEstimate(flops=2 * T * HEADS * D, bytes_accessed=2 << 20, transcendentals=0),
        compiler_params=PARAMS,
    )(*far(*arrays[:2]), arrays[2])


def final_kernel(
    kp_ref,
    vp_ref,
    pair_ref,
    pair2_ref,
    weight_ref,
    after_ref,
    after2_ref,
    second_ref,
    second2_ref,
    ko_ref,
    vo_ref,
):
    core = lax.axis_index("core")
    for turn, after, second, grads_ref in (
        (0, after_ref, second_ref, pair_ref),
        (1, after2_ref, second2_ref, pair2_ref),
    ):
        seq = lax.rem(core + turn, 2)
        weight = weight_of(seq, weight_ref)
        for g in range(KV_HEADS):
            span = slice(g * D, (g + 1) * D)
            later = after[g].astype(F32)
            later = jnp.where(core == 0, later + second[g], later).astype(BF16)
            key_grad = grads_ref[0, :, span] + dot(vp_ref[0, seq, :, span], later, 1, 1)
            value_grad = grads_ref[1, :, span] + dot(kp_ref[0, seq, :, span], later, 1, 0)
            ko_ref[0, seq, :, span] = (weight * key_grad).astype(BF16)
            vo_ref[0, seq, :, span] = (weight * value_grad).astype(BF16)


def final_pass(kp, vp, pair, pair2, weight, after, after2, second, second2):
    shape = pltpu.HBM((1, 2, T, KV_HEADS * D), BF16)
    return pl.pallas_call(
        final_kernel,
        out_shape=(shape, shape),
        in_specs=[pl.BlockSpec(memory_space=pltpu.VMEM)] * 9,
        out_specs=(pl.BlockSpec(memory_space=pltpu.VMEM),) * 2,
        name="final_pass",
        cost_estimate=pl.CostEstimate(flops=16 * 2 * D * D * T, bytes_accessed=3 << 20, transcendentals=0),
        compiler_params=pltpu.CompilerParams(vmem_limit_bytes=SMALL_VMEM),
    )(*near(kp, vp, pair, pair2), weight, *near(after, after2, second, second2))


def swap(x):
    return lax.ppermute(x, "core", SWAP)


def exchange(x):
    return lax.all_to_all(x, "chip", 0, 0, tiled=True)


def shards(qp, kp, vp, qr, kr, vr, read, mask):
    shared = tuple(swap(x) for x in (kp, vp, kr, vr, mask))
    held = own_states(kp, vp, kr, vr, mask)
    shared, (mine, mask), (qp, qr, read) = lax.optimization_barrier((shared, held, (qp, qr, read)))
    kp2, vp2, kr2, vr2, mask2 = shared
    qp2, qr2, read2 = swap(qp), swap(qr), swap(read)
    total = chip_states(mine, kp2, vp2, kr2, vr2)
    spread = exchange(total)
    before = exchange(exclusive_prefix(spread)).reshape(2, KV_HEADS, D, D)
    own = (qp, qr, read, kp, vp, kr, vr, mask)
    other = (qp2, qr2, read2, kp2, vp2, kr2, vr2, mask2)
    pulled, payload, second, carried = forward_pass(*own, *other, before)
    arrived = exchange(payload)
    second2 = swap(second)
    grads = backward_pass(qp, kp, vp, qp2, kp2, vp2, pulled, carried)
    arrived, grads = lax.optimization_barrier((arrived, grads))
    qg, pair, qg2, pair2 = grads
    qg2, pair2 = swap(qg2), swap(pair2)
    after, mine = exclusive_suffix(arrived)
    after = exchange(after).reshape(KV_HEADS, D, D)

    delta = mine + swap(mine)
    loss = jax.nn.softplus(-DPO_BETA * delta)
    pairs = lax.axis_size("dp")
    one, two, three = (lax.ppermute(loss, "dp", [(i, i ^ k) for i in range(pairs)]) for k in (1, 2, 3))
    pair_loss = ((loss + one) + (two + three)) / pairs
    scale = math.sqrt(HEADS * D * T * lax.axis_size("chip") * 2)
    weight = DPO_BETA * jax.nn.sigmoid(-DPO_BETA * delta) * scale
    query_rows = scaled_queries(qg, qg2, weight)
    after, query_rows, pair2, second2 = lax.optimization_barrier((after, query_rows, pair2, second2))
    key_rows, value_rows = final_pass(kp, vp, pair, pair2, weight, after, swap(after), second, second2)
    return query_rows, key_rows, value_rows, pair_loss[0, 0]


def solution(mesh):
    devices = mesh.devices
    split = Mesh(devices.reshape(devices.shape[0] // 2, 2, devices.shape[1]), ("chip", "core", "dp"))
    placed = P("dp", None, ("chip", "core"), None)
    return jax.shard_map(
        shards,
        mesh=split,
        in_specs=(placed,) * 7 + (P("dp", None, ("chip", "core")),),
        out_specs=(placed, placed, placed, P()),
        check_vma=False,
    )
```

time: 96.9 us -> 88.5 us (0.913)
  blocking collectives: 20.9 us -> 36 us
  Pallas kernels: 27.2 us -> 18.8 us
  starting transfers between devices: 31.5 us -> 24.3 us
  waiting for transfers between devices: 13.6 us -> 7.09 us
  local copies, waits for them, and re-layouts: 2.29 us -> 1.05 us
    all_to_all x1 -> x2, blocking collectives: 20.9 us -> 36 us  [exchange(): return lax.all_to_all(x, 'chip', 0, 0, tiled=True)]
    pallas_call x6, Pallas kernels: 25.3 us -> 17.6 us  [the longest x1 6.52 us: forward_pass(): pl.pallas_call(forward_kernel, in_specs=[in_vmem] * 17, out_specs=(IN_HBM...]
    all_to_all x3 -> x2, starting transfers between devices: 15.1 us -> 9.73 us  [exchange(): return lax.all_to_all(x, 'chip', 0, 0, tiled=True)]
    ppermute x3, waiting for transfers between devices: 2.69 us -> 0.01 us  [shards(): lax.ppermute(loss, 'dp', [(i, i ^ k) for i in range(pairs)])]
    all_to_all x3 -> x2, waiting for transfers between devices: 8.04 us -> 5.72 us  [exchange(): return lax.all_to_all(x, 'chip', 0, 0, tiled=True)]
    ppermute x3, starting transfers between devices: 5.27 us -> 3.5 us  [shards(): lax.ppermute(loss, 'dp', [(i, i ^ k) for i in range(pairs)])]
    ppermute x13, waiting for transfers between devices: 2.88 us -> 1.37 us  [swap(): return lax.ppermute(x, 'core', SWAP)]
    unnamed x24 -> x30, local copies, waits for them, and re-layouts: 1.78 us -> 0.54 us
  transfers between devices with their start and end apart: 19 -> 18, of which waited for: 9 -> 5; matrix products, arithmetic and copies ran while one was open for 1% -> 1% of each run, Pallas kernels for 18% -> 13%
where the time goes in v2:
time: 88.5 us; the launch traced here: 88.1 us
  blocking collectives  36 us (41%)
  starting transfers between devices  24.3 us (27%)
  Pallas kernels  18.8 us (21%)
  waiting for transfers between devices  7.09 us (8%)
  local copies, waits for them, and re-layouts  1.05 us (1%)
    all_to_all x2, blocking collectives, exchange(): return lax.all_to_all(x, 'chip', 0, 0, tiled=True)  36 us
    ppermute x13, starting transfers between devices, swap(): return lax.ppermute(x, 'core', SWAP)  11.1 us
    all_to_all x2, starting transfers between devices, exchange(): return lax.all_to_all(x, 'chip', 0, 0, tiled=True)  9.73 us
    pallas_call x1, Pallas kernels, forward_pass(): pl.pallas_call(forward_kernel, in_specs=[in_vmem] * 17, out_specs=(IN_HBM...  6.52 us
    pallas_call x1, Pallas kernels, backward_pass(): pl.pallas_call(backward_kernel, in_specs=[IN_HBM] * 8, out_specs=out_vmem...  6.15 us
    all_to_all x2, waiting for transfers between devices, exchange(): return lax.all_to_all(x, 'chip', 0, 0, tiled=True)  5.72 us
    ppermute x3, starting transfers between devices, shards(): lax.ppermute(loss, 'dp', [(i, i ^ k) for i in range(pairs)])  3.5 us
    pallas_call x1, Pallas kernels, scaled_queries(): pl.pallas_call(scale_kernel, in_specs=in_vmem(3), out_specs=out_vmem(1)[0...  2.62 us
  transfers between devices with their start and end apart: 18, of which 5 were waited for; matrix products, arithmetic and copies ran while one was open for 1% of the time, Pallas kernels for 13%

profile of v2, /device:TPU:1, one launch (start us, length us, event | category | flops | bytes accessed | tf_op | source)
XLA Modules:
  0.0 88.1 jit_solution(701334567396771250)
XLA Ops:
  0.6 0.0 copy-start
  0.6 3.3 %collective-permute-start.2 = (bf16[1,2,128,512]{3,2,1,0:T(8,128)(2,1)}, bf16[1,2,128,512]{3,2,1,0:T(8,128)(2,1)S(1)}, u32[]{:S(2)}, u32[]{:S(2)}) collective-permute-start(bf16[1,2,128,512]{3,2,1,0:T(8,128)(2,1)} %refs_5_.1), channel_id=1, source_target_pairs={{0,4},{4,0},{1,5},{5,1},{2,6},{6,2},{3,7},{7,3},{8,12},{12,8},{9,1... | collective-permute-start | bytes 786440 | tf_op jit(solution)/shard_map/ppermute | solution.py:418
  4.0 0.1 collective-permute-start.3
  4.1 0.4 collective-permute-start
  4.5 0.1 collective-permute-start.1
  4.6 0.4 collective-permute-start.4
  5.0 1.4 %own_states.1 = (f32[2,4,128,128]{3,2,1,0:T(8,128)S(1)}, s32[1,2,128]{2,1,0:T(2,128)S(1)}) custom-call(bf16[1,2,128,512]{3,2,1,0:T(8,128)(2,1)} %kp_ref.1, bf16[1,2,128,512]{3,2,1,0:T(8,128)(2,1)} %vp_ref.1, bf16[1,2,128,512]{3,2,1,0:T(8,128)(2,1)} %refs_5_.1, bf16[1,2,128,512]{3,2,1,0:T(8,128)(2,1)} %refs_6_.1, s32[1,2,128]{2,1,0:T(2,128)} %refs_4_.2), custom_call_target="tpu_custom_call" | custom-call | flops 33554432 | bytes 1048576 | tf_op jit(solution)/shard_map/own_states/pallas_call | solution.py:67
  6.4 0.1 collective-permute-done.4.refs_15_
  6.5 0.0 collective-permute-done.2.kr2_ref.refs_13_
  6.5 0.0 collective-permute-done.3.vr2_ref.refs_14_
  6.5 0.0 collective-permute-done.kp2_ref.refs_11_.refs_4_
  6.5 0.0 copy-start.6
  6.5 0.0 copy-start.7
  6.5 0.5 collective-permute-start.6
  7.0 0.1 collective-permute-start.7
  7.1 0.4 collective-permute-start.5
  7.5 0.3 chip_states.1
  7.8 0.0 copy-start.8
  7.8 21.1 %all_to_all.20.x_ref = bf16[32,32,128]{2,1,0:T(8,128)(2,1)S(1)} all-to-all(bf16[32,32,128]{2,1,0:T(8,128)(2,1)S(1)} %chip_states.1), channel_id=1, replica_groups=mesh['chip'=32,'core'=2,'dp'=4] {'chip'}, dimensions={0} | all-to-all | bytes 524288 | tf_op jit(solution)/shard_map/all_to_all | solution.py:422
  28.9 0.0 copy-start.2
  28.9 0.0 copy-start.4
  28.9 14.9 %all_to_all.21 = bf16[32,32,128]{2,1,0:T(8,128)(2,1)S(1)} all-to-all(bf16[32,32,128]{2,1,0:T(8,128)(2,1)S(1)} %exclusive_prefix.1), channel_id=1, replica_groups=mesh['chip'=32,'core'=2,'dp'=4] {'chip'}, dimensions={0} | all-to-all | bytes 524288 | tf_op jit(solution)/shard_map/all_to_all | solution.py:422
  43.8 0.0 collective-permute-done.6.refs_9_
  43.8 0.0 collective-permute-done.7.refs_10_
  43.8 0.0 copy-start.1
  43.9 6.5 %forward_pass.1 = (bf16[2,4,512,128]{3,2,1,0:T(8,128)(2,1)}, bf16[32,24,128]{2,1,0:T(8,128)(2,1)}, f32[4,128,128]{2,1,0:T(8,128)}, bf16[2,4,128,128]{3,2,1,0:T(8,128)(2,1)}) custom-call(bf16[1,2,128,2048]{3,2,1,0:T(8,128)(2,1)S(1)} %copy-done, bf16[1,2,128,2048]{3,2,1,0:T(8,128)(2,1)S(1)} %copy-done.8, bf16[1,2,128,2048]{3,2,1,0:T(8,128)(2,1)S(1)} %copy-done.9, ...), custom_call_target="tpu_custom_call" | custom-call | flops 805306368 | bytes 8388608 | tf_op jit(solution)/shard_map/forward_pass/pallas_call | solution.py:268
  50.4 5.1 %all-to-all-start.2 = ((bf16[32,24,128]{2,1,0:T(8,128)(2,1)}), bf16[32,24,128]{2,1,0:T(8,128)(2,1)S(1)}, u32[]{:S(2)}, u32[]{:S(2)}) async-start(bf16[32,24,128]{2,1,0:T(8,128)(2,1)} %get-tuple-element.49), calls=%async_computation.2 | async-start | bytes 393216 | tf_op jit(solution)/shard_map/all_to_all | solution.py:422
  55.5 6.2 %backward_pass.1 = (bf16[128,2048]{1,0:T(8,128)(2,1)}, f32[2,128,512]{2,1,0:T(8,128)}, bf16[128,2048]{1,0:T(8,128)(2,1)}, f32[2,128,512]{2,1,0:T(8,128)}) custom-call(bf16[1,2,128,2048]{3,2,1,0:T(8,128)(2,1)} %refs_0_.3, bf16[1,2,128,512]{3,2,1,0:T(8,128)(2,1)} %kp_ref.1, bf16[1,2,128,512]{3,2,1,0:T(8,128)(2,1)} %vp_ref.1, ...), custom_call_target="tpu_custom_call" | custom-call | flops 671088640 | bytes 6291456 | tf_op jit(solution)/shard_map/backward_pass/pallas_call | solution.py:329
  61.7 3.7 %all-to-all-done.2.x_ref = bf16[32,24,128]{2,1,0:T(8,128)(2,1)S(1)} async-done(((bf16[32,24,128]{2,1,0:T(8,128)(2,1)}), bf16[32,24,128]{2,1,0:T(8,128)(2,1)S(1)}, u32[]{:S(2)}, u32[]{:S(2)}) %all-to-all-start.2) | async-done | bytes 196640 | tf_op jit(solution)/shard_map/all_to_all | solution.py:422
  65.4 3.3 %collective-permute-start.8 = (bf16[128,2048]{1,0:T(8,128)(2,1)}, bf16[128,2048]{1,0:T(8,128)(2,1)S(1)}, u32[]{:S(2)}, u32[]{:S(2)}) collective-permute-start(bf16[128,2048]{1,0:T(8,128)(2,1)} %get-tuple-element.59), channel_id=1, source_target_pairs={{0,4},{4,0},{1,5},{5,1},{2,6},{6,2},{3,7},{7,3},{8,12},{12,8},{9,1... | collective-permute-start | bytes 1572872 | tf_op jit(solution)/shard_map/ppermute | solution.py:418
  68.7 0.0 collective-permute-start.10
  68.8 0.5 collective-permute-start.11
  69.3 0.7 exclusive_suffix.1
  70.0 4.6 %all-to-all-start.3 = ((bf16[32,16,128]{2,1,0:T(8,128)(2,1)}), bf16[32,16,128]{2,1,0:T(8,128)(2,1)S(1)}, u32[]{:S(2)}, u32[]{:S(2)}) async-start(bf16[32,16,128]{2,1,0:T(8,128)(2,1)} %get-tuple-element.57), calls=%async_computation.3 | async-start | bytes 262144 | tf_op jit(solution)/shard_map/all_to_all | solution.py:422
  74.6 0.4 collective-permute-start.9
  75.1 0.8 collective-permute-done.9
  75.9 2.8 %collective-permute-start.15 = (f32[8,128]{1,0:T(8,128)S(1)}, f32[8,128]{1,0:T(8,128)S(1)}, u32[]{:S(2)}, u32[]{:S(2)}) collective-permute-start(f32[8,128]{1,0:T(8,128)S(1)} %get-tuple-element.70), channel_id=1, source_target_pairs={{0,3},{1,2},{2,1},{3,0},{4,7},{5,6},{6,5},{7,4},{8,11},{9,10},{10,... | collective-permute-start | bytes 12296 | tf_op jit(solution)/shard_map/ppermute | solution.py:449
  78.7 0.3 collective-permute-start.14
  79.1 0.3 collective-permute-start.13
  79.4 0.5 copy-done.14
  79.9 2.6 %scaled_queries.1 = bf16[1,2,128,2048]{3,2,1,0:T(8,128)(2,1)} custom-call(bf16[128,2048]{1,0:T(8,128)(2,1)} %get-tuple-element.58.own_ref, bf16[128,2048]{1,0:T(8,128)(2,1)} %copy-done.14, f32[8,128]{1,0:T(8,128)S(1)} %get-tuple-element.71.weight_ref), custom_call_target="tpu_custom_call" | custom-call | flops 524288 | bytes 2097152 | tf_op jit(solution)/shard_map/scaled_queries/pallas_call | solution.py:363
  82.5 0.0 collective-permute-done.11.second2_ref
  82.5 2.0 %all-to-all-done.3 = bf16[32,16,128]{2,1,0:T(8,128)(2,1)S(1)} async-done(((bf16[32,16,128]{2,1,0:T(8,128)(2,1)}), bf16[32,16,128]{2,1,0:T(8,128)(2,1)S(1)}, u32[]{:S(2)}, u32[]{:S(2)}) %all-to-all-start.3) | async-done | bytes 131104 | tf_op jit(solution)/shard_map/all_to_all | solution.py:422
  84.5 0.0 collective-permute-done.10.pair2_ref
  84.5 1.4 %collective-permute-start.12 = (bf16[4,128,128]{2,1,0:T(8,128)(2,1)S(1)}, bf16[4,128,128]{2,1,0:T(8,128)(2,1)S(1)}, u32[]{:S(2)}, u32[]{:S(2)}) collective-permute-start(bf16[4,128,128]{2,1,0:T(8,128)(2,1)S(1)} %bitcast.4), channel_id=1, source_target_pairs={{0,4},{4,0},{1,5},{5,1},{2,6},{6,2},{3,7},{7,3},{8,12},{12,8},{9,1... | collective-permute-start | bytes 393224 | tf_op jit(solution)/shard_map/ppermute | solution.py:418
  86.0 0.5 slice.3
  86.5 0.4 collective-permute-done.12.after2_ref
  87.0 1.2 %final_pass.1 = (bf16[1,2,128,512]{3,2,1,0:T(8,128)(2,1)}, bf16[1,2,128,512]{3,2,1,0:T(8,128)(2,1)}) custom-call(bf16[1,2,128,512]{3,2,1,0:T(8,128)(2,1)S(1)} %copy-done.3, bf16[1,2,128,512]{3,2,1,0:T(8,128)(2,1)S(1)} %copy-done.5, f32[2,128,512]{2,1,0:T(8,128)S(1)} %copy-done.12, f32[2,128,512]{2,1,0:T(8,128)S(1)} %collective-permute-done.10.pair2_ref, ...), custom_call_target="tpu_custom_call" | custom-call | flops 67108864 | bytes 3145728 | tf_op jit(solution)/shard_map/final_pass/pallas_call | solution.py:406
  (31 shorter events, 0.1 us)
Async XLA Ops:
  0.6 6.5 %copy-start = (bf16[1,2,128,2048]{3,2,1,0:T(8,128)(2,1)S(1)}, bf16[1,2,128,2048]{3,2,1,0:T(8,128)(2,1)}, u32[]{:S(2)}) copy-start(bf16[1,2,128,2048]{3,2,1,0:T(8,128)(2,1)} %refs_0_.3) | copy-start | bytes 3145732
  0.6 5.8 %collective-permute-start.2 = (bf16[1,2,128,512]{3,2,1,0:T(8,128)(2,1)}, bf16[1,2,128,512]{3,2,1,0:T(8,128)(2,1)S(1)}, u32[]{:S(2)}, u32[]{:S(2)}) collective-permute-start(bf16[1,2,128,512]{3,2,1,0:T(8,128)(2,1)} %refs_5_.1), channel_id=1, source_target_pairs={{0,4},{4,0},{1,5},{5,1},{2,6},{6,2},{3,7},{7,3},{8,12},{12,8},{9,1... | collective-permute-start | bytes 786440 | tf_op jit(solution)/shard_map/ppermute | solution.py:418
  4.0 2.5 %collective-permute-start.3 = (bf16[1,2,128,512]{3,2,1,0:T(8,128)(2,1)}, bf16[1,2,128,512]{3,2,1,0:T(8,128)(2,1)S(1)}, u32[]{:S(2)}, u32[]{:S(2)}) collective-permute-start(bf16[1,2,128,512]{3,2,1,0:T(8,128)(2,1)} %refs_6_.1), channel_id=1, source_target_pairs={{0,4},{4,0},{1,5},{5,1},{2,6},{6,2},{3,7},{7,3},{8,12},{12,8},{9,1... | collective-permute-start | bytes 786440 | tf_op jit(solution)/shard_map/ppermute | solution.py:418
  4.1 2.4 %collective-permute-start = (bf16[1,2,128,512]{3,2,1,0:T(8,128)(2,1)}, bf16[1,2,128,512]{3,2,1,0:T(8,128)(2,1)S(1)}, u32[]{:S(2)}, u32[]{:S(2)}) collective-permute-start(bf16[1,2,128,512]{3,2,1,0:T(8,128)(2,1)} %kp_ref.1), channel_id=1, source_target_pairs={{0,4},{4,0},{1,5},{5,1},{2,6},{6,2},{3,7},{7,3},{8,12},{12,8},{9,1... | collective-permute-start | bytes 786440 | tf_op jit(solution)/shard_map/ppermute | solution.py:418
  4.5 2.0 %collective-permute-start.1 = (bf16[1,2,128,512]{3,2,1,0:T(8,128)(2,1)}, bf16[1,2,128,512]{3,2,1,0:T(8,128)(2,1)S(1)}, u32[]{:S(2)}, u32[]{:S(2)}) collective-permute-start(bf16[1,2,128,512]{3,2,1,0:T(8,128)(2,1)} %vp_ref.1), channel_id=1, source_target_pairs={{0,4},{4,0},{1,5},{5,1},{2,6},{6,2},{3,7},{7,3},{8,12},{12,8},{9,1... | collective-permute-start | bytes 786440 | tf_op jit(solution)/shard_map/ppermute | solution.py:418
  4.6 1.9 %collective-permute-start.4 = (s32[1,2,128]{2,1,0:T(2,128)}, s32[1,2,128]{2,1,0:T(2,128)S(1)}, u32[]{:S(2)}, u32[]{:S(2)}) collective-permute-start(s32[1,2,128]{2,1,0:T(2,128)} %refs_4_.2), channel_id=1, source_target_pairs={{0,4},{4,0},{1,5},{5,1},{2,6},{6,2},{3,7},{7,3},{8,12},{12,8},{9,1... | collective-permute-start | bytes 3080 | tf_op jit(solution)/shard_map/ppermute | solution.py:418
  6.5 37.3 %copy-start.6 = (bf16[1,2,128,512]{3,2,1,0:T(8,128)(2,1)}, bf16[1,2,128,512]{3,2,1,0:T(8,128)(2,1)S(1)}, u32[]{:S(2)}) copy-start(bf16[1,2,128,512]{3,2,1,0:T(8,128)(2,1)S(1)} %collective-permute-done.kp2_ref.refs_11_.refs_4_) | copy-start | bytes 786436
  6.5 37.3 %copy-start.7 = (bf16[1,2,128,512]{3,2,1,0:T(8,128)(2,1)}, bf16[1,2,128,512]{3,2,1,0:T(8,128)(2,1)S(1)}, u32[]{:S(2)}) copy-start(bf16[1,2,128,512]{3,2,1,0:T(8,128)(2,1)S(1)} %collective-permute-done.1.vp2_ref.refs_12_.refs_5_) | copy-start | bytes 786436
  6.5 37.3 %collective-permute-start.6 = (bf16[1,2,128,2048]{3,2,1,0:T(8,128)(2,1)}, bf16[1,2,128,2048]{3,2,1,0:T(8,128)(2,1)S(1)}, u32[]{:S(2)}, u32[]{:S(2)}) collective-permute-start(bf16[1,2,128,2048]{3,2,1,0:T(8,128)(2,1)} %refs_1_.3), channel_id=1, source_target_pairs={{0,4},{4,0},{1,5},{5,1},{2,6},{6,2},{3,7},{7,3},{8,12},{12,8},{9,1... | collective-permute-start | bytes 3145736 | tf_op jit(solution)/shard_map/ppermute | solution.py:418
  7.0 36.8 %collective-permute-start.7 = (bf16[1,2,128,2048]{3,2,1,0:T(8,128)(2,1)}, bf16[1,2,128,2048]{3,2,1,0:T(8,128)(2,1)S(1)}, u32[]{:S(2)}, u32[]{:S(2)}) collective-permute-start(bf16[1,2,128,2048]{3,2,1,0:T(8,128)(2,1)} %refs_2_.3), channel_id=1, source_target_pairs={{0,4},{4,0},{1,5},{5,1},{2,6},{6,2},{3,7},{7,3},{8,12},{12,8},{9,1... | collective-permute-start | bytes 3145736 | tf_op jit(solution)/shard_map/ppermute | solution.py:418
  7.1 36.7 %collective-permute-start.5 = (bf16[1,2,128,2048]{3,2,1,0:T(8,128)(2,1)S(1)}, bf16[1,2,128,2048]{3,2,1,0:T(8,128)(2,1)S(1)}, u32[]{:S(2)}, u32[]{:S(2)}) collective-permute-start(bf16[1,2,128,2048]{3,2,1,0:T(8,128)(2,1)S(1)} %copy-done), channel_id=1, source_target_pairs={{0,4},{4,0},{1,5},{5,1},{2,6},{6,2},{3,7},{7,3},{8,12},{12,8},{9,1... | collective-permute-start | bytes 3145736 | tf_op jit(solution)/shard_map/ppermute | solution.py:418
  7.5 36.4 %copy-start.9 = (bf16[1,2,128,2048]{3,2,1,0:T(8,128)(2,1)S(1)}, bf16[1,2,128,2048]{3,2,1,0:T(8,128)(2,1)}, u32[]{:S(2)}) copy-start(bf16[1,2,128,2048]{3,2,1,0:T(8,128)(2,1)} %refs_2_.3) | copy-start | bytes 3145732
  7.5 36.4 %copy-start.10 = (bf16[1,2,128,512]{3,2,1,0:T(8,128)(2,1)S(1)}, bf16[1,2,128,512]{3,2,1,0:T(8,128)(2,1)}, u32[]{:S(2)}) copy-start(bf16[1,2,128,512]{3,2,1,0:T(8,128)(2,1)} %refs_5_.1) | copy-start | bytes 786436
  7.5 36.4 %copy-start.11 = (bf16[1,2,128,512]{3,2,1,0:T(8,128)(2,1)S(1)}, bf16[1,2,128,512]{3,2,1,0:T(8,128)(2,1)}, u32[]{:S(2)}) copy-start(bf16[1,2,128,512]{3,2,1,0:T(8,128)(2,1)} %refs_6_.1) | copy-start | bytes 786436
  7.8 36.1 %copy-start.8 = (bf16[1,2,128,2048]{3,2,1,0:T(8,128)(2,1)S(1)}, bf16[1,2,128,2048]{3,2,1,0:T(8,128)(2,1)}, u32[]{:S(2)}) copy-start(bf16[1,2,128,2048]{3,2,1,0:T(8,128)(2,1)} %refs_1_.3) | copy-start | bytes 3145732
  28.9 15.0 %copy-start.2 = (bf16[1,2,128,512]{3,2,1,0:T(8,128)(2,1)S(1)}, bf16[1,2,128,512]{3,2,1,0:T(8,128)(2,1)}, u32[]{:S(2)}) copy-start(bf16[1,2,128,512]{3,2,1,0:T(8,128)(2,1)} %kp_ref.1) | copy-start | bytes 786436
  28.9 15.0 %copy-start.4 = (bf16[1,2,128,512]{3,2,1,0:T(8,128)(2,1)S(1)}, bf16[1,2,128,512]{3,2,1,0:T(8,128)(2,1)}, u32[]{:S(2)}) copy-start(bf16[1,2,128,512]{3,2,1,0:T(8,128)(2,1)} %vp_ref.1) | copy-start | bytes 786436
  43.8 6.6 %copy-start.1 = (bf16[1,2,128,2048]{3,2,1,0:T(8,128)(2,1)}, bf16[1,2,128,2048]{3,2,1,0:T(8,128)(2,1)S(1)}, u32[]{:S(2)}) copy-start(bf16[1,2,128,2048]{3,2,1,0:T(8,128)(2,1)S(1)} %collective-permute-done.5.refs_8_.refs_3_) | copy-start | bytes 3145732
  50.4 15.0 %all-to-all-start.2 = ((bf16[32,24,128]{2,1,0:T(8,128)(2,1)}), bf16[32,24,128]{2,1,0:T(8,128)(2,1)S(1)}, u32[]{:S(2)}, u32[]{:S(2)}) async-start(bf16[32,24,128]{2,1,0:T(8,128)(2,1)} %get-tuple-element.49), calls=%async_computation.2 | async-start | bytes 393216 | tf_op jit(solution)/shard_map/all_to_all | solution.py:422
  55.5 13.2 %copy-start.13 = (f32[4,128,128]{2,1,0:T(8,128)S(1)}, f32[4,128,128]{2,1,0:T(8,128)}, u32[]{:S(2)}) copy-start(f32[4,128,128]{2,1,0:T(8,128)} %get-tuple-element.62.second_ref) | copy-start | bytes 786436
  65.4 13.7 %collective-permute-start.8 = (bf16[128,2048]{1,0:T(8,128)(2,1)}, bf16[128,2048]{1,0:T(8,128)(2,1)S(1)}, u32[]{:S(2)}, u32[]{:S(2)}) collective-permute-start(bf16[128,2048]{1,0:T(8,128)(2,1)} %get-tuple-element.59), channel_id=1, source_target_pairs={{0,4},{4,0},{1,5},{5,1},{2,6},{6,2},{3,7},{7,3},{8,12},{12,8},{9,1... | collective-permute-start | bytes 1572872 | tf_op jit(solution)/shard_map/ppermute | solution.py:418
  68.7 15.8 %collective-permute-start.10 = (f32[2,128,512]{2,1,0:T(8,128)}, f32[2,128,512]{2,1,0:T(8,128)S(1)}, u32[]{:S(2)}, u32[]{:S(2)}) collective-permute-start(f32[2,128,512]{2,1,0:T(8,128)} %get-tuple-element.61), channel_id=1, source_target_pairs={{0,4},{4,0},{1,5},{5,1},{2,6},{6,2},{3,7},{7,3},{8,12},{12,8},{9,1... | collective-permute-start | bytes 1572872 | tf_op jit(solution)/shard_map/ppermute | solution.py:418
  68.8 13.7 %collective-permute-start.11 = (f32[4,128,128]{2,1,0:T(8,128)S(1)}, f32[4,128,128]{2,1,0:T(8,128)S(1)}, u32[]{:S(2)}, u32[]{:S(2)}) collective-permute-start(f32[4,128,128]{2,1,0:T(8,128)S(1)} %copy-done.13), channel_id=1, source_target_pairs={{0,4},{4,0},{1,5},{5,1},{2,6},{6,2},{3,7},{7,3},{8,12},{12,8},{9,1... | collective-permute-start | bytes 786440 | tf_op jit(solution)/shard_map/ppermute | solution.py:418
  70.0 14.6 %all-to-all-start.3 = ((bf16[32,16,128]{2,1,0:T(8,128)(2,1)}), bf16[32,16,128]{2,1,0:T(8,128)(2,1)S(1)}, u32[]{:S(2)}, u32[]{:S(2)}) async-start(bf16[32,16,128]{2,1,0:T(8,128)(2,1)} %get-tuple-element.57), calls=%async_computation.3 | async-start | bytes 262144 | tf_op jit(solution)/shard_map/all_to_all | solution.py:422
  74.6 1.3 %collective-permute-start.9 = (f32[8,128]{1,0:T(8,128)S(1)}, f32[8,128]{1,0:T(8,128)S(1)}, u32[]{:S(2)}, u32[]{:S(2)}) collective-permute-start(f32[8,128]{1,0:T(8,128)S(1)} %get-tuple-element.60), channel_id=1, source_target_pairs={{0,4},{4,0},{1,5},{5,1},{2,6},{6,2},{3,7},{7,3},{8,12},{12,8},{9,1... | collective-permute-start | bytes 12296 | tf_op jit(solution)/shard_map/ppermute | solution.py:418
  75.9 10.1 %collective-permute-start.15 = (f32[8,128]{1,0:T(8,128)S(1)}, f32[8,128]{1,0:T(8,128)S(1)}, u32[]{:S(2)}, u32[]{:S(2)}) collective-permute-start(f32[8,128]{1,0:T(8,128)S(1)} %get-tuple-element.70), channel_id=1, source_target_pairs={{0,3},{1,2},{2,1},{3,0},{4,7},{5,6},{6,5},{7,4},{8,11},{9,10},{10,... | collective-permute-start | bytes 12296 | tf_op jit(solution)/shard_map/ppermute | solution.py:449
  78.7 7.3 %collective-permute-start.14 = (f32[8,128]{1,0:T(8,128)S(1)}, f32[8,128]{1,0:T(8,128)S(1)}, u32[]{:S(2)}, u32[]{:S(2)}) collective-permute-start(f32[8,128]{1,0:T(8,128)S(1)} %get-tuple-element.70), channel_id=1, source_target_pairs={{0,2},{1,3},{2,0},{3,1},{4,6},{5,7},{6,4},{7,5},{8,10},{9,11},{10,... | collective-permute-start | bytes 12296 | tf_op jit(solution)/shard_map/ppermute | solution.py:449
  79.1 0.8 copy-start.14
  79.1 6.9 %collective-permute-start.13 = (f32[8,128]{1,0:T(8,128)S(1)}, f32[8,128]{1,0:T(8,128)S(1)}, u32[]{:S(2)}, u32[]{:S(2)}) collective-permute-start(f32[8,128]{1,0:T(8,128)S(1)} %get-tuple-element.70), channel_id=1, source_target_pairs={{0,1},{1,0},{2,3},{3,2},{4,5},{5,4},{6,7},{7,6},{8,9},{9,8},{10,11... | collective-permute-start | bytes 12296 | tf_op jit(solution)/shard_map/ppermute | solution.py:449
  79.9 7.1 %copy-start.3 = (bf16[1,2,128,512]{3,2,1,0:T(8,128)(2,1)S(1)}, bf16[1,2,128,512]{3,2,1,0:T(8,128)(2,1)}, u32[]{:S(2)}) copy-start(bf16[1,2,128,512]{3,2,1,0:T(8,128)(2,1)} %kp_ref.1) | copy-start | bytes 786436
  79.9 7.1 %copy-start.5 = (bf16[1,2,128,512]{3,2,1,0:T(8,128)(2,1)S(1)}, bf16[1,2,128,512]{3,2,1,0:T(8,128)(2,1)}, u32[]{:S(2)}) copy-start(bf16[1,2,128,512]{3,2,1,0:T(8,128)(2,1)} %vp_ref.1) | copy-start | bytes 786436
  79.9 7.1 %copy-start.12 = (f32[2,128,512]{2,1,0:T(8,128)S(1)}, f32[2,128,512]{2,1,0:T(8,128)}, u32[]{:S(2)}) copy-start(f32[2,128,512]{2,1,0:T(8,128)} %get-tuple-element.64.pair_ref) | copy-start | bytes 1572868
  84.5 2.4 %collective-permute-start.12 = (bf16[4,128,128]{2,1,0:T(8,128)(2,1)S(1)}, bf16[4,128,128]{2,1,0:T(8,128)(2,1)S(1)}, u32[]{:S(2)}, u32[]{:S(2)}) collective-permute-start(bf16[4,128,128]{2,1,0:T(8,128)(2,1)S(1)} %bitcast.4), channel_id=1, source_target_pairs={{0,4},{4,0},{1,5},{5,1},{2,6},{6,2},{3,7},{7,3},{8,12},{12,8},{9,1... | collective-permute-start | bytes 393224 | tf_op jit(solution)/shard_map/ppermute | solution.py:418

commit v3 on v2

--- a/solution.py
+++ b/solution.py
@@ -19,7 +19,7 @@
 BF16 = jnp.bfloat16
 SWAP = [(0, 1), (1, 0)]
 SCALAR_ROWS = 8
-UNROLL = 2
+UNROLL = 4
 VMEM_LIMIT = 20 * 1024 * 1024
 SMALL_VMEM = 8 * 1024 * 1024
 
@@ -290,60 +290,86 @@
 
 def backward_kernel(*refs):
     (qp_hbm, kp_hbm, vp_hbm, qp2_hbm, kp2_hbm, vp2_hbm, pulled_hbm, carried_hbm) = refs[:8]
-    qg_ref, kv_ref, qg2_ref, kvg2_ref = refs[8:12]
-    qp_ref, kp_ref, vp_ref, qp2_ref, kp2_ref, vp2_ref, pulled_ref, carried_ref, sems = refs[12:]
+    outs = refs[8:16]
+    qp_ref, kp_ref, vp_ref, qp2_ref, kp2_ref, vp2_ref, pulled_ref, carried_ref = refs[16:24]
+    qg_ref, pair_ref, qg2_ref, pair2_ref, in_sems, out_sems = refs[24:]
     core = lax.axis_index("core")
     causal = causal_rows()
-    moves = [
-        (qp_hbm.at[0, core], qp_ref),
-        (kp_hbm.at[0, core], kp_ref),
-        (vp_hbm.at[0, core], vp_ref),
-        (pulled_hbm, pulled_ref),
-        (qp2_hbm.at[0, core], qp2_ref),
-        (kp2_hbm.at[0, core], kp2_ref),
-        (vp2_hbm.at[0, core], vp2_ref),
-        (carried_hbm, carried_ref),
-    ]
-    for copy in staged(moves, sems):
-        copy.wait()
-    blocks = ((qp_ref, kp_ref, vp_ref, qg_ref, kv_ref), (qp2_ref, kp2_ref, vp2_ref, qg2_ref, kvg2_ref))
+
+    def load(start, count, sems):
+        heads = pl.ds(start * WIDE, count * WIDE)
+        shared = pl.ds(start * D, count * D)
+        groups = pl.ds(start, count)
+        moves = [
+            (pulled_hbm.at[:, groups], pulled_ref.at[:, groups]),
+            (vp_hbm.at[0, core, :, shared], vp_ref.at[:, shared]),
+            (vp2_hbm.at[0, core, :, shared], vp2_ref.at[:, shared]),
+            (kp_hbm.at[0, core, :, shared], kp_ref.at[:, shared]),
+            (kp2_hbm.at[0, core, :, shared], kp2_ref.at[:, shared]),
+            (carried_hbm.at[:, groups], carried_ref.at[:, groups]),
+            (qp_hbm.at[0, core, :, heads], qp_ref.at[:, heads]),
+            (qp2_hbm.at[0, core, :, heads], qp2_ref.at[:, heads]),
+        ]
+        return staged(moves, sems)
+
+    def stores(g):
+        heads, shared = slice(g * WIDE, (g + 1) * WIDE), slice(g * D, (g + 1) * D)
+        held = (
+            (qg_ref.at[:, heads], outs[0].at[:, heads]),
+            (pair_ref.at[:, :, shared], outs[1].at[:, :, shared]),
+            (qg2_ref.at[:, heads], outs[4 + g]),
+            (pair2_ref.at[0, :, shared], outs[2].at[:, shared]),
+            (pair2_ref.at[1, :, shared], outs[3].at[:, shared]),
+        )
+        return [pltpu.make_async_copy(a, b, out_sems.at[i, g]) for i, (a, b) in enumerate(held)]
+
+    blocks = ((qp_ref, kp_ref, vp_ref, qg_ref, pair_ref), (qp2_ref, kp2_ref, vp2_ref, qg2_ref, pair2_ref))
 
     def group(g):
+        heads, shared = slice(g * WIDE, (g + 1) * WIDE), slice(g * D, (g + 1) * D)
         for i, (q_ref, k_ref, v_ref, q_out, kv_out) in enumerate(blocks):
-            query, key, value = rows_of(q_ref[:, at(g, WIDE)]), k_ref[:, at(g, D)], v_ref[:, at(g, D)]
+            query, key, value = rows_of(q_ref[:, heads]), k_ref[:, shared], v_ref[:, shared]
             pulled = pulled_ref[i, g]
             dscore = jnp.where(causal, dot(pulled, value, 1, 1), 0.0).astype(BF16)
             query_grad = (dot(dscore, key, 1, 0) + dot(pulled, carried_ref[i, g], 1, 1)).astype(BF16)
-            q_out[:, at(g, WIDE)] = jnp.concatenate([query_grad[r * T : (r + 1) * T] for r in range(GROUP)], axis=1)
-            kv_out[0, :, at(g, D)] = dot(dscore, query, 0, 0)
+            q_out[:, heads] = jnp.concatenate([query_grad[r * T : (r + 1) * T] for r in range(GROUP)], axis=1)
+            kv_out[0, :, shared] = dot(dscore, query, 0, 0).astype(kv_out.dtype)
             scores = jnp.where(causal, dot(query, key, 1, 1), 0.0).astype(BF16)
-            kv_out[1, :, at(g, D)] = dot(scores, pulled, 0, 0)
-
-    each_group(group)
+            kv_out[1, :, shared] = dot(scores, pulled, 0, 0).astype(kv_out.dtype)
+        for copy in stores(g):
+            copy.start()
+
+    head = load(0, 1, in_sems.at[0])
+    tail = load(1, KV_HEADS - 1, in_sems.at[1])
+    for copy in head:
+        copy.wait()
+    group(0)
+    for copy in tail:
+        copy.wait()
+    for g in range(1, KV_HEADS):
+        group(g)
+    for g in range(KV_HEADS):
+        for copy in stores(g):
+            copy.wait()
 
 
 def backward_pass(*arrays):
-    query_shape = pltpu.HBM((T, HEADS * D), BF16)
-    pair_shape = pltpu.HBM((2, T, KV_HEADS * D), F32)
-    wide, narrow = pltpu.VMEM((T, HEADS * D), BF16), pltpu.VMEM((T, KV_HEADS * D), BF16)
+    wide, narrow = (T, HEADS * D), (T, KV_HEADS * D)
+    query, pair = pltpu.HBM(wide, BF16), pltpu.HBM((2,) + narrow, F32)
     return pl.pallas_call(
         backward_kernel,
         in_specs=[IN_HBM] * 8,
-        out_specs=out_vmem(4),
-        out_shape=(query_shape, pair_shape, query_shape, pair_shape),
-        scratch_shapes=[
-            wide,
-            narrow,
-            narrow,
-            wide,
-            narrow,
-            narrow,
+        out_specs=(IN_HBM,) * 8,
+        out_shape=(query, pair) + (pltpu.HBM(narrow, BF16),) * 2 + (pltpu.HBM((T, WIDE), BF16),) * GROUP,
+        scratch_shapes=[pltpu.VMEM(wide, BF16), pltpu.VMEM(narrow, BF16), pltpu.VMEM(narrow, BF16)] * 2
+        + [
             pltpu.VMEM((2, KV_HEADS, GROUP * T, D), BF16),
             pltpu.VMEM((2, KV_HEADS, D, D), BF16),
-            pltpu.SemaphoreType.DMA((8,)),
-        ],
+        ]
+        + [pltpu.VMEM(wide, BF16), pltpu.VMEM((2,) + narrow, F32), pltpu.VMEM(wide, BF16), pltpu.VMEM((2,) + narrow, BF16)]
+        + [pltpu.SemaphoreType.DMA((2, 8)), pltpu.SemaphoreType.DMA((5, KV_HEADS))],
         name="backward_pass",
-        cost_estimate=pl.CostEstimate(flops=160 * 2 * D * D * T, bytes_accessed=6 << 20, transcendentals=0),
+        cost_estimate=pl.CostEstimate(flops=192 * 2 * D * D * T, bytes_accessed=6 << 20, transcendentals=0),
         compiler_params=PARAMS,
     )(*far(*arrays))
 
@@ -352,66 +378,111 @@
     return jnp.where(seq == 0, -weight_ref[0:1, 0:1], weight_ref[0:1, 0:1])
 
 
-def scale_kernel(own_ref, other_ref, weight_ref, o_ref):
+def scale_kernel(own_hbm, *refs):
+    others, weight_ref, o_hbm = refs[:GROUP], refs[GROUP], refs[GROUP + 1]
+    own_ref, scaled_ref, in_sem, out_sems = refs[GROUP + 2 :]
     core = lax.axis_index("core")
-    for turn, ref in ((0, own_ref), (1, other_ref)):
-        seq = lax.rem(core + turn, 2)
-        o_ref[0, seq] = (ref[...].astype(F32) * weight_of(seq, weight_ref)).astype(BF16)
-
-
-def scaled_queries(*arrays):
-    return pl.pallas_call(
-        scale_kernel,
-        in_specs=in_vmem(3),
-        out_specs=out_vmem(1)[0],
-        out_shape=pltpu.HBM((1, 2, T, HEADS * D), BF16),
-        name="scaled_queries",
-        cost_estimate=pl.CostEstimate(flops=2 * T * HEADS * D, bytes_accessed=2 << 20, transcendentals=0),
-        compiler_params=PARAMS,
-    )(*far(*arrays[:2]), arrays[2])
-
-
-def final_kernel(
-    kp_ref,
-    vp_ref,
-    pair_ref,
-    pair2_ref,
-    weight_ref,
-    after_ref,
-    after2_ref,
-    second_ref,
-    second2_ref,
-    ko_ref,
-    vo_ref,
-):
-    core = lax.axis_index("core")
-    for turn, after, second, grads_ref in (
-        (0, after_ref, second_ref, pair_ref),
-        (1, after2_ref, second2_ref, pair2_ref),
-    ):
+    arriving = pltpu.make_async_copy(own_hbm, own_ref, in_sem)
+    arriving.start()
+    leaving = []
+    for turn in (1, 0):
+        if turn == 0:
+            arriving.wait()
         seq = lax.rem(core + turn, 2)
         weight = weight_of(seq, weight_ref)
-        for g in range(KV_HEADS):
-            span = slice(g * D, (g + 1) * D)
-            later = after[g].astype(F32)
-            later = jnp.where(core == 0, later + second[g], later).astype(BF16)
-            key_grad = grads_ref[0, :, span] + dot(vp_ref[0, seq, :, span], later, 1, 1)
-            value_grad = grads_ref[1, :, span] + dot(kp_ref[0, seq, :, span], later, 1, 0)
-            ko_ref[0, seq, :, span] = (weight * key_grad).astype(BF16)
-            vo_ref[0, seq, :, span] = (weight * value_grad).astype(BF16)
-
-
-def final_pass(kp, vp, pair, pair2, weight, after, after2, second, second2):
-    shape = pltpu.HBM((1, 2, T, KV_HEADS * D), BF16)
-    return pl.pallas_call(
-        final_kernel,
-        out_shape=(shape, shape),
-        in_specs=[pl.BlockSpec(memory_space=pltpu.VMEM)] * 9,
-        out_specs=(pl.BlockSpec(memory_space=pltpu.VMEM),) * 2,
-        name="final_pass",
-        cost_estimate=pl.CostEstimate(flops=16 * 2 * D * D * T, bytes_accessed=3 << 20, transcendentals=0),
-        compiler_params=pltpu.CompilerParams(vmem_limit_bytes=SMALL_VMEM),
-    )(*near(kp, vp, pair, pair2), weight, *near(after, after2, second, second2))
+        for g in range(GROUP):
+            heads = slice(g * WIDE, (g + 1) * WIDE)
+            piece = others[g][...] if turn else own_ref[:, heads]
+            scaled_ref[turn, :, heads] = (piece.astype(F32) * weight).astype(BF16)
+            copy = pltpu.make_async_copy(scaled_ref.at[turn, :, heads], o_hbm.at[0, seq, :, heads], out_sems.at[turn, g])
+            copy.start()
+            leaving.append(copy)
+    for copy in leaving:
+        copy.wait()
+
+
+def scaled_queries(own, others, weight):
+    in_vmem = pl.BlockSpec(memory_space=pltpu.VMEM)
+    return pl.pallas_call(
+        scale_kernel,
+        in_specs=[IN_HBM] + [in_vmem] * (GROUP + 1),
+        out_specs=IN_HBM,
+        out_shape=pltpu.HBM((1, 2, T, HEADS * D), BF16),
+        scratch_shapes=[
+            pltpu.VMEM((T, HEADS * D), BF16),
+            pltpu.VMEM((2, T, HEADS * D), BF16),
+            pltpu.SemaphoreType.DMA(()),
+            pltpu.SemaphoreType.DMA((2, GROUP)),
+        ],
+        name="scaled_queries",
+        cost_estimate=pl.CostEstimate(flops=2 * T * HEADS * D, bytes_accessed=T, transcendentals=0),
+        compiler_params=PARAMS,
+    )(*far(own), *near(*others), weight)
+
+
+def shared_gradients(turn, k_ref, v_ref, grads, weight_ref, after_ref, second_ref, out_refs, hbm_refs, sems):
+    core = lax.axis_index("core")
+    seq = lax.rem(core + turn, 2)
+    weight = weight_of(seq, weight_ref)
+    for g in range(KV_HEADS):
+        span = slice(g * D, (g + 1) * D)
+        later = after_ref[g].astype(F32)
+        later = jnp.where(core == 0, later + second_ref[g].astype(F32), later).astype(BF16)
+        key_grad = grads[0][:, span].astype(F32) + dot(v_ref[0, seq, :, span], later, 1, 1)
+        value_grad = grads[1][:, span].astype(F32) + dot(k_ref[0, seq, :, span], later, 1, 0)
+        out_refs[0][:, span] = (weight * key_grad).astype(BF16)
+        out_refs[1][:, span] = (weight * value_grad).astype(BF16)
+    for copy in staged([(a, b.at[0, seq]) for a, b in zip(out_refs, hbm_refs)], sems):
+        copy.wait()
+
+
+def own_kernel(k_ref, v_ref, pair_ref, weight_ref, after_ref, second_ref, ko_hbm, vo_hbm, ko_ref, vo_ref, sems):
+    grads = (pair_ref.at[0], pair_ref.at[1])
+    shared_gradients(
+        0, k_ref, v_ref, grads, weight_ref, after_ref, second_ref, (ko_ref, vo_ref), (ko_hbm, vo_hbm), sems
+    )
+
+
+def other_kernel(*refs):
+    k_ref, v_ref, kg_ref, vg_ref, weight_ref, after_ref, second_ref, loss_ref, one_ref, two_ref, three_ref = refs[:11]
+    ko_hbm, vo_hbm, pair_loss_ref, ko_ref, vo_ref, sems = refs[13:]
+    pairs = lax.axis_size("dp")
+    loss = ((loss_ref[...] + one_ref[...]) + (two_ref[...] + three_ref[...])) / pairs
+    pair_loss_ref[0, 0] = jnp.max(loss)
+    shared_gradients(
+        1, k_ref, v_ref, (kg_ref, vg_ref), weight_ref, after_ref, second_ref, (ko_ref, vo_ref), (ko_hbm, vo_hbm), sems
+    )
+
+
+ROWS = (1, 2, T, KV_HEADS * D)
+FINAL = dict(
+    scratch_shapes=[pltpu.VMEM(ROWS[2:], BF16)] * 2 + [pltpu.SemaphoreType.DMA((2,))],
+    cost_estimate=pl.CostEstimate(flops=8 * 2 * D * D * T, bytes_accessed=1 << 20, transcendentals=0),
+    compiler_params=pltpu.CompilerParams(vmem_limit_bytes=SMALL_VMEM),
+)
+
+
+def own_gradients(*arrays):
+    return pl.pallas_call(
+        own_kernel,
+        in_specs=list(out_vmem(6)),
+        out_specs=(IN_HBM,) * 2,
+        out_shape=(pltpu.HBM(ROWS, BF16),) * 2,
+        name="own_gradients",
+        **FINAL,
+    )(*near(*arrays))
+
+
+def other_gradients(*arrays):
+    return pl.pallas_call(
+        other_kernel,
+        in_specs=list(out_vmem(11)) + [IN_HBM] * 2,
+        out_specs=(IN_HBM, IN_HBM, pl.BlockSpec(memory_space=pltpu.SMEM)),
+        out_shape=(pltpu.HBM(ROWS, BF16),) * 2 + (jax.ShapeDtypeStruct((1, 1), F32),),
+        input_output_aliases={11: 0, 12: 1},
+        name="other_gradients",
+        **FINAL,
+    )(*near(*arrays[:11]), *far(*arrays[11:]))
 
 
 def swap(x):
@@ -435,25 +506,29 @@
     other = (qp2, qr2, read2, kp2, vp2, kr2, vr2, mask2)
     pulled, payload, second, carried = forward_pass(*own, *other, before)
     arrived = exchange(payload)
-    second2 = swap(second)
-    grads = backward_pass(qp, kp, vp, qp2, kp2, vp2, pulled, carried)
-    arrived, grads = lax.optimization_barrier((arrived, grads))
-    qg, pair, qg2, pair2 = grads
-    qg2, pair2 = swap(qg2), swap(pair2)
+    qg, pair, kg2, vg2, *qg2 = backward_pass(qp, kp, vp, qp2, kp2, vp2, pulled, carried)
+    arrived, qg, pair, qg2, kg2, vg2 = lax.optimization_barrier((arrived, qg, pair, qg2, kg2, vg2))
     after, mine = exclusive_suffix(arrived)
+    after, mine, qg2, kg2, vg2, second2 = lax.optimization_barrier(
+        (after, mine, qg2, kg2, vg2, second.astype(BF16))
+    )
+    kg2, vg2, second2 = swap(kg2), swap(vg2), swap(second2)
+    qg2 = tuple(swap(x) for x in qg2)
     after = exchange(after).reshape(KV_HEADS, D, D)
 
     delta = mine + swap(mine)
     loss = jax.nn.softplus(-DPO_BETA * delta)
     pairs = lax.axis_size("dp")
     one, two, three = (lax.ppermute(loss, "dp", [(i, i ^ k) for i in range(pairs)]) for k in (1, 2, 3))
-    pair_loss = ((loss + one) + (two + three)) / pairs
     scale = math.sqrt(HEADS * D * T * lax.axis_size("chip") * 2)
     weight = DPO_BETA * jax.nn.sigmoid(-DPO_BETA * delta) * scale
     query_rows = scaled_queries(qg, qg2, weight)
-    after, query_rows, pair2, second2 = lax.optimization_barrier((after, query_rows, pair2, second2))
-    key_rows, value_rows = final_pass(kp, vp, pair, pair2, weight, after, swap(after), second, second2)
-    return query_rows, key_rows, value_rows, pair_loss[0, 0]
+    after, query_rows, one, two, three = lax.optimization_barrier((after, query_rows, one, two, three))
+    held = own_gradients(kp, vp, pair, weight, after, second)
+    key_rows, value_rows, pair_loss = other_gradients(
+        kp, vp, kg2, vg2, weight, swap(after), second2, loss, one, two, three, *held
+    )
+    return query_rows, key_rows, value_rows, pair_loss.reshape(())
 
 
 def solution(mesh):

time: 88.5 us -> 87.3 us (0.986)
  waiting for transfers between devices: 7.09 us -> 4.27 us
  starting transfers between devices: 24.3 us -> 26.7 us
  local copies, waits for them, and re-layouts: 1.05 us -> 0.08 us
    all_to_all x2, waiting for transfers between devices: 5.72 us -> 4.14 us  [exchange(): return lax.all_to_all(x, 'chip', 0, 0, tiled=True)]
    ppermute x13 -> x17, starting transfers between devices: 11.1 us -> 12.4 us  [swap(): return lax.ppermute(x, 'core', SWAP)]
    ppermute x13 -> x17, waiting for transfers between devices: 1.37 us -> 0.12 us  [swap(): return lax.ppermute(x, 'core', SWAP)]
    pallas_call x3 -> x4, Pallas kernels: 9.94 us -> 10.3 us  [the longest x1 5.51 us: backward_pass(): pl.pallas_call(backward_kernel, in_specs=[IN_HBM] * 8, out_specs=(IN_HBM,...]
  transfers between devices with their start and end apart: 18 -> 22, of which waited for: 5 -> 2; matrix products, arithmetic and copies ran while one was open for 1% -> 0% of each run, Pallas kernels for 13% -> 12%
where the time goes in v3:
time: 87.3 us; the launch traced here: 86.9 us
  blocking collectives  36 us (41%)
  starting transfers between devices  26.7 us (31%)
  Pallas kernels  18.8 us (22%)
  waiting for transfers between devices  4.27 us (5%)
  between operations  1.09 us (1%)
    all_to_all x2, blocking collectives, exchange(): return lax.all_to_all(x, 'chip', 0, 0, tiled=True)  36 us
    ppermute x17, starting transfers between devices, swap(): return lax.ppermute(x, 'core', SWAP)  12.4 us
    all_to_all x2, starting transfers between devices, exchange(): return lax.all_to_all(x, 'chip', 0, 0, tiled=True)  10.5 us
    pallas_call x1, Pallas kernels, forward_pass(): pl.pallas_call(forward_kernel, in_specs=[in_vmem] * 17, out_specs=(IN_HBM...  6.18 us
    pallas_call x1, Pallas kernels, backward_pass(): pl.pallas_call(backward_kernel, in_specs=[IN_HBM] * 8, out_specs=(IN_HBM,...  5.51 us
    all_to_all x2, waiting for transfers between devices, exchange(): return lax.all_to_all(x, 'chip', 0, 0, tiled=True)  4.14 us
    ppermute x3, starting transfers between devices, shards(): lax.ppermute(loss, 'dp', [(i, i ^ k) for i in range(pairs)])  3.83 us
    pallas_call x1, Pallas kernels, scaled_queries(): pl.pallas_call(scale_kernel, in_specs=[IN_HBM] + [in_vmem] * (GROUP + 1),...  2.26 us
  transfers between devices with their start and end apart: 22, of which 2 were waited for; matrix products, arithmetic and copies ran while one was open for 0% of the time, Pallas kernels for 12%

profile of v3, /device:TPU:1, one launch (start us, length us, event | category | flops | bytes accessed | tf_op | source)
XLA Modules:
  0.0 86.9 jit_solution(3938524280317872112)
XLA Ops:
  0.6 0.0 copy-start.4
  0.6 3.3 %collective-permute-start.2 = (bf16[1,2,128,512]{3,2,1,0:T(8,128)(2,1)}, bf16[1,2,128,512]{3,2,1,0:T(8,128)(2,1)S(1)}, u32[]{:S(2)}, u32[]{:S(2)}) collective-permute-start(bf16[1,2,128,512]{3,2,1,0:T(8,128)(2,1)} %refs_5_.1), channel_id=1, source_target_pairs={{0,4},{4,0},{1,5},{5,1},{2,6},{6,2},{3,7},{7,3},{8,12},{12,8},{9,1... | collective-permute-start | bytes 786440 | tf_op jit(solution)/shard_map/ppermute | solution.py:489
  4.0 0.1 collective-permute-start.3
  4.1 0.4 collective-permute-start
  4.5 0.1 collective-permute-start.1
  4.6 0.4 collective-permute-start.4
  5.0 1.4 %own_states.1 = (f32[2,4,128,128]{3,2,1,0:T(8,128)S(1)}, s32[1,2,128]{2,1,0:T(2,128)S(1)}) custom-call(bf16[1,2,128,512]{3,2,1,0:T(8,128)(2,1)} %refs_0_.5, bf16[1,2,128,512]{3,2,1,0:T(8,128)(2,1)} %refs_1_.6, bf16[1,2,128,512]{3,2,1,0:T(8,128)(2,1)} %refs_5_.1, bf16[1,2,128,512]{3,2,1,0:T(8,128)(2,1)} %refs_6_.1, s32[1,2,128]{2,1,0:T(2,128)} %refs_4_.2), custom_call_target="tpu_custom_call" | custom-call | flops 33554432 | bytes 1048576 | tf_op jit(solution)/shard_map/own_states/pallas_call | solution.py:67
  6.4 0.1 collective-permute-done.4.refs_15_
  6.5 0.0 collective-permute-done.2.kr2_ref.refs_13_
  6.5 0.0 collective-permute-done.3.vr2_ref.refs_14_
  6.5 0.0 copy-start.6
  6.5 0.0 copy-start.7
  6.5 0.5 collective-permute-start.6
  7.0 0.1 collective-permute-start.7
  7.1 0.4 collective-permute-start.5
  7.5 0.3 chip_states.1
  7.8 0.0 copy-start.8
  7.8 21.1 %all_to_all.20.x_ref = bf16[32,32,128]{2,1,0:T(8,128)(2,1)S(1)} all-to-all(bf16[32,32,128]{2,1,0:T(8,128)(2,1)S(1)} %chip_states.1), channel_id=1, replica_groups=mesh['chip'=32,'core'=2,'dp'=4] {'chip'}, dimensions={0} | all-to-all | bytes 524288 | tf_op jit(solution)/shard_map/all_to_all | solution.py:493
  28.9 0.0 copy-start
  28.9 0.0 copy-start.2
  28.9 14.9 %all_to_all.21 = bf16[32,32,128]{2,1,0:T(8,128)(2,1)S(1)} all-to-all(bf16[32,32,128]{2,1,0:T(8,128)(2,1)S(1)} %exclusive_prefix.1), channel_id=1, replica_groups=mesh['chip'=32,'core'=2,'dp'=4] {'chip'}, dimensions={0} | all-to-all | bytes 524288 | tf_op jit(solution)/shard_map/all_to_all | solution.py:493
  43.8 0.0 copy-start.5
  43.9 6.2 %forward_pass.1 = (bf16[2,4,512,128]{3,2,1,0:T(8,128)(2,1)}, bf16[32,24,128]{2,1,0:T(8,128)(2,1)}, f32[4,128,128]{2,1,0:T(8,128)}, bf16[2,4,128,128]{3,2,1,0:T(8,128)(2,1)}) custom-call(bf16[1,2,128,2048]{3,2,1,0:T(8,128)(2,1)S(1)} %copy-done.4, bf16[1,2,128,2048]{3,2,1,0:T(8,128)(2,1)S(1)} %copy-done.8, bf16[1,2,128,2048]{3,2,1,0:T(8,128)(2,1)S(1)} %copy-done.9, ...), custom_call_target="tpu_custom_call" | custom-call | flops 805306368 | bytes 8388608 | tf_op jit(solution)/shard_map/forward_pass/pallas_call | solution.py:268
  50.1 5.4 %all-to-all-start.2 = ((bf16[32,24,128]{2,1,0:T(8,128)(2,1)}), bf16[32,24,128]{2,1,0:T(8,128)(2,1)S(1)}, u32[]{:S(2)}, u32[]{:S(2)}) async-start(bf16[32,24,128]{2,1,0:T(8,128)(2,1)} %get-tuple-element.70), calls=%async_computation.2 | async-start | bytes 393216 | tf_op jit(solution)/shard_map/all_to_all | solution.py:493
  55.6 5.5 %backward_pass.1 = (bf16[128,2048]{1,0:T(8,128)(2,1)}, f32[2,128,512]{2,1,0:T(8,128)}, bf16[128,512]{1,0:T(8,128)(2,1)}, bf16[128,512]{1,0:T(8,128)(2,1)}, bf16[...) custom-call(bf16[1,2,128,2048]{3,2,1,0:T(8,128)(2,1)} %refs_0_.4, ...), custom_call_target="tpu_custom_call" | custom-call | flops 805306368 | bytes 6291456 | tf_op jit(solution)/shard_map/backward_pass/pallas_call | solution.py:359
  61.1 4.1 %all-to-all-done.2.x_ref = bf16[32,24,128]{2,1,0:T(8,128)(2,1)S(1)} async-done(((bf16[32,24,128]{2,1,0:T(8,128)(2,1)}), bf16[32,24,128]{2,1,0:T(8,128)(2,1)S(1)}, u32[]{:S(2)}, u32[]{:S(2)}) %all-to-all-start.2) | async-done | bytes 196640 | tf_op jit(solution)/shard_map/all_to_all | solution.py:493
  65.2 0.7 exclusive_suffix.1
  65.9 5.1 %all-to-all-start.3 = ((bf16[32,16,128]{2,1,0:T(8,128)(2,1)}), bf16[32,16,128]{2,1,0:T(8,128)(2,1)S(1)}, u32[]{:S(2)}, u32[]{:S(2)}) async-start(bf16[32,16,128]{2,1,0:T(8,128)(2,1)} %get-tuple-element.91), calls=%async_computation.3 | async-start | bytes 262144 | tf_op jit(solution)/shard_map/all_to_all | solution.py:493
  71.0 2.7 %collective-permute-start.12 = (f32[8,128]{1,0:T(8,128)S(1)}, f32[8,128]{1,0:T(8,128)S(1)}, u32[]{:S(2)}, u32[]{:S(2)}) collective-permute-start(f32[8,128]{1,0:T(8,128)S(1)} %get-tuple-element.97), channel_id=1, source_target_pairs={{0,4},{4,0},{1,5},{5,1},{2,6},{6,2},{3,7},{7,3},{8,12},{12,8},{9,1... | collective-permute-start | bytes 12296 | tf_op jit(solution)/shard_map/ppermute | solution.py:489
  73.7 0.1 collective-permute-start.8
  73.8 0.4 collective-permute-start.9
  74.2 0.1 collective-permute-start.10
  74.3 0.4 collective-permute-start.11
  74.7 0.0 collective-permute-done.12
  74.7 2.8 %collective-permute-start.15 = (f32[8,128]{1,0:T(8,128)S(1)}, f32[8,128]{1,0:T(8,128)S(1)}, u32[]{:S(2)}, u32[]{:S(2)}) collective-permute-start(f32[8,128]{1,0:T(8,128)S(1)} %get-tuple-element.112.refs_7_), channel_id=1, source_target_pairs={{0,3},{1,2},{2,1},{3,0},{4,7},{5,6},{6,5},{7,4},{8,11},{9,10},{10,... | collective-permute-start | bytes 12296 | tf_op jit(solution)/shard_map/ppermute | solution.py:522
  77.6 0.0 collective-permute-done.8.refs_0_
  77.6 0.6 collective-permute-start.14
  78.2 0.4 collective-permute-start.13
  78.6 0.7 collective-permute-start.16
  79.3 0.1 collective-permute-start.17
  79.4 2.3 %scaled_queries.1 = bf16[1,2,128,2048]{3,2,1,0:T(8,128)(2,1)} custom-call(bf16[128,2048]{1,0:T(8,128)(2,1)} %get-tuple-element.92.own_hbm, bf16[128,512]{1,0:T(8,128)(2,1)S(1)} %collective-permute-done.8.refs_0_, bf16[128,512]{1,0:T(8,128)(2,1)S(1)} %collective-permute-done.9.refs_1_, bf16[128,512]{1,0:T(8,128)(2,1)S(1)} %collective-permute-done.10.refs_2_, ...), custom_call_target="tpu_custom_call" | custom-call | flops 524288 | bytes 128 | tf_op jit(solution)/shard_map/scaled_queries/pallas_call | solution.py:406
  81.7 0.5 collective-permute-start.19
  82.2 0.0 all-to-all-done.3
  82.2 2.0 %collective-permute-start.18 = (bf16[4,128,128]{2,1,0:T(8,128)(2,1)S(1)}, bf16[4,128,128]{2,1,0:T(8,128)(2,1)S(1)}, u32[]{:S(2)}, u32[]{:S(2)}) collective-permute-start(bf16[4,128,128]{2,1,0:T(8,128)(2,1)S(1)} %bitcast.4), channel_id=1, source_target_pairs={{0,4},{4,0},{1,5},{5,1},{2,6},{6,2},{3,7},{7,3},{8,12},{12,8},{9,1... | collective-permute-start | bytes 393224 | tf_op jit(solution)/shard_map/ppermute | solution.py:489
  84.2 1.0 %own_gradients.1 = (bf16[1,2,128,512]{3,2,1,0:T(8,128)(2,1)}, bf16[1,2,128,512]{3,2,1,0:T(8,128)(2,1)}) custom-call(bf16[1,2,128,512]{3,2,1,0:T(8,128)(2,1)S(1)} %copy-done.1, bf16[1,2,128,512]{3,2,1,0:T(8,128)(2,1)S(1)} %copy-done.3, f32[2,128,512]{2,1,0:T(8,128)S(1)} %copy-done.13, f32[8,128]{1,0:T(8,128)S(1)} %get-tuple-element.113.refs_4_.weight_ref, ...), custom_call_target="tpu_custom_call" | custom-call | flops 33554432 | bytes 1048576 | tf_op jit(solution)/shard_map/own_gradients/pallas_call | solution.py:466
  85.2 0.0 collective-permute-done.17.refs_3_
  85.2 0.0 collective-permute-done.19.refs_6_
  85.3 1.5 %other_gradients.1 = (bf16[1,2,128,512]{3,2,1,0:T(8,128)(2,1)}, bf16[1,2,128,512]{3,2,1,0:T(8,128)(2,1)}, f32[1,1]{1,0:T(1,128)}) custom-call(bf16[1,2,128,512]{3,2,1,0:T(8,128)(2,1)S(1)} %copy-done.1, bf16[1,2,128,512]{3,2,1,0:T(8,128)(2,1)S(1)} %copy-done.3, ...), custom_call_target="tpu_custom_call", output_to_operand_aliasing={{0}: (11, {}), {1}: (12, {})} | custom-call | flops 33554432 | bytes 1048576 | tf_op jit(solution)/shard_map/other_gradients/pallas_call | solution.py:477
  (43 shorter events, 0.2 us)
Async XLA Ops:
  0.6 6.5 %copy-start.4 = (bf16[1,2,128,2048]{3,2,1,0:T(8,128)(2,1)S(1)}, bf16[1,2,128,2048]{3,2,1,0:T(8,128)(2,1)}, u32[]{:S(2)}) copy-start(bf16[1,2,128,2048]{3,2,1,0:T(8,128)(2,1)} %refs_0_.4) | copy-start | bytes 3145732
  0.6 5.8 %collective-permute-start.2 = (bf16[1,2,128,512]{3,2,1,0:T(8,128)(2,1)}, bf16[1,2,128,512]{3,2,1,0:T(8,128)(2,1)S(1)}, u32[]{:S(2)}, u32[]{:S(2)}) collective-permute-start(bf16[1,2,128,512]{3,2,1,0:T(8,128)(2,1)} %refs_5_.1), channel_id=1, source_target_pairs={{0,4},{4,0},{1,5},{5,1},{2,6},{6,2},{3,7},{7,3},{8,12},{12,8},{9,1... | collective-permute-start | bytes 786440 | tf_op jit(solution)/shard_map/ppermute | solution.py:489
  4.0 2.5 %collective-permute-start.3 = (bf16[1,2,128,512]{3,2,1,0:T(8,128)(2,1)}, bf16[1,2,128,512]{3,2,1,0:T(8,128)(2,1)S(1)}, u32[]{:S(2)}, u32[]{:S(2)}) collective-permute-start(bf16[1,2,128,512]{3,2,1,0:T(8,128)(2,1)} %refs_6_.1), channel_id=1, source_target_pairs={{0,4},{4,0},{1,5},{5,1},{2,6},{6,2},{3,7},{7,3},{8,12},{12,8},{9,1... | collective-permute-start | bytes 786440 | tf_op jit(solution)/shard_map/ppermute | solution.py:489
  4.1 2.4 %collective-permute-start = (bf16[1,2,128,512]{3,2,1,0:T(8,128)(2,1)}, bf16[1,2,128,512]{3,2,1,0:T(8,128)(2,1)S(1)}, u32[]{:S(2)}, u32[]{:S(2)}) collective-permute-start(bf16[1,2,128,512]{3,2,1,0:T(8,128)(2,1)} %refs_0_.5), channel_id=1, source_target_pairs={{0,4},{4,0},{1,5},{5,1},{2,6},{6,2},{3,7},{7,3},{8,12},{12,8},{9,1... | collective-permute-start | bytes 786440 | tf_op jit(solution)/shard_map/ppermute | solution.py:489
  4.5 2.0 %collective-permute-start.1 = (bf16[1,2,128,512]{3,2,1,0:T(8,128)(2,1)}, bf16[1,2,128,512]{3,2,1,0:T(8,128)(2,1)S(1)}, u32[]{:S(2)}, u32[]{:S(2)}) collective-permute-start(bf16[1,2,128,512]{3,2,1,0:T(8,128)(2,1)} %refs_1_.6), channel_id=1, source_target_pairs={{0,4},{4,0},{1,5},{5,1},{2,6},{6,2},{3,7},{7,3},{8,12},{12,8},{9,1... | collective-permute-start | bytes 786440 | tf_op jit(solution)/shard_map/ppermute | solution.py:489
  4.6 1.9 %collective-permute-start.4 = (s32[1,2,128]{2,1,0:T(2,128)}, s32[1,2,128]{2,1,0:T(2,128)S(1)}, u32[]{:S(2)}, u32[]{:S(2)}) collective-permute-start(s32[1,2,128]{2,1,0:T(2,128)} %refs_4_.2), channel_id=1, source_target_pairs={{0,4},{4,0},{1,5},{5,1},{2,6},{6,2},{3,7},{7,3},{8,12},{12,8},{9,1... | collective-permute-start | bytes 3080 | tf_op jit(solution)/shard_map/ppermute | solution.py:489
  6.5 37.3 %copy-start.6 = (bf16[1,2,128,512]{3,2,1,0:T(8,128)(2,1)}, bf16[1,2,128,512]{3,2,1,0:T(8,128)(2,1)S(1)}, u32[]{:S(2)}) copy-start(bf16[1,2,128,512]{3,2,1,0:T(8,128)(2,1)S(1)} %collective-permute-done.kp2_ref.refs_11_.refs_4_) | copy-start | bytes 786436
  6.5 37.3 %copy-start.7 = (bf16[1,2,128,512]{3,2,1,0:T(8,128)(2,1)}, bf16[1,2,128,512]{3,2,1,0:T(8,128)(2,1)S(1)}, u32[]{:S(2)}) copy-start(bf16[1,2,128,512]{3,2,1,0:T(8,128)(2,1)S(1)} %collective-permute-done.1.vp2_ref.refs_12_.refs_5_) | copy-start | bytes 786436
  6.5 37.3 %collective-permute-start.6 = (bf16[1,2,128,2048]{3,2,1,0:T(8,128)(2,1)}, bf16[1,2,128,2048]{3,2,1,0:T(8,128)(2,1)S(1)}, u32[]{:S(2)}, u32[]{:S(2)}) collective-permute-start(bf16[1,2,128,2048]{3,2,1,0:T(8,128)(2,1)} %refs_1_.4), channel_id=1, source_target_pairs={{0,4},{4,0},{1,5},{5,1},{2,6},{6,2},{3,7},{7,3},{8,12},{12,8},{9,1... | collective-permute-start | bytes 3145736 | tf_op jit(solution)/shard_map/ppermute | solution.py:489
  7.0 36.8 %collective-permute-start.7 = (bf16[1,2,128,2048]{3,2,1,0:T(8,128)(2,1)}, bf16[1,2,128,2048]{3,2,1,0:T(8,128)(2,1)S(1)}, u32[]{:S(2)}, u32[]{:S(2)}) collective-permute-start(bf16[1,2,128,2048]{3,2,1,0:T(8,128)(2,1)} %refs_2_.3), channel_id=1, source_target_pairs={{0,4},{4,0},{1,5},{5,1},{2,6},{6,2},{3,7},{7,3},{8,12},{12,8},{9,1... | collective-permute-start | bytes 3145736 | tf_op jit(solution)/shard_map/ppermute | solution.py:489
  7.1 36.7 %collective-permute-start.5 = (bf16[1,2,128,2048]{3,2,1,0:T(8,128)(2,1)S(1)}, bf16[1,2,128,2048]{3,2,1,0:T(8,128)(2,1)S(1)}, u32[]{:S(2)}, u32[]{:S(2)}) collective-permute-start(bf16[1,2,128,2048]{3,2,1,0:T(8,128)(2,1)S(1)} %copy-done.4), channel_id=1, source_target_pairs={{0,4},{4,0},{1,5},{5,1},{2,6},{6,2},{3,7},{7,3},{8,12},{12,8},{9,1... | collective-permute-start | bytes 3145736 | tf_op jit(solution)/shard_map/ppermute | solution.py:489
  7.5 36.4 %copy-start.9 = (bf16[1,2,128,2048]{3,2,1,0:T(8,128)(2,1)S(1)}, bf16[1,2,128,2048]{3,2,1,0:T(8,128)(2,1)}, u32[]{:S(2)}) copy-start(bf16[1,2,128,2048]{3,2,1,0:T(8,128)(2,1)} %refs_2_.3) | copy-start | bytes 3145732
  7.5 36.4 %copy-start.10 = (bf16[1,2,128,512]{3,2,1,0:T(8,128)(2,1)S(1)}, bf16[1,2,128,512]{3,2,1,0:T(8,128)(2,1)}, u32[]{:S(2)}) copy-start(bf16[1,2,128,512]{3,2,1,0:T(8,128)(2,1)} %refs_5_.1) | copy-start | bytes 786436
  7.5 36.4 %copy-start.11 = (bf16[1,2,128,512]{3,2,1,0:T(8,128)(2,1)S(1)}, bf16[1,2,128,512]{3,2,1,0:T(8,128)(2,1)}, u32[]{:S(2)}) copy-start(bf16[1,2,128,512]{3,2,1,0:T(8,128)(2,1)} %refs_6_.1) | copy-start | bytes 786436
  7.8 36.1 %copy-start.8 = (bf16[1,2,128,2048]{3,2,1,0:T(8,128)(2,1)S(1)}, bf16[1,2,128,2048]{3,2,1,0:T(8,128)(2,1)}, u32[]{:S(2)}) copy-start(bf16[1,2,128,2048]{3,2,1,0:T(8,128)(2,1)} %refs_1_.4) | copy-start | bytes 3145732
  28.9 15.0 %copy-start = (bf16[1,2,128,512]{3,2,1,0:T(8,128)(2,1)S(1)}, bf16[1,2,128,512]{3,2,1,0:T(8,128)(2,1)}, u32[]{:S(2)}) copy-start(bf16[1,2,128,512]{3,2,1,0:T(8,128)(2,1)} %refs_0_.5) | copy-start | bytes 786436
  28.9 15.0 %copy-start.2 = (bf16[1,2,128,512]{3,2,1,0:T(8,128)(2,1)S(1)}, bf16[1,2,128,512]{3,2,1,0:T(8,128)(2,1)}, u32[]{:S(2)}) copy-start(bf16[1,2,128,512]{3,2,1,0:T(8,128)(2,1)} %refs_1_.6) | copy-start | bytes 786436
  43.8 6.3 %copy-start.5 = (bf16[1,2,128,2048]{3,2,1,0:T(8,128)(2,1)}, bf16[1,2,128,2048]{3,2,1,0:T(8,128)(2,1)S(1)}, u32[]{:S(2)}) copy-start(bf16[1,2,128,2048]{3,2,1,0:T(8,128)(2,1)S(1)} %collective-permute-done.5.refs_8_.refs_3_) | copy-start | bytes 3145732
  50.1 5.4 %copy-start.12 = (f32[4,128,128]{2,1,0:T(8,128)S(1)}, f32[4,128,128]{2,1,0:T(8,128)}, u32[]{:S(2)}) copy-start(f32[4,128,128]{2,1,0:T(8,128)} %get-tuple-element.90.second_ref) | copy-start | bytes 786436
  50.1 15.1 %all-to-all-start.2 = ((bf16[32,24,128]{2,1,0:T(8,128)(2,1)}), bf16[32,24,128]{2,1,0:T(8,128)(2,1)S(1)}, u32[]{:S(2)}, u32[]{:S(2)}) async-start(bf16[32,24,128]{2,1,0:T(8,128)(2,1)} %get-tuple-element.70), calls=%async_computation.2 | async-start | bytes 393216 | tf_op jit(solution)/shard_map/all_to_all | solution.py:493
  65.2 9.1 %copy-start.16 = (bf16[128,512]{1,0:T(8,128)(2,1)S(1)}, bf16[128,512]{1,0:T(8,128)(2,1)}, u32[]{:S(2)}) copy-start(bf16[128,512]{1,0:T(8,128)(2,1)} %get-tuple-element.96) | copy-start | bytes 393220
  65.9 12.7 %copy-start.15 = (bf16[128,512]{1,0:T(8,128)(2,1)S(1)}, bf16[128,512]{1,0:T(8,128)(2,1)}, u32[]{:S(2)}) copy-start(bf16[128,512]{1,0:T(8,128)(2,1)} %get-tuple-element.99) | copy-start | bytes 393220
  65.9 13.4 %copy-start.14 = (bf16[128,512]{1,0:T(8,128)(2,1)S(1)}, bf16[128,512]{1,0:T(8,128)(2,1)}, u32[]{:S(2)}) copy-start(bf16[128,512]{1,0:T(8,128)(2,1)} %get-tuple-element.100) | copy-start | bytes 393220
  65.9 16.3 %all-to-all-start.3 = ((bf16[32,16,128]{2,1,0:T(8,128)(2,1)}), bf16[32,16,128]{2,1,0:T(8,128)(2,1)S(1)}, u32[]{:S(2)}, u32[]{:S(2)}) async-start(bf16[32,16,128]{2,1,0:T(8,128)(2,1)} %get-tuple-element.91), calls=%async_computation.3 | async-start | bytes 262144 | tf_op jit(solution)/shard_map/all_to_all | solution.py:493
  71.0 3.7 %collective-permute-start.12 = (f32[8,128]{1,0:T(8,128)S(1)}, f32[8,128]{1,0:T(8,128)S(1)}, u32[]{:S(2)}, u32[]{:S(2)}) collective-permute-start(f32[8,128]{1,0:T(8,128)S(1)} %get-tuple-element.97), channel_id=1, source_target_pairs={{0,4},{4,0},{1,5},{5,1},{2,6},{6,2},{3,7},{7,3},{8,12},{12,8},{9,1... | collective-permute-start | bytes 12296 | tf_op jit(solution)/shard_map/ppermute | solution.py:489
  73.7 3.9 %collective-permute-start.8 = (bf16[128,512]{1,0:T(8,128)(2,1)}, bf16[128,512]{1,0:T(8,128)(2,1)S(1)}, u32[]{:S(2)}, u32[]{:S(2)}) collective-permute-start(bf16[128,512]{1,0:T(8,128)(2,1)} %get-tuple-element.93), channel_id=1, source_target_pairs={{0,4},{4,0},{1,5},{5,1},{2,6},{6,2},{3,7},{7,3},{8,12},{12,8},{9,1... | collective-permute-start | bytes 393224 | tf_op jit(solution)/shard_map/ppermute | solution.py:489
  73.8 4.4 %collective-permute-start.9 = (bf16[128,512]{1,0:T(8,128)(2,1)}, bf16[128,512]{1,0:T(8,128)(2,1)S(1)}, u32[]{:S(2)}, u32[]{:S(2)}) collective-permute-start(bf16[128,512]{1,0:T(8,128)(2,1)} %get-tuple-element.94), channel_id=1, source_target_pairs={{0,4},{4,0},{1,5},{5,1},{2,6},{6,2},{3,7},{7,3},{8,12},{12,8},{9,1... | collective-permute-start | bytes 393224 | tf_op jit(solution)/shard_map/ppermute | solution.py:489
  74.2 4.4 %collective-permute-start.10 = (bf16[128,512]{1,0:T(8,128)(2,1)}, bf16[128,512]{1,0:T(8,128)(2,1)S(1)}, u32[]{:S(2)}, u32[]{:S(2)}) collective-permute-start(bf16[128,512]{1,0:T(8,128)(2,1)} %get-tuple-element.95), channel_id=1, source_target_pairs={{0,4},{4,0},{1,5},{5,1},{2,6},{6,2},{3,7},{7,3},{8,12},{12,8},{9,1... | collective-permute-start | bytes 393224 | tf_op jit(solution)/shard_map/ppermute | solution.py:489
  74.3 5.0 %collective-permute-start.11 = (bf16[128,512]{1,0:T(8,128)(2,1)S(1)}, bf16[128,512]{1,0:T(8,128)(2,1)S(1)}, u32[]{:S(2)}, u32[]{:S(2)}) collective-permute-start(bf16[128,512]{1,0:T(8,128)(2,1)S(1)} %copy-done.16), channel_id=1, source_target_pairs={{0,4},{4,0},{1,5},{5,1},{2,6},{6,2},{3,7},{7,3},{8,12},{12,8},{9,1... | collective-permute-start | bytes 393224 | tf_op jit(solution)/shard_map/ppermute | solution.py:489
  74.7 7.0 %collective-permute-start.15 = (f32[8,128]{1,0:T(8,128)S(1)}, f32[8,128]{1,0:T(8,128)S(1)}, u32[]{:S(2)}, u32[]{:S(2)}) collective-permute-start(f32[8,128]{1,0:T(8,128)S(1)} %get-tuple-element.112.refs_7_), channel_id=1, source_target_pairs={{0,3},{1,2},{2,1},{3,0},{4,7},{5,6},{6,5},{7,4},{8,11},{9,10},{10,... | collective-permute-start | bytes 12296 | tf_op jit(solution)/shard_map/ppermute | solution.py:522
  77.6 4.6 %collective-permute-start.14 = (f32[8,128]{1,0:T(8,128)S(1)}, f32[8,128]{1,0:T(8,128)S(1)}, u32[]{:S(2)}, u32[]{:S(2)}) collective-permute-start(f32[8,128]{1,0:T(8,128)S(1)} %get-tuple-element.112.refs_7_), channel_id=1, source_target_pairs={{0,2},{1,3},{2,0},{3,1},{4,6},{5,7},{6,4},{7,5},{8,10},{9,11},{10,... | collective-permute-start | bytes 12296 | tf_op jit(solution)/shard_map/ppermute | solution.py:522
  78.2 4.0 %collective-permute-start.13 = (f32[8,128]{1,0:T(8,128)S(1)}, f32[8,128]{1,0:T(8,128)S(1)}, u32[]{:S(2)}, u32[]{:S(2)}) collective-permute-start(f32[8,128]{1,0:T(8,128)S(1)} %get-tuple-element.112.refs_7_), channel_id=1, source_target_pairs={{0,1},{1,0},{2,3},{3,2},{4,5},{5,4},{6,7},{7,6},{8,9},{9,8},{10,11... | collective-permute-start | bytes 12296 | tf_op jit(solution)/shard_map/ppermute | solution.py:522
  78.6 6.7 %collective-permute-start.16 = (bf16[128,512]{1,0:T(8,128)(2,1)S(1)}, bf16[128,512]{1,0:T(8,128)(2,1)S(1)}, u32[]{:S(2)}, u32[]{:S(2)}) collective-permute-start(bf16[128,512]{1,0:T(8,128)(2,1)S(1)} %copy-done.15), channel_id=1, source_target_pairs={{0,4},{4,0},{1,5},{5,1},{2,6},{6,2},{3,7},{7,3},{8,12},{12,8},{9,1... | collective-permute-start | bytes 393224 | tf_op jit(solution)/shard_map/ppermute | solution.py:489
  79.3 5.9 %collective-permute-start.17 = (bf16[128,512]{1,0:T(8,128)(2,1)S(1)}, bf16[128,512]{1,0:T(8,128)(2,1)S(1)}, u32[]{:S(2)}, u32[]{:S(2)}) collective-permute-start(bf16[128,512]{1,0:T(8,128)(2,1)S(1)} %copy-done.14), channel_id=1, source_target_pairs={{0,4},{4,0},{1,5},{5,1},{2,6},{6,2},{3,7},{7,3},{8,12},{12,8},{9,1... | collective-permute-start | bytes 393224 | tf_op jit(solution)/shard_map/ppermute | solution.py:489
  79.4 4.8 %copy-start.1 = (bf16[1,2,128,512]{3,2,1,0:T(8,128)(2,1)S(1)}, bf16[1,2,128,512]{3,2,1,0:T(8,128)(2,1)}, u32[]{:S(2)}) copy-start(bf16[1,2,128,512]{3,2,1,0:T(8,128)(2,1)} %refs_0_.5) | copy-start | bytes 786436
  79.4 4.8 %copy-start.3 = (bf16[1,2,128,512]{3,2,1,0:T(8,128)(2,1)S(1)}, bf16[1,2,128,512]{3,2,1,0:T(8,128)(2,1)}, u32[]{:S(2)}) copy-start(bf16[1,2,128,512]{3,2,1,0:T(8,128)(2,1)} %refs_1_.6) | copy-start | bytes 786436
  79.4 4.8 %copy-start.13 = (f32[2,128,512]{2,1,0:T(8,128)S(1)}, f32[2,128,512]{2,1,0:T(8,128)}, u32[]{:S(2)}) copy-start(f32[2,128,512]{2,1,0:T(8,128)} %get-tuple-element.106.pair_ref) | copy-start | bytes 1572868
  81.7 3.6 %collective-permute-start.19 = (bf16[4,128,128]{2,1,0:T(8,128)(2,1)S(1)}, bf16[4,128,128]{2,1,0:T(8,128)(2,1)S(1)}, u32[]{:S(2)}, u32[]{:S(2)}) collective-permute-start(bf16[4,128,128]{2,1,0:T(8,128)(2,1)S(1)} %convert_element_type.3), channel_id=1, source_target_pairs={{0,4},{4,0},{1,5},{5,1},{2,6},{6,2},{3,7},{7,3},{8,12},{12,8},{9,1... | collective-permute-start | bytes 393224 | tf_op jit(solution)/shard_map/ppermute | solution.py:489
  82.2 3.1 %collective-permute-start.18 = (bf16[4,128,128]{2,1,0:T(8,128)(2,1)S(1)}, bf16[4,128,128]{2,1,0:T(8,128)(2,1)S(1)}, u32[]{:S(2)}, u32[]{:S(2)}) collective-permute-start(bf16[4,128,128]{2,1,0:T(8,128)(2,1)S(1)} %bitcast.4), channel_id=1, source_target_pairs={{0,4},{4,0},{1,5},{5,1},{2,6},{6,2},{3,7},{7,3},{8,12},{12,8},{9,1... | collective-permute-start | bytes 393224 | tf_op jit(solution)/shard_map/ppermute | solution.py:489

commit v4 on v3

--- a/solution.py
+++ b/solution.py
@@ -420,69 +420,41 @@
     )(*far(own), *near(*others), weight)
 
 
-def shared_gradients(turn, k_ref, v_ref, grads, weight_ref, after_ref, second_ref, out_refs, hbm_refs, sems):
-    core = lax.axis_index("core")
-    seq = lax.rem(core + turn, 2)
-    weight = weight_of(seq, weight_ref)
-    for g in range(KV_HEADS):
-        span = slice(g * D, (g + 1) * D)
-        later = after_ref[g].astype(F32)
-        later = jnp.where(core == 0, later + second_ref[g].astype(F32), later).astype(BF16)
-        key_grad = grads[0][:, span].astype(F32) + dot(v_ref[0, seq, :, span], later, 1, 1)
-        value_grad = grads[1][:, span].astype(F32) + dot(k_ref[0, seq, :, span], later, 1, 0)
-        out_refs[0][:, span] = (weight * key_grad).astype(BF16)
-        out_refs[1][:, span] = (weight * value_grad).astype(BF16)
-    for copy in staged([(a, b.at[0, seq]) for a, b in zip(out_refs, hbm_refs)], sems):
-        copy.wait()
-
-
-def own_kernel(k_ref, v_ref, pair_ref, weight_ref, after_ref, second_ref, ko_hbm, vo_hbm, ko_ref, vo_ref, sems):
-    grads = (pair_ref.at[0], pair_ref.at[1])
-    shared_gradients(
-        0, k_ref, v_ref, grads, weight_ref, after_ref, second_ref, (ko_ref, vo_ref), (ko_hbm, vo_hbm), sems
-    )
-
-
-def other_kernel(*refs):
-    k_ref, v_ref, kg_ref, vg_ref, weight_ref, after_ref, second_ref, loss_ref, one_ref, two_ref, three_ref = refs[:11]
-    ko_hbm, vo_hbm, pair_loss_ref, ko_ref, vo_ref, sems = refs[13:]
+def final_kernel(*refs):
+    k_ref, v_ref, pair_ref, kg2_ref, vg2_ref, weight_ref = refs[:6]
+    after_ref, after2_ref, second_ref, second2_ref = refs[6:10]
+    loss_ref, one_ref, two_ref, three_ref, ko_ref, vo_ref, pair_loss_ref = refs[10:]
     pairs = lax.axis_size("dp")
     loss = ((loss_ref[...] + one_ref[...]) + (two_ref[...] + three_ref[...])) / pairs
     pair_loss_ref[0, 0] = jnp.max(loss)
-    shared_gradients(
-        1, k_ref, v_ref, (kg_ref, vg_ref), weight_ref, after_ref, second_ref, (ko_ref, vo_ref), (ko_hbm, vo_hbm), sems
-    )
-
-
-ROWS = (1, 2, T, KV_HEADS * D)
-FINAL = dict(
-    scratch_shapes=[pltpu.VMEM(ROWS[2:], BF16)] * 2 + [pltpu.SemaphoreType.DMA((2,))],
-    cost_estimate=pl.CostEstimate(flops=8 * 2 * D * D * T, bytes_accessed=1 << 20, transcendentals=0),
-    compiler_params=pltpu.CompilerParams(vmem_limit_bytes=SMALL_VMEM),
-)
-
-
-def own_gradients(*arrays):
-    return pl.pallas_call(
-        own_kernel,
-        in_specs=list(out_vmem(6)),
-        out_specs=(IN_HBM,) * 2,
-        out_shape=(pltpu.HBM(ROWS, BF16),) * 2,
-        name="own_gradients",
-        **FINAL,
+    core = lax.axis_index("core")
+    for turn, after, second, key_part, value_part in (
+        (0, after_ref, second_ref, pair_ref.at[0], pair_ref.at[1]),
+        (1, after2_ref, second2_ref, kg2_ref, vg2_ref),
+    ):
+        seq = lax.rem(core + turn, 2)
+        weight = weight_of(seq, weight_ref)
+        for g in range(KV_HEADS):
+            span = slice(g * D, (g + 1) * D)
+            later = after[g].astype(F32)
+            later = jnp.where(core == 0, later + second[g].astype(F32), later).astype(BF16)
+            key_grad = key_part[:, span].astype(F32) + dot(v_ref[0, seq, :, span], later, 1, 1)
+            value_grad = value_part[:, span].astype(F32) + dot(k_ref[0, seq, :, span], later, 1, 0)
+            ko_ref[0, seq, :, span] = (weight * key_grad).astype(BF16)
+            vo_ref[0, seq, :, span] = (weight * value_grad).astype(BF16)
+
+
+def final_pass(*arrays):
+    shape = pltpu.HBM((1, 2, T, KV_HEADS * D), BF16)
+    return pl.pallas_call(
+        final_kernel,
+        in_specs=list(out_vmem(14)),
+        out_specs=out_vmem(2) + (pl.BlockSpec(memory_space=pltpu.SMEM),),
+        out_shape=(shape, shape, jax.ShapeDtypeStruct((1, 1), F32)),
+        name="final_pass",
+        cost_estimate=pl.CostEstimate(flops=16 * 2 * D * D * T, bytes_accessed=3 << 20, transcendentals=0),
+        compiler_params=pltpu.CompilerParams(vmem_limit_bytes=SMALL_VMEM),
     )(*near(*arrays))
-
-
-def other_gradients(*arrays):
-    return pl.pallas_call(
-        other_kernel,
-        in_specs=list(out_vmem(11)) + [IN_HBM] * 2,
-        out_specs=(IN_HBM, IN_HBM, pl.BlockSpec(memory_space=pltpu.SMEM)),
-        out_shape=(pltpu.HBM(ROWS, BF16),) * 2 + (jax.ShapeDtypeStruct((1, 1), F32),),
-        input_output_aliases={11: 0, 12: 1},
-        name="other_gradients",
-        **FINAL,
-    )(*near(*arrays[:11]), *far(*arrays[11:]))
 
 
 def swap(x):
@@ -524,9 +496,8 @@
     weight = DPO_BETA * jax.nn.sigmoid(-DPO_BETA * delta) * scale
     query_rows = scaled_queries(qg, qg2, weight)
     after, query_rows, one, two, three = lax.optimization_barrier((after, query_rows, one, two, three))
-    held = own_gradients(kp, vp, pair, weight, after, second)
-    key_rows, value_rows, pair_loss = other_gradients(
-        kp, vp, kg2, vg2, weight, swap(after), second2, loss, one, two, three, *held
+    key_rows, value_rows, pair_loss = final_pass(
+        kp, vp, pair, kg2, vg2, weight, after, swap(after), second, second2, loss, one, two, three
     )
     return query_rows, key_rows, value_rows, pair_loss.reshape(())
 

time: 87.3 us -> 87 us (level)
  Pallas kernels: 18.8 us -> 17.5 us
  waiting for transfers between devices: 4.27 us -> 5.23 us
    pallas_call x2 -> x1, Pallas kernels: 2.49 us -> 1.19 us  [final_pass(): pl.pallas_call(final_kernel, in_specs=list(out_vmem(14)), out_specs=out_v...]
    ppermute x17, waiting for transfers between devices: 0.12 us -> 1.09 us  [swap(): return lax.ppermute(x, 'core', SWAP)]
  transfers between devices with their start and end apart: 22 -> 22, of which waited for: 2 -> 3; matrix products, arithmetic and copies ran while one was open for 0% -> 0% of each run, Pallas kernels for 12% -> 11%
where the time goes in v4:
time: 87 us; the launch traced here: 86.6 us
  blocking collectives  36 us (41%)
  starting transfers between devices  26.7 us (31%)
  Pallas kernels  17.5 us (20%)
  waiting for transfers between devices  5.23 us (6%)
  between operations  1.05 us (1%)
    all_to_all x2, blocking collectives, exchange(): return lax.all_to_all(x, 'chip', 0, 0, tiled=True)  36 us
    ppermute x17, starting transfers between devices, swap(): return lax.ppermute(x, 'core', SWAP)  12.4 us
    all_to_all x2, starting transfers between devices, exchange(): return lax.all_to_all(x, 'chip', 0, 0, tiled=True)  10.5 us
    pallas_call x1, Pallas kernels, forward_pass(): pl.pallas_call(forward_kernel, in_specs=[in_vmem] * 17, out_specs=(IN_HBM...  6.18 us
    pallas_call x1, Pallas kernels, backward_pass(): pl.pallas_call(backward_kernel, in_specs=[IN_HBM] * 8, out_specs=(IN_HBM,...  5.51 us
    all_to_all x2, waiting for transfers between devices, exchange(): return lax.all_to_all(x, 'chip', 0, 0, tiled=True)  4.14 us
    ppermute x3, starting transfers between devices, shards(): lax.ppermute(loss, 'dp', [(i, i ^ k) for i in range(pairs)])  3.82 us
    pallas_call x1, Pallas kernels, scaled_queries(): pl.pallas_call(scale_kernel, in_specs=[IN_HBM] + [in_vmem] * (GROUP + 1),...  2.26 us
  transfers between devices with their start and end apart: 22, of which 3 were waited for; matrix products, arithmetic and copies ran while one was open for 0% of the time, Pallas kernels for 11%

profile of v4, /device:TPU:1, one launch (start us, length us, event | category | flops | bytes accessed | tf_op | source)
XLA Modules:
  0.0 86.6 jit_solution(4186049788218898031)
XLA Ops:
  0.6 0.0 copy-start
  0.6 3.3 %collective-permute-start.2 = (bf16[1,2,128,512]{3,2,1,0:T(8,128)(2,1)}, bf16[1,2,128,512]{3,2,1,0:T(8,128)(2,1)S(1)}, u32[]{:S(2)}, u32[]{:S(2)}) collective-permute-start(bf16[1,2,128,512]{3,2,1,0:T(8,128)(2,1)} %refs_5_.1), channel_id=1, source_target_pairs={{0,4},{4,0},{1,5},{5,1},{2,6},{6,2},{3,7},{7,3},{8,12},{12,8},{9,1... | collective-permute-start | bytes 786440 | tf_op jit(solution)/shard_map/ppermute | solution.py:461
  4.0 0.1 collective-permute-start.3
  4.1 0.4 collective-permute-start
  4.5 0.1 collective-permute-start.1
  4.6 0.4 collective-permute-start.4
  5.0 1.4 %own_states.1 = (f32[2,4,128,128]{3,2,1,0:T(8,128)S(1)}, s32[1,2,128]{2,1,0:T(2,128)S(1)}) custom-call(bf16[1,2,128,512]{3,2,1,0:T(8,128)(2,1)} %refs_0_.5, bf16[1,2,128,512]{3,2,1,0:T(8,128)(2,1)} %refs_1_.6, bf16[1,2,128,512]{3,2,1,0:T(8,128)(2,1)} %refs_5_.1, bf16[1,2,128,512]{3,2,1,0:T(8,128)(2,1)} %refs_6_.1, s32[1,2,128]{2,1,0:T(2,128)} %refs_4_.2), custom_call_target="tpu_custom_call" | custom-call | flops 33554432 | bytes 1048576 | tf_op jit(solution)/shard_map/own_states/pallas_call | solution.py:67
  6.4 0.1 collective-permute-done.4.refs_15_
  6.5 0.0 collective-permute-done.3.vr2_ref.refs_14_
  6.5 0.0 collective-permute-done.kp2_ref.refs_11_.refs_4_
  6.5 0.0 copy-start.6
  6.5 0.0 collective-permute-done.1.vp2_ref.refs_12_.refs_5_
  6.5 0.0 copy-start.7
  6.5 0.5 collective-permute-start.6
  7.0 0.1 collective-permute-start.7
  7.1 0.4 collective-permute-start.5
  7.5 0.3 chip_states.1
  7.8 0.0 copy-start.8
  7.8 21.1 %all_to_all.20.x_ref = bf16[32,32,128]{2,1,0:T(8,128)(2,1)S(1)} all-to-all(bf16[32,32,128]{2,1,0:T(8,128)(2,1)S(1)} %chip_states.1), channel_id=1, replica_groups=mesh['chip'=32,'core'=2,'dp'=4] {'chip'}, dimensions={0} | all-to-all | bytes 524288 | tf_op jit(solution)/shard_map/all_to_all | solution.py:465
  28.9 0.0 copy-start.2
  28.9 0.0 copy-start.4
  28.9 14.9 %all_to_all.21 = bf16[32,32,128]{2,1,0:T(8,128)(2,1)S(1)} all-to-all(bf16[32,32,128]{2,1,0:T(8,128)(2,1)S(1)} %exclusive_prefix.1), channel_id=1, replica_groups=mesh['chip'=32,'core'=2,'dp'=4] {'chip'}, dimensions={0} | all-to-all | bytes 524288 | tf_op jit(solution)/shard_map/all_to_all | solution.py:465
  43.8 0.0 collective-permute-done.6.refs_9_
  43.8 0.0 collective-permute-done.7.refs_10_
  43.8 0.0 collective-permute-done.5.refs_8_.refs_3_
  43.8 0.0 copy-start.1
  43.9 6.2 %forward_pass.1 = (bf16[2,4,512,128]{3,2,1,0:T(8,128)(2,1)}, bf16[32,24,128]{2,1,0:T(8,128)(2,1)}, f32[4,128,128]{2,1,0:T(8,128)}, bf16[2,4,128,128]{3,2,1,0:T(8,128)(2,1)}) custom-call(bf16[1,2,128,2048]{3,2,1,0:T(8,128)(2,1)S(1)} %copy-done, bf16[1,2,128,2048]{3,2,1,0:T(8,128)(2,1)S(1)} %copy-done.8, bf16[1,2,128,2048]{3,2,1,0:T(8,128)(2,1)S(1)} %copy-done.9, ...), custom_call_target="tpu_custom_call" | custom-call | flops 805306368 | bytes 8388608 | tf_op jit(solution)/shard_map/forward_pass/pallas_call | solution.py:268
  50.1 5.4 %all-to-all-start.2 = ((bf16[32,24,128]{2,1,0:T(8,128)(2,1)}), bf16[32,24,128]{2,1,0:T(8,128)(2,1)S(1)}, u32[]{:S(2)}, u32[]{:S(2)}) async-start(bf16[32,24,128]{2,1,0:T(8,128)(2,1)} %get-tuple-element.68), calls=%async_computation.2 | async-start | bytes 393216 | tf_op jit(solution)/shard_map/all_to_all | solution.py:465
  55.6 5.5 %backward_pass.1 = (bf16[128,2048]{1,0:T(8,128)(2,1)}, f32[2,128,512]{2,1,0:T(8,128)}, bf16[128,512]{1,0:T(8,128)(2,1)}, bf16[128,512]{1,0:T(8,128)(2,1)}, bf16[...) custom-call(bf16[1,2,128,2048]{3,2,1,0:T(8,128)(2,1)} %refs_0_.4, ...), custom_call_target="tpu_custom_call" | custom-call | flops 805306368 | bytes 6291456 | tf_op jit(solution)/shard_map/backward_pass/pallas_call | solution.py:359
  61.1 4.1 %all-to-all-done.2.x_ref = bf16[32,24,128]{2,1,0:T(8,128)(2,1)S(1)} async-done(((bf16[32,24,128]{2,1,0:T(8,128)(2,1)}), bf16[32,24,128]{2,1,0:T(8,128)(2,1)S(1)}, u32[]{:S(2)}, u32[]{:S(2)}) %all-to-all-start.2) | async-done | bytes 196640 | tf_op jit(solution)/shard_map/all_to_all | solution.py:465
  65.2 0.7 exclusive_suffix.1
  65.9 5.1 %all-to-all-start.3 = ((bf16[32,16,128]{2,1,0:T(8,128)(2,1)}), bf16[32,16,128]{2,1,0:T(8,128)(2,1)S(1)}, u32[]{:S(2)}, u32[]{:S(2)}) async-start(bf16[32,16,128]{2,1,0:T(8,128)(2,1)} %get-tuple-element.89), calls=%async_computation.3 | async-start | bytes 262144 | tf_op jit(solution)/shard_map/all_to_all | solution.py:465
  71.0 2.7 %collective-permute-start.12 = (f32[8,128]{1,0:T(8,128)S(1)}, f32[8,128]{1,0:T(8,128)S(1)}, u32[]{:S(2)}, u32[]{:S(2)}) collective-permute-start(f32[8,128]{1,0:T(8,128)S(1)} %get-tuple-element.95), channel_id=1, source_target_pairs={{0,4},{4,0},{1,5},{5,1},{2,6},{6,2},{3,7},{7,3},{8,12},{12,8},{9,1... | collective-permute-start | bytes 12296 | tf_op jit(solution)/shard_map/ppermute | solution.py:461
  73.7 0.1 collective-permute-start.8
  73.8 0.4 collective-permute-start.9
  74.2 0.1 collective-permute-start.10
  74.3 0.4 collective-permute-start.11
  74.7 0.0 collective-permute-done.12
  74.7 2.8 %collective-permute-start.15 = (f32[8,128]{1,0:T(8,128)S(1)}, f32[8,128]{1,0:T(8,128)S(1)}, u32[]{:S(2)}, u32[]{:S(2)}) collective-permute-start(f32[8,128]{1,0:T(8,128)S(1)} %get-tuple-element.108.refs_10_), channel_id=1, source_target_pairs={{0,3},{1,2},{2,1},{3,0},{4,7},{5,6},{6,5},{7,4},{8,11},{9,10},{10,... | collective-permute-start | bytes 12296 | tf_op jit(solution)/shard_map/ppermute | solution.py:494
  77.6 0.6 collective-permute-start.14
  78.2 0.4 collective-permute-start.13
  78.6 0.7 collective-permute-start.16
  79.3 0.1 collective-permute-start.17
  79.4 2.3 %scaled_queries.1 = bf16[1,2,128,2048]{3,2,1,0:T(8,128)(2,1)} custom-call(bf16[128,2048]{1,0:T(8,128)(2,1)} %get-tuple-element.90.own_hbm, bf16[128,512]{1,0:T(8,128)(2,1)S(1)} %collective-permute-done.8.refs_0_, bf16[128,512]{1,0:T(8,128)(2,1)S(1)} %collective-permute-done.9.refs_1_, bf16[128,512]{1,0:T(8,128)(2,1)S(1)} %collective-permute-done.10.refs_2_, ...), custom_call_target="tpu_custom_call" | custom-call | flops 524288 | bytes 128 | tf_op jit(solution)/shard_map/scaled_queries/pallas_call | solution.py:406
  81.7 0.5 collective-permute-start.19
  82.2 2.0 %collective-permute-start.18 = (bf16[4,128,128]{2,1,0:T(8,128)(2,1)S(1)}, bf16[4,128,128]{2,1,0:T(8,128)(2,1)S(1)}, u32[]{:S(2)}, u32[]{:S(2)}) collective-permute-start(bf16[4,128,128]{2,1,0:T(8,128)(2,1)S(1)} %bitcast.4), channel_id=1, source_target_pairs={{0,4},{4,0},{1,5},{5,1},{2,6},{6,2},{3,7},{7,3},{8,12},{12,8},{9,1... | collective-permute-start | bytes 393224 | tf_op jit(solution)/shard_map/ppermute | solution.py:461
  84.3 1.0 %collective-permute-done.18.refs_7_ = bf16[4,128,128]{2,1,0:T(8,128)(2,1)S(1)} collective-permute-done((bf16[4,128,128]{2,1,0:T(8,128)(2,1)S(1)}, bf16[4,128,128]{2,1,0:T(8,128)(2,1)S(1)}, u32[]{:S(2)}, u32[]{:S(2)}) %collective-permute-start.18) | collective-permute-done | bytes 131104 | tf_op jit(solution)/shard_map/ppermute | solution.py:461
  85.2 1.2 %final_pass.1 = (bf16[1,2,128,512]{3,2,1,0:T(8,128)(2,1)}, bf16[1,2,128,512]{3,2,1,0:T(8,128)(2,1)}, f32[1,1]{1,0:T(1,128)}) custom-call(bf16[1,2,128,512]{3,2,1,0:T(8,128)(2,1)S(1)} %copy-done.3, bf16[1,2,128,512]{3,2,1,0:T(8,128)(2,1)S(1)} %copy-done.5, f32[2,128,512]{2,1,0:T(8,128)S(1)} %copy-done.13, ...), custom_call_target="tpu_custom_call" | custom-call | flops 67108864 | bytes 3145728 | tf_op jit(solution)/shard_map/final_pass/pallas_call | solution.py:449
  (42 shorter events, 0.2 us)
Async XLA Ops:
  0.6 6.5 %copy-start = (bf16[1,2,128,2048]{3,2,1,0:T(8,128)(2,1)S(1)}, bf16[1,2,128,2048]{3,2,1,0:T(8,128)(2,1)}, u32[]{:S(2)}) copy-start(bf16[1,2,128,2048]{3,2,1,0:T(8,128)(2,1)} %refs_0_.4) | copy-start | bytes 3145732
  0.6 5.8 %collective-permute-start.2 = (bf16[1,2,128,512]{3,2,1,0:T(8,128)(2,1)}, bf16[1,2,128,512]{3,2,1,0:T(8,128)(2,1)S(1)}, u32[]{:S(2)}, u32[]{:S(2)}) collective-permute-start(bf16[1,2,128,512]{3,2,1,0:T(8,128)(2,1)} %refs_5_.1), channel_id=1, source_target_pairs={{0,4},{4,0},{1,5},{5,1},{2,6},{6,2},{3,7},{7,3},{8,12},{12,8},{9,1... | collective-permute-start | bytes 786440 | tf_op jit(solution)/shard_map/ppermute | solution.py:461
  4.0 2.5 %collective-permute-start.3 = (bf16[1,2,128,512]{3,2,1,0:T(8,128)(2,1)}, bf16[1,2,128,512]{3,2,1,0:T(8,128)(2,1)S(1)}, u32[]{:S(2)}, u32[]{:S(2)}) collective-permute-start(bf16[1,2,128,512]{3,2,1,0:T(8,128)(2,1)} %refs_6_.1), channel_id=1, source_target_pairs={{0,4},{4,0},{1,5},{5,1},{2,6},{6,2},{3,7},{7,3},{8,12},{12,8},{9,1... | collective-permute-start | bytes 786440 | tf_op jit(solution)/shard_map/ppermute | solution.py:461
  4.1 2.4 %collective-permute-start = (bf16[1,2,128,512]{3,2,1,0:T(8,128)(2,1)}, bf16[1,2,128,512]{3,2,1,0:T(8,128)(2,1)S(1)}, u32[]{:S(2)}, u32[]{:S(2)}) collective-permute-start(bf16[1,2,128,512]{3,2,1,0:T(8,128)(2,1)} %refs_0_.5), channel_id=1, source_target_pairs={{0,4},{4,0},{1,5},{5,1},{2,6},{6,2},{3,7},{7,3},{8,12},{12,8},{9,1... | collective-permute-start | bytes 786440 | tf_op jit(solution)/shard_map/ppermute | solution.py:461
  4.5 2.0 %collective-permute-start.1 = (bf16[1,2,128,512]{3,2,1,0:T(8,128)(2,1)}, bf16[1,2,128,512]{3,2,1,0:T(8,128)(2,1)S(1)}, u32[]{:S(2)}, u32[]{:S(2)}) collective-permute-start(bf16[1,2,128,512]{3,2,1,0:T(8,128)(2,1)} %refs_1_.6), channel_id=1, source_target_pairs={{0,4},{4,0},{1,5},{5,1},{2,6},{6,2},{3,7},{7,3},{8,12},{12,8},{9,1... | collective-permute-start | bytes 786440 | tf_op jit(solution)/shard_map/ppermute | solution.py:461
  4.6 1.9 %collective-permute-start.4 = (s32[1,2,128]{2,1,0:T(2,128)}, s32[1,2,128]{2,1,0:T(2,128)S(1)}, u32[]{:S(2)}, u32[]{:S(2)}) collective-permute-start(s32[1,2,128]{2,1,0:T(2,128)} %refs_4_.2), channel_id=1, source_target_pairs={{0,4},{4,0},{1,5},{5,1},{2,6},{6,2},{3,7},{7,3},{8,12},{12,8},{9,1... | collective-permute-start | bytes 3080 | tf_op jit(solution)/shard_map/ppermute | solution.py:461
  6.5 37.3 %copy-start.6 = (bf16[1,2,128,512]{3,2,1,0:T(8,128)(2,1)}, bf16[1,2,128,512]{3,2,1,0:T(8,128)(2,1)S(1)}, u32[]{:S(2)}) copy-start(bf16[1,2,128,512]{3,2,1,0:T(8,128)(2,1)S(1)} %collective-permute-done.kp2_ref.refs_11_.refs_4_) | copy-start | bytes 786436
  6.5 37.3 %copy-start.7 = (bf16[1,2,128,512]{3,2,1,0:T(8,128)(2,1)}, bf16[1,2,128,512]{3,2,1,0:T(8,128)(2,1)S(1)}, u32[]{:S(2)}) copy-start(bf16[1,2,128,512]{3,2,1,0:T(8,128)(2,1)S(1)} %collective-permute-done.1.vp2_ref.refs_12_.refs_5_) | copy-start | bytes 786436
  6.5 37.3 %collective-permute-start.6 = (bf16[1,2,128,2048]{3,2,1,0:T(8,128)(2,1)}, bf16[1,2,128,2048]{3,2,1,0:T(8,128)(2,1)S(1)}, u32[]{:S(2)}, u32[]{:S(2)}) collective-permute-start(bf16[1,2,128,2048]{3,2,1,0:T(8,128)(2,1)} %refs_1_.4), channel_id=1, source_target_pairs={{0,4},{4,0},{1,5},{5,1},{2,6},{6,2},{3,7},{7,3},{8,12},{12,8},{9,1... | collective-permute-start | bytes 3145736 | tf_op jit(solution)/shard_map/ppermute | solution.py:461
  7.0 36.8 %collective-permute-start.7 = (bf16[1,2,128,2048]{3,2,1,0:T(8,128)(2,1)}, bf16[1,2,128,2048]{3,2,1,0:T(8,128)(2,1)S(1)}, u32[]{:S(2)}, u32[]{:S(2)}) collective-permute-start(bf16[1,2,128,2048]{3,2,1,0:T(8,128)(2,1)} %refs_2_.3), channel_id=1, source_target_pairs={{0,4},{4,0},{1,5},{5,1},{2,6},{6,2},{3,7},{7,3},{8,12},{12,8},{9,1... | collective-permute-start | bytes 3145736 | tf_op jit(solution)/shard_map/ppermute | solution.py:461
  7.1 36.7 %collective-permute-start.5 = (bf16[1,2,128,2048]{3,2,1,0:T(8,128)(2,1)S(1)}, bf16[1,2,128,2048]{3,2,1,0:T(8,128)(2,1)S(1)}, u32[]{:S(2)}, u32[]{:S(2)}) collective-permute-start(bf16[1,2,128,2048]{3,2,1,0:T(8,128)(2,1)S(1)} %copy-done), channel_id=1, source_target_pairs={{0,4},{4,0},{1,5},{5,1},{2,6},{6,2},{3,7},{7,3},{8,12},{12,8},{9,1... | collective-permute-start | bytes 3145736 | tf_op jit(solution)/shard_map/ppermute | solution.py:461
  7.5 36.4 %copy-start.9 = (bf16[1,2,128,2048]{3,2,1,0:T(8,128)(2,1)S(1)}, bf16[1,2,128,2048]{3,2,1,0:T(8,128)(2,1)}, u32[]{:S(2)}) copy-start(bf16[1,2,128,2048]{3,2,1,0:T(8,128)(2,1)} %refs_2_.3) | copy-start | bytes 3145732
  7.5 36.4 %copy-start.10 = (bf16[1,2,128,512]{3,2,1,0:T(8,128)(2,1)S(1)}, bf16[1,2,128,512]{3,2,1,0:T(8,128)(2,1)}, u32[]{:S(2)}) copy-start(bf16[1,2,128,512]{3,2,1,0:T(8,128)(2,1)} %refs_5_.1) | copy-start | bytes 786436
  7.5 36.4 %copy-start.11 = (bf16[1,2,128,512]{3,2,1,0:T(8,128)(2,1)S(1)}, bf16[1,2,128,512]{3,2,1,0:T(8,128)(2,1)}, u32[]{:S(2)}) copy-start(bf16[1,2,128,512]{3,2,1,0:T(8,128)(2,1)} %refs_6_.1) | copy-start | bytes 786436
  7.8 36.1 %copy-start.8 = (bf16[1,2,128,2048]{3,2,1,0:T(8,128)(2,1)S(1)}, bf16[1,2,128,2048]{3,2,1,0:T(8,128)(2,1)}, u32[]{:S(2)}) copy-start(bf16[1,2,128,2048]{3,2,1,0:T(8,128)(2,1)} %refs_1_.4) | copy-start | bytes 3145732
  28.9 15.0 %copy-start.2 = (bf16[1,2,128,512]{3,2,1,0:T(8,128)(2,1)S(1)}, bf16[1,2,128,512]{3,2,1,0:T(8,128)(2,1)}, u32[]{:S(2)}) copy-start(bf16[1,2,128,512]{3,2,1,0:T(8,128)(2,1)} %refs_0_.5) | copy-start | bytes 786436
  28.9 15.0 %copy-start.4 = (bf16[1,2,128,512]{3,2,1,0:T(8,128)(2,1)S(1)}, bf16[1,2,128,512]{3,2,1,0:T(8,128)(2,1)}, u32[]{:S(2)}) copy-start(bf16[1,2,128,512]{3,2,1,0:T(8,128)(2,1)} %refs_1_.6) | copy-start | bytes 786436
  43.8 6.3 %copy-start.1 = (bf16[1,2,128,2048]{3,2,1,0:T(8,128)(2,1)}, bf16[1,2,128,2048]{3,2,1,0:T(8,128)(2,1)S(1)}, u32[]{:S(2)}) copy-start(bf16[1,2,128,2048]{3,2,1,0:T(8,128)(2,1)S(1)} %collective-permute-done.5.refs_8_.refs_3_) | copy-start | bytes 3145732
  50.1 5.4 %copy-start.12 = (f32[4,128,128]{2,1,0:T(8,128)S(1)}, f32[4,128,128]{2,1,0:T(8,128)}, u32[]{:S(2)}) copy-start(f32[4,128,128]{2,1,0:T(8,128)} %get-tuple-element.88.refs_8_) | copy-start | bytes 786436
  50.1 15.1 %all-to-all-start.2 = ((bf16[32,24,128]{2,1,0:T(8,128)(2,1)}), bf16[32,24,128]{2,1,0:T(8,128)(2,1)S(1)}, u32[]{:S(2)}, u32[]{:S(2)}) async-start(bf16[32,24,128]{2,1,0:T(8,128)(2,1)} %get-tuple-element.68), calls=%async_computation.2 | async-start | bytes 393216 | tf_op jit(solution)/shard_map/all_to_all | solution.py:465
  65.2 9.1 %copy-start.16 = (bf16[128,512]{1,0:T(8,128)(2,1)S(1)}, bf16[128,512]{1,0:T(8,128)(2,1)}, u32[]{:S(2)}) copy-start(bf16[128,512]{1,0:T(8,128)(2,1)} %get-tuple-element.94) | copy-start | bytes 393220
  65.9 12.7 %copy-start.15 = (bf16[128,512]{1,0:T(8,128)(2,1)S(1)}, bf16[128,512]{1,0:T(8,128)(2,1)}, u32[]{:S(2)}) copy-start(bf16[128,512]{1,0:T(8,128)(2,1)} %get-tuple-element.98) | copy-start | bytes 393220
  65.9 13.4 %copy-start.14 = (bf16[128,512]{1,0:T(8,128)(2,1)S(1)}, bf16[128,512]{1,0:T(8,128)(2,1)}, u32[]{:S(2)}) copy-start(bf16[128,512]{1,0:T(8,128)(2,1)} %get-tuple-element.99) | copy-start | bytes 393220
  65.9 16.3 %all-to-all-start.3 = ((bf16[32,16,128]{2,1,0:T(8,128)(2,1)}), bf16[32,16,128]{2,1,0:T(8,128)(2,1)S(1)}, u32[]{:S(2)}, u32[]{:S(2)}) async-start(bf16[32,16,128]{2,1,0:T(8,128)(2,1)} %get-tuple-element.89), calls=%async_computation.3 | async-start | bytes 262144 | tf_op jit(solution)/shard_map/all_to_all | solution.py:465
  71.0 3.7 %collective-permute-start.12 = (f32[8,128]{1,0:T(8,128)S(1)}, f32[8,128]{1,0:T(8,128)S(1)}, u32[]{:S(2)}, u32[]{:S(2)}) collective-permute-start(f32[8,128]{1,0:T(8,128)S(1)} %get-tuple-element.95), channel_id=1, source_target_pairs={{0,4},{4,0},{1,5},{5,1},{2,6},{6,2},{3,7},{7,3},{8,12},{12,8},{9,1... | collective-permute-start | bytes 12296 | tf_op jit(solution)/shard_map/ppermute | solution.py:461
  73.7 3.9 %collective-permute-start.8 = (bf16[128,512]{1,0:T(8,128)(2,1)}, bf16[128,512]{1,0:T(8,128)(2,1)S(1)}, u32[]{:S(2)}, u32[]{:S(2)}) collective-permute-start(bf16[128,512]{1,0:T(8,128)(2,1)} %get-tuple-element.91), channel_id=1, source_target_pairs={{0,4},{4,0},{1,5},{5,1},{2,6},{6,2},{3,7},{7,3},{8,12},{12,8},{9,1... | collective-permute-start | bytes 393224 | tf_op jit(solution)/shard_map/ppermute | solution.py:461
  73.8 4.4 %collective-permute-start.9 = (bf16[128,512]{1,0:T(8,128)(2,1)}, bf16[128,512]{1,0:T(8,128)(2,1)S(1)}, u32[]{:S(2)}, u32[]{:S(2)}) collective-permute-start(bf16[128,512]{1,0:T(8,128)(2,1)} %get-tuple-element.92), channel_id=1, source_target_pairs={{0,4},{4,0},{1,5},{5,1},{2,6},{6,2},{3,7},{7,3},{8,12},{12,8},{9,1... | collective-permute-start | bytes 393224 | tf_op jit(solution)/shard_map/ppermute | solution.py:461
  74.2 4.4 %collective-permute-start.10 = (bf16[128,512]{1,0:T(8,128)(2,1)}, bf16[128,512]{1,0:T(8,128)(2,1)S(1)}, u32[]{:S(2)}, u32[]{:S(2)}) collective-permute-start(bf16[128,512]{1,0:T(8,128)(2,1)} %get-tuple-element.93), channel_id=1, source_target_pairs={{0,4},{4,0},{1,5},{5,1},{2,6},{6,2},{3,7},{7,3},{8,12},{12,8},{9,1... | collective-permute-start | bytes 393224 | tf_op jit(solution)/shard_map/ppermute | solution.py:461
  74.3 5.0 %collective-permute-start.11 = (bf16[128,512]{1,0:T(8,128)(2,1)S(1)}, bf16[128,512]{1,0:T(8,128)(2,1)S(1)}, u32[]{:S(2)}, u32[]{:S(2)}) collective-permute-start(bf16[128,512]{1,0:T(8,128)(2,1)S(1)} %copy-done.16), channel_id=1, source_target_pairs={{0,4},{4,0},{1,5},{5,1},{2,6},{6,2},{3,7},{7,3},{8,12},{12,8},{9,1... | collective-permute-start | bytes 393224 | tf_op jit(solution)/shard_map/ppermute | solution.py:461
  74.7 6.9 %collective-permute-start.15 = (f32[8,128]{1,0:T(8,128)S(1)}, f32[8,128]{1,0:T(8,128)S(1)}, u32[]{:S(2)}, u32[]{:S(2)}) collective-permute-start(f32[8,128]{1,0:T(8,128)S(1)} %get-tuple-element.108.refs_10_), channel_id=1, source_target_pairs={{0,3},{1,2},{2,1},{3,0},{4,7},{5,6},{6,5},{7,4},{8,11},{9,10},{10,... | collective-permute-start | bytes 12296 | tf_op jit(solution)/shard_map/ppermute | solution.py:494
  77.6 4.6 %collective-permute-start.14 = (f32[8,128]{1,0:T(8,128)S(1)}, f32[8,128]{1,0:T(8,128)S(1)}, u32[]{:S(2)}, u32[]{:S(2)}) collective-permute-start(f32[8,128]{1,0:T(8,128)S(1)} %get-tuple-element.108.refs_10_), channel_id=1, source_target_pairs={{0,2},{1,3},{2,0},{3,1},{4,6},{5,7},{6,4},{7,5},{8,10},{9,11},{10,... | collective-permute-start | bytes 12296 | tf_op jit(solution)/shard_map/ppermute | solution.py:494
  78.2 4.0 %collective-permute-start.13 = (f32[8,128]{1,0:T(8,128)S(1)}, f32[8,128]{1,0:T(8,128)S(1)}, u32[]{:S(2)}, u32[]{:S(2)}) collective-permute-start(f32[8,128]{1,0:T(8,128)S(1)} %get-tuple-element.108.refs_10_), channel_id=1, source_target_pairs={{0,1},{1,0},{2,3},{3,2},{4,5},{5,4},{6,7},{7,6},{8,9},{9,8},{10,11... | collective-permute-start | bytes 12296 | tf_op jit(solution)/shard_map/ppermute | solution.py:494
  78.6 5.7 %collective-permute-start.16 = (bf16[128,512]{1,0:T(8,128)(2,1)S(1)}, bf16[128,512]{1,0:T(8,128)(2,1)S(1)}, u32[]{:S(2)}, u32[]{:S(2)}) collective-permute-start(bf16[128,512]{1,0:T(8,128)(2,1)S(1)} %copy-done.15), channel_id=1, source_target_pairs={{0,4},{4,0},{1,5},{5,1},{2,6},{6,2},{3,7},{7,3},{8,12},{12,8},{9,1... | collective-permute-start | bytes 393224 | tf_op jit(solution)/shard_map/ppermute | solution.py:461
  79.3 4.9 %collective-permute-start.17 = (bf16[128,512]{1,0:T(8,128)(2,1)S(1)}, bf16[128,512]{1,0:T(8,128)(2,1)S(1)}, u32[]{:S(2)}, u32[]{:S(2)}) collective-permute-start(bf16[128,512]{1,0:T(8,128)(2,1)S(1)} %copy-done.14), channel_id=1, source_target_pairs={{0,4},{4,0},{1,5},{5,1},{2,6},{6,2},{3,7},{7,3},{8,12},{12,8},{9,1... | collective-permute-start | bytes 393224 | tf_op jit(solution)/shard_map/ppermute | solution.py:461
  79.4 5.8 %copy-start.3 = (bf16[1,2,128,512]{3,2,1,0:T(8,128)(2,1)S(1)}, bf16[1,2,128,512]{3,2,1,0:T(8,128)(2,1)}, u32[]{:S(2)}) copy-start(bf16[1,2,128,512]{3,2,1,0:T(8,128)(2,1)} %refs_0_.5) | copy-start | bytes 786436
  79.4 5.8 %copy-start.5 = (bf16[1,2,128,512]{3,2,1,0:T(8,128)(2,1)S(1)}, bf16[1,2,128,512]{3,2,1,0:T(8,128)(2,1)}, u32[]{:S(2)}) copy-start(bf16[1,2,128,512]{3,2,1,0:T(8,128)(2,1)} %refs_1_.6) | copy-start | bytes 786436
  79.4 5.8 %copy-start.13 = (f32[2,128,512]{2,1,0:T(8,128)S(1)}, f32[2,128,512]{2,1,0:T(8,128)}, u32[]{:S(2)}) copy-start(f32[2,128,512]{2,1,0:T(8,128)} %get-tuple-element.97.refs_2_) | copy-start | bytes 1572868
  81.7 2.6 %collective-permute-start.19 = (bf16[4,128,128]{2,1,0:T(8,128)(2,1)S(1)}, bf16[4,128,128]{2,1,0:T(8,128)(2,1)S(1)}, u32[]{:S(2)}, u32[]{:S(2)}) collective-permute-start(bf16[4,128,128]{2,1,0:T(8,128)(2,1)S(1)} %convert_element_type.3), channel_id=1, source_target_pairs={{0,4},{4,0},{1,5},{5,1},{2,6},{6,2},{3,7},{7,3},{8,12},{12,8},{9,1... | collective-permute-start | bytes 393224 | tf_op jit(solution)/shard_map/ppermute | solution.py:461
  82.2 3.0 %collective-permute-start.18 = (bf16[4,128,128]{2,1,0:T(8,128)(2,1)S(1)}, bf16[4,128,128]{2,1,0:T(8,128)(2,1)S(1)}, u32[]{:S(2)}, u32[]{:S(2)}) collective-permute-start(bf16[4,128,128]{2,1,0:T(8,128)(2,1)S(1)} %bitcast.4), channel_id=1, source_target_pairs={{0,4},{4,0},{1,5},{5,1},{2,6},{6,2},{3,7},{7,3},{8,12},{12,8},{9,1... | collective-permute-start | bytes 393224 | tf_op jit(solution)/shard_map/ppermute | solution.py:461

commit v5 on v4

--- a/solution.py
+++ b/solution.py
@@ -175,8 +175,8 @@
 def forward_kernel(*refs):
     blocks = (refs[:8], refs[8:16])
     before_ref = refs[16]
-    pulled_out, total_ref, second_out, carried_out = refs[17:21]
-    pulled_ref, second_ref, carried_ref, acc_ref, out_sems = refs[21:]
+    pulled_out, payload_out, second_out, carried_out = refs[17:21]
+    pulled_ref, second_ref, carried_ref, acc_ref, total_ref, out_sems, score_sem = refs[21:]
     core = lax.axis_index("core")
     causal = causal_rows()
     row = lax.broadcasted_iota(jnp.int32, (T, T), 0)
@@ -211,6 +211,11 @@
 
     def copies(g):
         return (
+            pltpu.make_async_copy(
+                total_ref.at[pl.ds(g * chunks, chunks), 0:rows],
+                payload_out.at[pl.ds(g * chunks, chunks), 0:rows],
+                out_sems.at[3, g],
+            ),
             pltpu.make_async_copy(pulled_ref.at[:, g], pulled_out.at[:, g], out_sems.at[0, g]),
             pltpu.make_async_copy(second_ref.at[g], second_out.at[g], out_sems.at[1, g]),
             pltpu.make_async_copy(carried_ref.at[:, g], carried_out.at[:, g], out_sems.at[2, g]),
@@ -257,9 +262,14 @@
     pieces = jnp.where(place == 0, high, jnp.where(place == 1, middle, jnp.where(place == 2, low, 0.0))).astype(BF16)
     for chip in range(CHIPS):
         total_ref[chip, rows : rows + SCALAR_ROWS, :] = pieces
+    scores_copy = pltpu.make_async_copy(
+        total_ref.at[:, rows : rows + SCALAR_ROWS], payload_out.at[:, rows : rows + SCALAR_ROWS], score_sem
+    )
+    scores_copy.start()
     for g in range(KV_HEADS):
         for copy in copies(g):
             copy.wait()
+    scores_copy.wait()
 
 
 def forward_pass(*arrays):
@@ -268,7 +278,7 @@
     return pl.pallas_call(
         forward_kernel,
         in_specs=[in_vmem] * 17,
-        out_specs=(IN_HBM, in_vmem, IN_HBM, IN_HBM),
+        out_specs=(IN_HBM,) * 4,
         out_shape=(
             pltpu.HBM((2, KV_HEADS, GROUP * T, D), BF16),
             pltpu.HBM((CHIPS, rows, D), BF16),
@@ -280,7 +290,9 @@
             pltpu.VMEM((KV_HEADS, D, D), F32),
             pltpu.VMEM((2, KV_HEADS, D, D), BF16),
             pltpu.VMEM((8, D), F32),
-            pltpu.SemaphoreType.DMA((3, KV_HEADS)),
+            pltpu.VMEM((CHIPS, rows, D), BF16),
+            pltpu.SemaphoreType.DMA((4, KV_HEADS)),
+            pltpu.SemaphoreType.DMA(()),
         ],
         name="forward_pass",
         cost_estimate=pl.CostEstimate(flops=192 * 2 * D * D * T, bytes_accessed=8 << 20, transcendentals=65536),

time: 87 us -> 86.6 us (level)
  no operation moved by 1% of the time
where the time goes in v5:
time: 86.6 us; the launch traced here: 86.2 us
  blocking collectives  36 us (42%)
  starting transfers between devices  26.7 us (31%)
  Pallas kernels  17.1 us (20%)
  waiting for transfers between devices  5.23 us (6%)
  between operations  1.05 us (1%)
    all_to_all x2, blocking collectives, exchange(): return lax.all_to_all(x, 'chip', 0, 0, tiled=True)  36 us
    ppermute x17, starting transfers between devices, swap(): return lax.ppermute(x, 'core', SWAP)  12.4 us
    all_to_all x2, starting transfers between devices, exchange(): return lax.all_to_all(x, 'chip', 0, 0, tiled=True)  10.5 us
    pallas_call x1, Pallas kernels, forward_pass(): pl.pallas_call(forward_kernel, in_specs=[in_vmem] * 17, out_specs=(IN_HBM...  5.76 us
    pallas_call x1, Pallas kernels, backward_pass(): pl.pallas_call(backward_kernel, in_specs=[IN_HBM] * 8, out_specs=(IN_HBM,...  5.51 us
    all_to_all x2, waiting for transfers between devices, exchange(): return lax.all_to_all(x, 'chip', 0, 0, tiled=True)  4.13 us
    ppermute x3, starting transfers between devices, shards(): lax.ppermute(loss, 'dp', [(i, i ^ k) for i in range(pairs)])  3.83 us
    pallas_call x1, Pallas kernels, scaled_queries(): pl.pallas_call(scale_kernel, in_specs=[IN_HBM] + [in_vmem] * (GROUP + 1),...  2.26 us
  transfers between devices with their start and end apart: 22, of which 3 were waited for; matrix products, arithmetic and copies ran while one was open for 0% of the time, Pallas kernels for 11%

profile of v5, /device:TPU:1, one launch (start us, length us, event | category | flops | bytes accessed | tf_op | source)
XLA Modules:
  0.0 86.2 jit_solution(2330816665049750561)
XLA Ops:
  0.6 0.0 copy-start
  0.6 3.3 %collective-permute-start.2 = (bf16[1,2,128,512]{3,2,1,0:T(8,128)(2,1)}, bf16[1,2,128,512]{3,2,1,0:T(8,128)(2,1)S(1)}, u32[]{:S(2)}, u32[]{:S(2)}) collective-permute-start(bf16[1,2,128,512]{3,2,1,0:T(8,128)(2,1)} %refs_5_.1), channel_id=1, source_target_pairs={{0,4},{4,0},{1,5},{5,1},{2,6},{6,2},{3,7},{7,3},{8,12},{12,8},{9,1... | collective-permute-start | bytes 786440 | tf_op jit(solution)/shard_map/ppermute | solution.py:473
  4.0 0.1 collective-permute-start.3
  4.1 0.4 collective-permute-start
  4.5 0.1 collective-permute-start.1
  4.6 0.4 collective-permute-start.4
  5.0 1.4 %own_states.1 = (f32[2,4,128,128]{3,2,1,0:T(8,128)S(1)}, s32[1,2,128]{2,1,0:T(2,128)S(1)}) custom-call(bf16[1,2,128,512]{3,2,1,0:T(8,128)(2,1)} %refs_0_.5, bf16[1,2,128,512]{3,2,1,0:T(8,128)(2,1)} %refs_1_.6, bf16[1,2,128,512]{3,2,1,0:T(8,128)(2,1)} %refs_5_.1, bf16[1,2,128,512]{3,2,1,0:T(8,128)(2,1)} %refs_6_.1, s32[1,2,128]{2,1,0:T(2,128)} %refs_4_.2), custom_call_target="tpu_custom_call" | custom-call | flops 33554432 | bytes 1048576 | tf_op jit(solution)/shard_map/own_states/pallas_call | solution.py:67
  6.4 0.1 collective-permute-done.4.refs_15_
  6.5 0.0 collective-permute-done.2.kr2_ref.refs_13_
  6.5 0.0 collective-permute-done.3.vr2_ref.refs_14_
  6.5 0.0 collective-permute-done.kp2_ref.refs_11_.refs_4_
  6.5 0.0 copy-start.6
  6.5 0.0 collective-permute-done.1.vp2_ref.refs_12_.refs_5_
  6.5 0.0 copy-start.7
  6.5 0.5 collective-permute-start.6
  7.0 0.1 collective-permute-start.7
  7.1 0.4 collective-permute-start.5
  7.5 0.3 chip_states.1
  7.8 0.0 copy-start.8
  7.8 21.1 %all_to_all.20.x_ref = bf16[32,32,128]{2,1,0:T(8,128)(2,1)S(1)} all-to-all(bf16[32,32,128]{2,1,0:T(8,128)(2,1)S(1)} %chip_states.1), channel_id=1, replica_groups=mesh['chip'=32,'core'=2,'dp'=4] {'chip'}, dimensions={0} | all-to-all | bytes 524288 | tf_op jit(solution)/shard_map/all_to_all | solution.py:477
  28.9 0.0 copy-start.2
  28.9 0.0 copy-start.4
  28.9 14.9 %all_to_all.21 = bf16[32,32,128]{2,1,0:T(8,128)(2,1)S(1)} all-to-all(bf16[32,32,128]{2,1,0:T(8,128)(2,1)S(1)} %exclusive_prefix.1), channel_id=1, replica_groups=mesh['chip'=32,'core'=2,'dp'=4] {'chip'}, dimensions={0} | all-to-all | bytes 524288 | tf_op jit(solution)/shard_map/all_to_all | solution.py:477
  43.8 0.0 collective-permute-done.6.refs_9_
  43.8 0.0 collective-permute-done.7.refs_10_
  43.8 0.0 collective-permute-done.5.refs_8_.refs_3_
  43.8 0.0 copy-start.1
  43.9 5.8 %forward_pass.1 = (bf16[2,4,512,128]{3,2,1,0:T(8,128)(2,1)}, bf16[32,24,128]{2,1,0:T(8,128)(2,1)}, f32[4,128,128]{2,1,0:T(8,128)}, bf16[2,4,128,128]{3,2,1,0:T(8,128)(2,1)}) custom-call(bf16[1,2,128,2048]{3,2,1,0:T(8,128)(2,1)S(1)} %copy-done, bf16[1,2,128,2048]{3,2,1,0:T(8,128)(2,1)S(1)} %copy-done.8, bf16[1,2,128,2048]{3,2,1,0:T(8,128)(2,1)S(1)} %copy-done.9, ...), custom_call_target="tpu_custom_call" | custom-call | flops 805306368 | bytes 8388608 | tf_op jit(solution)/shard_map/forward_pass/pallas_call | solution.py:278
  49.7 5.4 %all-to-all-start.2 = ((bf16[32,24,128]{2,1,0:T(8,128)(2,1)}), bf16[32,24,128]{2,1,0:T(8,128)(2,1)S(1)}, u32[]{:S(2)}, u32[]{:S(2)}) async-start(bf16[32,24,128]{2,1,0:T(8,128)(2,1)} %get-tuple-element.68), calls=%async_computation.2 | async-start | bytes 393216 | tf_op jit(solution)/shard_map/all_to_all | solution.py:477
  55.1 5.5 %backward_pass.1 = (bf16[128,2048]{1,0:T(8,128)(2,1)}, f32[2,128,512]{2,1,0:T(8,128)}, bf16[128,512]{1,0:T(8,128)(2,1)}, bf16[128,512]{1,0:T(8,128)(2,1)}, bf16[...) custom-call(bf16[1,2,128,2048]{3,2,1,0:T(8,128)(2,1)} %refs_0_.4, ...), custom_call_target="tpu_custom_call" | custom-call | flops 805306368 | bytes 6291456 | tf_op jit(solution)/shard_map/backward_pass/pallas_call | solution.py:371
  60.7 4.1 %all-to-all-done.2.x_ref = bf16[32,24,128]{2,1,0:T(8,128)(2,1)S(1)} async-done(((bf16[32,24,128]{2,1,0:T(8,128)(2,1)}), bf16[32,24,128]{2,1,0:T(8,128)(2,1)S(1)}, u32[]{:S(2)}, u32[]{:S(2)}) %all-to-all-start.2) | async-done | bytes 196640 | tf_op jit(solution)/shard_map/all_to_all | solution.py:477
  64.8 0.7 exclusive_suffix.1
  65.5 5.1 %all-to-all-start.3 = ((bf16[32,16,128]{2,1,0:T(8,128)(2,1)}), bf16[32,16,128]{2,1,0:T(8,128)(2,1)S(1)}, u32[]{:S(2)}, u32[]{:S(2)}) async-start(bf16[32,16,128]{2,1,0:T(8,128)(2,1)} %get-tuple-element.89), calls=%async_computation.3 | async-start | bytes 262144 | tf_op jit(solution)/shard_map/all_to_all | solution.py:477
  70.6 2.7 %collective-permute-start.12 = (f32[8,128]{1,0:T(8,128)S(1)}, f32[8,128]{1,0:T(8,128)S(1)}, u32[]{:S(2)}, u32[]{:S(2)}) collective-permute-start(f32[8,128]{1,0:T(8,128)S(1)} %get-tuple-element.95), channel_id=1, source_target_pairs={{0,4},{4,0},{1,5},{5,1},{2,6},{6,2},{3,7},{7,3},{8,12},{12,8},{9,1... | collective-permute-start | bytes 12296 | tf_op jit(solution)/shard_map/ppermute | solution.py:473
  73.3 0.1 collective-permute-start.8
  73.4 0.4 collective-permute-start.9
  73.8 0.1 collective-permute-start.10
  73.9 0.4 collective-permute-start.11
  74.3 2.8 %collective-permute-start.15 = (f32[8,128]{1,0:T(8,128)S(1)}, f32[8,128]{1,0:T(8,128)S(1)}, u32[]{:S(2)}, u32[]{:S(2)}) collective-permute-start(f32[8,128]{1,0:T(8,128)S(1)} %get-tuple-element.108.refs_10_), channel_id=1, source_target_pairs={{0,3},{1,2},{2,1},{3,0},{4,7},{5,6},{6,5},{7,4},{8,11},{9,10},{10,... | collective-permute-start | bytes 12296 | tf_op jit(solution)/shard_map/ppermute | solution.py:506
  77.1 0.6 collective-permute-start.14
  77.8 0.4 collective-permute-start.13
  78.2 0.7 collective-permute-start.16
  78.9 0.1 collective-permute-start.17
  79.0 2.3 %scaled_queries.1 = bf16[1,2,128,2048]{3,2,1,0:T(8,128)(2,1)} custom-call(bf16[128,2048]{1,0:T(8,128)(2,1)} %get-tuple-element.90.own_hbm, bf16[128,512]{1,0:T(8,128)(2,1)S(1)} %collective-permute-done.8.refs_0_, bf16[128,512]{1,0:T(8,128)(2,1)S(1)} %collective-permute-done.9.refs_1_, bf16[128,512]{1,0:T(8,128)(2,1)S(1)} %collective-permute-done.10.refs_2_, ...), custom_call_target="tpu_custom_call" | custom-call | flops 524288 | bytes 128 | tf_op jit(solution)/shard_map/scaled_queries/pallas_call | solution.py:418
  81.3 0.5 collective-permute-start.19
  81.8 2.0 %collective-permute-start.18 = (bf16[4,128,128]{2,1,0:T(8,128)(2,1)S(1)}, bf16[4,128,128]{2,1,0:T(8,128)(2,1)S(1)}, u32[]{:S(2)}, u32[]{:S(2)}) collective-permute-start(bf16[4,128,128]{2,1,0:T(8,128)(2,1)S(1)} %bitcast.4), channel_id=1, source_target_pairs={{0,4},{4,0},{1,5},{5,1},{2,6},{6,2},{3,7},{7,3},{8,12},{12,8},{9,1... | collective-permute-start | bytes 393224 | tf_op jit(solution)/shard_map/ppermute | solution.py:473
  83.8 1.0 %collective-permute-done.18.refs_7_ = bf16[4,128,128]{2,1,0:T(8,128)(2,1)S(1)} collective-permute-done((bf16[4,128,128]{2,1,0:T(8,128)(2,1)S(1)}, bf16[4,128,128]{2,1,0:T(8,128)(2,1)S(1)}, u32[]{:S(2)}, u32[]{:S(2)}) %collective-permute-start.18) | collective-permute-done | bytes 131104 | tf_op jit(solution)/shard_map/ppermute | solution.py:473
  84.8 1.2 %final_pass.1 = (bf16[1,2,128,512]{3,2,1,0:T(8,128)(2,1)}, bf16[1,2,128,512]{3,2,1,0:T(8,128)(2,1)}, f32[1,1]{1,0:T(1,128)}) custom-call(bf16[1,2,128,512]{3,2,1,0:T(8,128)(2,1)S(1)} %copy-done.3, bf16[1,2,128,512]{3,2,1,0:T(8,128)(2,1)S(1)} %copy-done.5, f32[2,128,512]{2,1,0:T(8,128)S(1)} %copy-done.13, ...), custom_call_target="tpu_custom_call" | custom-call | flops 67108864 | bytes 3145728 | tf_op jit(solution)/shard_map/final_pass/pallas_call | solution.py:461
  (42 shorter events, 0.2 us)
Async XLA Ops:
  0.6 6.5 %copy-start = (bf16[1,2,128,2048]{3,2,1,0:T(8,128)(2,1)S(1)}, bf16[1,2,128,2048]{3,2,1,0:T(8,128)(2,1)}, u32[]{:S(2)}) copy-start(bf16[1,2,128,2048]{3,2,1,0:T(8,128)(2,1)} %refs_0_.4) | copy-start | bytes 3145732
  0.6 5.8 %collective-permute-start.2 = (bf16[1,2,128,512]{3,2,1,0:T(8,128)(2,1)}, bf16[1,2,128,512]{3,2,1,0:T(8,128)(2,1)S(1)}, u32[]{:S(2)}, u32[]{:S(2)}) collective-permute-start(bf16[1,2,128,512]{3,2,1,0:T(8,128)(2,1)} %refs_5_.1), channel_id=1, source_target_pairs={{0,4},{4,0},{1,5},{5,1},{2,6},{6,2},{3,7},{7,3},{8,12},{12,8},{9,1... | collective-permute-start | bytes 786440 | tf_op jit(solution)/shard_map/ppermute | solution.py:473
  4.0 2.5 %collective-permute-start.3 = (bf16[1,2,128,512]{3,2,1,0:T(8,128)(2,1)}, bf16[1,2,128,512]{3,2,1,0:T(8,128)(2,1)S(1)}, u32[]{:S(2)}, u32[]{:S(2)}) collective-permute-start(bf16[1,2,128,512]{3,2,1,0:T(8,128)(2,1)} %refs_6_.1), channel_id=1, source_target_pairs={{0,4},{4,0},{1,5},{5,1},{2,6},{6,2},{3,7},{7,3},{8,12},{12,8},{9,1... | collective-permute-start | bytes 786440 | tf_op jit(solution)/shard_map/ppermute | solution.py:473
  4.1 2.4 %collective-permute-start = (bf16[1,2,128,512]{3,2,1,0:T(8,128)(2,1)}, bf16[1,2,128,512]{3,2,1,0:T(8,128)(2,1)S(1)}, u32[]{:S(2)}, u32[]{:S(2)}) collective-permute-start(bf16[1,2,128,512]{3,2,1,0:T(8,128)(2,1)} %refs_0_.5), channel_id=1, source_target_pairs={{0,4},{4,0},{1,5},{5,1},{2,6},{6,2},{3,7},{7,3},{8,12},{12,8},{9,1... | collective-permute-start | bytes 786440 | tf_op jit(solution)/shard_map/ppermute | solution.py:473
  4.5 2.0 %collective-permute-start.1 = (bf16[1,2,128,512]{3,2,1,0:T(8,128)(2,1)}, bf16[1,2,128,512]{3,2,1,0:T(8,128)(2,1)S(1)}, u32[]{:S(2)}, u32[]{:S(2)}) collective-permute-start(bf16[1,2,128,512]{3,2,1,0:T(8,128)(2,1)} %refs_1_.6), channel_id=1, source_target_pairs={{0,4},{4,0},{1,5},{5,1},{2,6},{6,2},{3,7},{7,3},{8,12},{12,8},{9,1... | collective-permute-start | bytes 786440 | tf_op jit(solution)/shard_map/ppermute | solution.py:473
  4.6 1.9 %collective-permute-start.4 = (s32[1,2,128]{2,1,0:T(2,128)}, s32[1,2,128]{2,1,0:T(2,128)S(1)}, u32[]{:S(2)}, u32[]{:S(2)}) collective-permute-start(s32[1,2,128]{2,1,0:T(2,128)} %refs_4_.2), channel_id=1, source_target_pairs={{0,4},{4,0},{1,5},{5,1},{2,6},{6,2},{3,7},{7,3},{8,12},{12,8},{9,1... | collective-permute-start | bytes 3080 | tf_op jit(solution)/shard_map/ppermute | solution.py:473
  6.5 37.3 %copy-start.6 = (bf16[1,2,128,512]{3,2,1,0:T(8,128)(2,1)}, bf16[1,2,128,512]{3,2,1,0:T(8,128)(2,1)S(1)}, u32[]{:S(2)}) copy-start(bf16[1,2,128,512]{3,2,1,0:T(8,128)(2,1)S(1)} %collective-permute-done.kp2_ref.refs_11_.refs_4_) | copy-start | bytes 786436
  6.5 37.3 %copy-start.7 = (bf16[1,2,128,512]{3,2,1,0:T(8,128)(2,1)}, bf16[1,2,128,512]{3,2,1,0:T(8,128)(2,1)S(1)}, u32[]{:S(2)}) copy-start(bf16[1,2,128,512]{3,2,1,0:T(8,128)(2,1)S(1)} %collective-permute-done.1.vp2_ref.refs_12_.refs_5_) | copy-start | bytes 786436
  6.5 37.3 %collective-permute-start.6 = (bf16[1,2,128,2048]{3,2,1,0:T(8,128)(2,1)}, bf16[1,2,128,2048]{3,2,1,0:T(8,128)(2,1)S(1)}, u32[]{:S(2)}, u32[]{:S(2)}) collective-permute-start(bf16[1,2,128,2048]{3,2,1,0:T(8,128)(2,1)} %refs_1_.4), channel_id=1, source_target_pairs={{0,4},{4,0},{1,5},{5,1},{2,6},{6,2},{3,7},{7,3},{8,12},{12,8},{9,1... | collective-permute-start | bytes 3145736 | tf_op jit(solution)/shard_map/ppermute | solution.py:473
  7.0 36.8 %collective-permute-start.7 = (bf16[1,2,128,2048]{3,2,1,0:T(8,128)(2,1)}, bf16[1,2,128,2048]{3,2,1,0:T(8,128)(2,1)S(1)}, u32[]{:S(2)}, u32[]{:S(2)}) collective-permute-start(bf16[1,2,128,2048]{3,2,1,0:T(8,128)(2,1)} %refs_2_.3), channel_id=1, source_target_pairs={{0,4},{4,0},{1,5},{5,1},{2,6},{6,2},{3,7},{7,3},{8,12},{12,8},{9,1... | collective-permute-start | bytes 3145736 | tf_op jit(solution)/shard_map/ppermute | solution.py:473
  7.1 36.7 %collective-permute-start.5 = (bf16[1,2,128,2048]{3,2,1,0:T(8,128)(2,1)S(1)}, bf16[1,2,128,2048]{3,2,1,0:T(8,128)(2,1)S(1)}, u32[]{:S(2)}, u32[]{:S(2)}) collective-permute-start(bf16[1,2,128,2048]{3,2,1,0:T(8,128)(2,1)S(1)} %copy-done), channel_id=1, source_target_pairs={{0,4},{4,0},{1,5},{5,1},{2,6},{6,2},{3,7},{7,3},{8,12},{12,8},{9,1... | collective-permute-start | bytes 3145736 | tf_op jit(solution)/shard_map/ppermute | solution.py:473
  7.5 36.4 %copy-start.9 = (bf16[1,2,128,2048]{3,2,1,0:T(8,128)(2,1)S(1)}, bf16[1,2,128,2048]{3,2,1,0:T(8,128)(2,1)}, u32[]{:S(2)}) copy-start(bf16[1,2,128,2048]{3,2,1,0:T(8,128)(2,1)} %refs_2_.3) | copy-start | bytes 3145732
  7.5 36.4 %copy-start.10 = (bf16[1,2,128,512]{3,2,1,0:T(8,128)(2,1)S(1)}, bf16[1,2,128,512]{3,2,1,0:T(8,128)(2,1)}, u32[]{:S(2)}) copy-start(bf16[1,2,128,512]{3,2,1,0:T(8,128)(2,1)} %refs_5_.1) | copy-start | bytes 786436
  7.5 36.4 %copy-start.11 = (bf16[1,2,128,512]{3,2,1,0:T(8,128)(2,1)S(1)}, bf16[1,2,128,512]{3,2,1,0:T(8,128)(2,1)}, u32[]{:S(2)}) copy-start(bf16[1,2,128,512]{3,2,1,0:T(8,128)(2,1)} %refs_6_.1) | copy-start | bytes 786436
  7.8 36.1 %copy-start.8 = (bf16[1,2,128,2048]{3,2,1,0:T(8,128)(2,1)S(1)}, bf16[1,2,128,2048]{3,2,1,0:T(8,128)(2,1)}, u32[]{:S(2)}) copy-start(bf16[1,2,128,2048]{3,2,1,0:T(8,128)(2,1)} %refs_1_.4) | copy-start | bytes 3145732
  28.9 15.0 %copy-start.2 = (bf16[1,2,128,512]{3,2,1,0:T(8,128)(2,1)S(1)}, bf16[1,2,128,512]{3,2,1,0:T(8,128)(2,1)}, u32[]{:S(2)}) copy-start(bf16[1,2,128,512]{3,2,1,0:T(8,128)(2,1)} %refs_0_.5) | copy-start | bytes 786436
  28.9 15.0 %copy-start.4 = (bf16[1,2,128,512]{3,2,1,0:T(8,128)(2,1)S(1)}, bf16[1,2,128,512]{3,2,1,0:T(8,128)(2,1)}, u32[]{:S(2)}) copy-start(bf16[1,2,128,512]{3,2,1,0:T(8,128)(2,1)} %refs_1_.6) | copy-start | bytes 786436
  43.8 5.9 %copy-start.1 = (bf16[1,2,128,2048]{3,2,1,0:T(8,128)(2,1)}, bf16[1,2,128,2048]{3,2,1,0:T(8,128)(2,1)S(1)}, u32[]{:S(2)}) copy-start(bf16[1,2,128,2048]{3,2,1,0:T(8,128)(2,1)S(1)} %collective-permute-done.5.refs_8_.refs_3_) | copy-start | bytes 3145732
  49.7 5.4 %copy-start.12 = (f32[4,128,128]{2,1,0:T(8,128)S(1)}, f32[4,128,128]{2,1,0:T(8,128)}, u32[]{:S(2)}) copy-start(f32[4,128,128]{2,1,0:T(8,128)} %get-tuple-element.88.refs_8_) | copy-start | bytes 786436
  49.7 15.1 %all-to-all-start.2 = ((bf16[32,24,128]{2,1,0:T(8,128)(2,1)}), bf16[32,24,128]{2,1,0:T(8,128)(2,1)S(1)}, u32[]{:S(2)}, u32[]{:S(2)}) async-start(bf16[32,24,128]{2,1,0:T(8,128)(2,1)} %get-tuple-element.68), calls=%async_computation.2 | async-start | bytes 393216 | tf_op jit(solution)/shard_map/all_to_all | solution.py:477
  64.8 9.1 %copy-start.16 = (bf16[128,512]{1,0:T(8,128)(2,1)S(1)}, bf16[128,512]{1,0:T(8,128)(2,1)}, u32[]{:S(2)}) copy-start(bf16[128,512]{1,0:T(8,128)(2,1)} %get-tuple-element.94) | copy-start | bytes 393220
  65.5 12.7 %copy-start.15 = (bf16[128,512]{1,0:T(8,128)(2,1)S(1)}, bf16[128,512]{1,0:T(8,128)(2,1)}, u32[]{:S(2)}) copy-start(bf16[128,512]{1,0:T(8,128)(2,1)} %get-tuple-element.98) | copy-start | bytes 393220
  65.5 13.4 %copy-start.14 = (bf16[128,512]{1,0:T(8,128)(2,1)S(1)}, bf16[128,512]{1,0:T(8,128)(2,1)}, u32[]{:S(2)}) copy-start(bf16[128,512]{1,0:T(8,128)(2,1)} %get-tuple-element.99) | copy-start | bytes 393220
  65.5 16.3 %all-to-all-start.3 = ((bf16[32,16,128]{2,1,0:T(8,128)(2,1)}), bf16[32,16,128]{2,1,0:T(8,128)(2,1)S(1)}, u32[]{:S(2)}, u32[]{:S(2)}) async-start(bf16[32,16,128]{2,1,0:T(8,128)(2,1)} %get-tuple-element.89), calls=%async_computation.3 | async-start | bytes 262144 | tf_op jit(solution)/shard_map/all_to_all | solution.py:477
  70.6 3.7 %collective-permute-start.12 = (f32[8,128]{1,0:T(8,128)S(1)}, f32[8,128]{1,0:T(8,128)S(1)}, u32[]{:S(2)}, u32[]{:S(2)}) collective-permute-start(f32[8,128]{1,0:T(8,128)S(1)} %get-tuple-element.95), channel_id=1, source_target_pairs={{0,4},{4,0},{1,5},{5,1},{2,6},{6,2},{3,7},{7,3},{8,12},{12,8},{9,1... | collective-permute-start | bytes 12296 | tf_op jit(solution)/shard_map/ppermute | solution.py:473
  73.3 3.9 %collective-permute-start.8 = (bf16[128,512]{1,0:T(8,128)(2,1)}, bf16[128,512]{1,0:T(8,128)(2,1)S(1)}, u32[]{:S(2)}, u32[]{:S(2)}) collective-permute-start(bf16[128,512]{1,0:T(8,128)(2,1)} %get-tuple-element.91), channel_id=1, source_target_pairs={{0,4},{4,0},{1,5},{5,1},{2,6},{6,2},{3,7},{7,3},{8,12},{12,8},{9,1... | collective-permute-start | bytes 393224 | tf_op jit(solution)/shard_map/ppermute | solution.py:473
  73.4 4.4 %collective-permute-start.9 = (bf16[128,512]{1,0:T(8,128)(2,1)}, bf16[128,512]{1,0:T(8,128)(2,1)S(1)}, u32[]{:S(2)}, u32[]{:S(2)}) collective-permute-start(bf16[128,512]{1,0:T(8,128)(2,1)} %get-tuple-element.92), channel_id=1, source_target_pairs={{0,4},{4,0},{1,5},{5,1},{2,6},{6,2},{3,7},{7,3},{8,12},{12,8},{9,1... | collective-permute-start | bytes 393224 | tf_op jit(solution)/shard_map/ppermute | solution.py:473
  73.8 4.4 %collective-permute-start.10 = (bf16[128,512]{1,0:T(8,128)(2,1)}, bf16[128,512]{1,0:T(8,128)(2,1)S(1)}, u32[]{:S(2)}, u32[]{:S(2)}) collective-permute-start(bf16[128,512]{1,0:T(8,128)(2,1)} %get-tuple-element.93), channel_id=1, source_target_pairs={{0,4},{4,0},{1,5},{5,1},{2,6},{6,2},{3,7},{7,3},{8,12},{12,8},{9,1... | collective-permute-start | bytes 393224 | tf_op jit(solution)/shard_map/ppermute | solution.py:473
  73.9 5.0 %collective-permute-start.11 = (bf16[128,512]{1,0:T(8,128)(2,1)S(1)}, bf16[128,512]{1,0:T(8,128)(2,1)S(1)}, u32[]{:S(2)}, u32[]{:S(2)}) collective-permute-start(bf16[128,512]{1,0:T(8,128)(2,1)S(1)} %copy-done.16), channel_id=1, source_target_pairs={{0,4},{4,0},{1,5},{5,1},{2,6},{6,2},{3,7},{7,3},{8,12},{12,8},{9,1... | collective-permute-start | bytes 393224 | tf_op jit(solution)/shard_map/ppermute | solution.py:473
  74.3 7.0 %collective-permute-start.15 = (f32[8,128]{1,0:T(8,128)S(1)}, f32[8,128]{1,0:T(8,128)S(1)}, u32[]{:S(2)}, u32[]{:S(2)}) collective-permute-start(f32[8,128]{1,0:T(8,128)S(1)} %get-tuple-element.108.refs_10_), channel_id=1, source_target_pairs={{0,3},{1,2},{2,1},{3,0},{4,7},{5,6},{6,5},{7,4},{8,11},{9,10},{10,... | collective-permute-start | bytes 12296 | tf_op jit(solution)/shard_map/ppermute | solution.py:506
  77.1 4.6 %collective-permute-start.14 = (f32[8,128]{1,0:T(8,128)S(1)}, f32[8,128]{1,0:T(8,128)S(1)}, u32[]{:S(2)}, u32[]{:S(2)}) collective-permute-start(f32[8,128]{1,0:T(8,128)S(1)} %get-tuple-element.108.refs_10_), channel_id=1, source_target_pairs={{0,2},{1,3},{2,0},{3,1},{4,6},{5,7},{6,4},{7,5},{8,10},{9,11},{10,... | collective-permute-start | bytes 12296 | tf_op jit(solution)/shard_map/ppermute | solution.py:506
  77.8 4.0 %collective-permute-start.13 = (f32[8,128]{1,0:T(8,128)S(1)}, f32[8,128]{1,0:T(8,128)S(1)}, u32[]{:S(2)}, u32[]{:S(2)}) collective-permute-start(f32[8,128]{1,0:T(8,128)S(1)} %get-tuple-element.108.refs_10_), channel_id=1, source_target_pairs={{0,1},{1,0},{2,3},{3,2},{4,5},{5,4},{6,7},{7,6},{8,9},{9,8},{10,11... | collective-permute-start | bytes 12296 | tf_op jit(solution)/shard_map/ppermute | solution.py:506
  78.2 5.7 %collective-permute-start.16 = (bf16[128,512]{1,0:T(8,128)(2,1)S(1)}, bf16[128,512]{1,0:T(8,128)(2,1)S(1)}, u32[]{:S(2)}, u32[]{:S(2)}) collective-permute-start(bf16[128,512]{1,0:T(8,128)(2,1)S(1)} %copy-done.15), channel_id=1, source_target_pairs={{0,4},{4,0},{1,5},{5,1},{2,6},{6,2},{3,7},{7,3},{8,12},{12,8},{9,1... | collective-permute-start | bytes 393224 | tf_op jit(solution)/shard_map/ppermute | solution.py:473
  78.9 4.9 %collective-permute-start.17 = (bf16[128,512]{1,0:T(8,128)(2,1)S(1)}, bf16[128,512]{1,0:T(8,128)(2,1)S(1)}, u32[]{:S(2)}, u32[]{:S(2)}) collective-permute-start(bf16[128,512]{1,0:T(8,128)(2,1)S(1)} %copy-done.14), channel_id=1, source_target_pairs={{0,4},{4,0},{1,5},{5,1},{2,6},{6,2},{3,7},{7,3},{8,12},{12,8},{9,1... | collective-permute-start | bytes 393224 | tf_op jit(solution)/shard_map/ppermute | solution.py:473
  79.0 5.8 %copy-start.3 = (bf16[1,2,128,512]{3,2,1,0:T(8,128)(2,1)S(1)}, bf16[1,2,128,512]{3,2,1,0:T(8,128)(2,1)}, u32[]{:S(2)}) copy-start(bf16[1,2,128,512]{3,2,1,0:T(8,128)(2,1)} %refs_0_.5) | copy-start | bytes 786436
  79.0 5.8 %copy-start.5 = (bf16[1,2,128,512]{3,2,1,0:T(8,128)(2,1)S(1)}, bf16[1,2,128,512]{3,2,1,0:T(8,128)(2,1)}, u32[]{:S(2)}) copy-start(bf16[1,2,128,512]{3,2,1,0:T(8,128)(2,1)} %refs_1_.6) | copy-start | bytes 786436
  79.0 5.8 %copy-start.13 = (f32[2,128,512]{2,1,0:T(8,128)S(1)}, f32[2,128,512]{2,1,0:T(8,128)}, u32[]{:S(2)}) copy-start(f32[2,128,512]{2,1,0:T(8,128)} %get-tuple-element.97.refs_2_) | copy-start | bytes 1572868
  81.3 2.6 %collective-permute-start.19 = (bf16[4,128,128]{2,1,0:T(8,128)(2,1)S(1)}, bf16[4,128,128]{2,1,0:T(8,128)(2,1)S(1)}, u32[]{:S(2)}, u32[]{:S(2)}) collective-permute-start(bf16[4,128,128]{2,1,0:T(8,128)(2,1)S(1)} %convert_element_type.3), channel_id=1, source_target_pairs={{0,4},{4,0},{1,5},{5,1},{2,6},{6,2},{3,7},{7,3},{8,12},{12,8},{9,1... | collective-permute-start | bytes 393224 | tf_op jit(solution)/shard_map/ppermute | solution.py:473
  81.8 3.0 %collective-permute-start.18 = (bf16[4,128,128]{2,1,0:T(8,128)(2,1)S(1)}, bf16[4,128,128]{2,1,0:T(8,128)(2,1)S(1)}, u32[]{:S(2)}, u32[]{:S(2)}) collective-permute-start(bf16[4,128,128]{2,1,0:T(8,128)(2,1)S(1)} %bitcast.4), channel_id=1, source_target_pairs={{0,4},{4,0},{1,5},{5,1},{2,6},{6,2},{3,7},{7,3},{8,12},{12,8},{9,1... | collective-permute-start | bytes 393224 | tf_op jit(solution)/shard_map/ppermute | solution.py:473

commit v6 on v5

--- a/solution.py
+++ b/solution.py
@@ -435,7 +435,8 @@
 def final_kernel(*refs):
     k_ref, v_ref, pair_ref, kg2_ref, vg2_ref, weight_ref = refs[:6]
     after_ref, after2_ref, second_ref, second2_ref = refs[6:10]
-    loss_ref, one_ref, two_ref, three_ref, ko_ref, vo_ref, pair_loss_ref = refs[10:]
+    loss_ref, one_ref, two_ref, three_ref, ko_hbm, vo_hbm, pair_loss_ref, ko_ref, vo_ref, sems = refs[10:]
+    leaving = []
     pairs = lax.axis_size("dp")
     loss = ((loss_ref[...] + one_ref[...]) + (two_ref[...] + three_ref[...])) / pairs
     pair_loss_ref[0, 0] = jnp.max(loss)
@@ -452,8 +453,12 @@
             later = jnp.where(core == 0, later + second[g].astype(F32), later).astype(BF16)
             key_grad = key_part[:, span].astype(F32) + dot(v_ref[0, seq, :, span], later, 1, 1)
             value_grad = value_part[:, span].astype(F32) + dot(k_ref[0, seq, :, span], later, 1, 0)
-            ko_ref[0, seq, :, span] = (weight * key_grad).astype(BF16)
-            vo_ref[0, seq, :, span] = (weight * value_grad).astype(BF16)
+            ko_ref[turn, :, span] = (weight * key_grad).astype(BF16)
+            vo_ref[turn, :, span] = (weight * value_grad).astype(BF16)
+        moves = [(ko_ref.at[turn], ko_hbm.at[0, seq]), (vo_ref.at[turn], vo_hbm.at[0, seq])]
+        leaving += staged(moves, sems.at[turn])
+    for copy in leaving:
+        copy.wait()
 
 
 def final_pass(*arrays):
@@ -461,8 +466,9 @@
     return pl.pallas_call(
         final_kernel,
         in_specs=list(out_vmem(14)),
-        out_specs=out_vmem(2) + (pl.BlockSpec(memory_space=pltpu.SMEM),),
+        out_specs=(IN_HBM, IN_HBM, pl.BlockSpec(memory_space=pltpu.SMEM)),
         out_shape=(shape, shape, jax.ShapeDtypeStruct((1, 1), F32)),
+        scratch_shapes=[pltpu.VMEM((2, T, KV_HEADS * D), BF16)] * 2 + [pltpu.SemaphoreType.DMA((2, 2))],
         name="final_pass",
         cost_estimate=pl.CostEstimate(flops=16 * 2 * D * D * T, bytes_accessed=3 << 20, transcendentals=0),
         compiler_params=pltpu.CompilerParams(vmem_limit_bytes=SMALL_VMEM),

time: 86.6 us -> 87 us (level)
  no operation moved by 1% of the time
where the time goes in v6:
time: 87 us; the launch traced here: 86.6 us
  blocking collectives  36 us (41%)
  starting transfers between devices  26.7 us (31%)
  Pallas kernels  17.6 us (20%)
  waiting for transfers between devices  5.23 us (6%)
  between operations  1.05 us (1%)
    all_to_all x2, blocking collectives, exchange(): return lax.all_to_all(x, 'chip', 0, 0, tiled=True)  36 us
    ppermute x17, starting transfers between devices, swap(): return lax.ppermute(x, 'core', SWAP)  12.4 us
    all_to_all x2, starting transfers between devices, exchange(): return lax.all_to_all(x, 'chip', 0, 0, tiled=True)  10.5 us
    pallas_call x1, Pallas kernels, forward_pass(): pl.pallas_call(forward_kernel, in_specs=[in_vmem] * 17, out_specs=(IN_HBM...  5.76 us
    pallas_call x1, Pallas kernels, backward_pass(): pl.pallas_call(backward_kernel, in_specs=[IN_HBM] * 8, out_specs=(IN_HBM,...  5.51 us
    all_to_all x2, waiting for transfers between devices, exchange(): return lax.all_to_all(x, 'chip', 0, 0, tiled=True)  4.13 us
    ppermute x3, starting transfers between devices, shards(): lax.ppermute(loss, 'dp', [(i, i ^ k) for i in range(pairs)])  3.83 us
    pallas_call x1, Pallas kernels, scaled_queries(): pl.pallas_call(scale_kernel, in_specs=[IN_HBM] + [in_vmem] * (GROUP + 1),...  2.26 us
  transfers between devices with their start and end apart: 22, of which 3 were waited for; matrix products, arithmetic and copies ran while one was open for 0% of the time, Pallas kernels for 11%

profile of v6, /device:TPU:1, one launch (start us, length us, event | category | flops | bytes accessed | tf_op | source)
XLA Modules:
  0.0 86.6 jit_solution(15159728954086448366)
XLA Ops:
  0.6 0.0 copy-start
  0.6 3.3 %collective-permute-start.2 = (bf16[1,2,128,512]{3,2,1,0:T(8,128)(2,1)}, bf16[1,2,128,512]{3,2,1,0:T(8,128)(2,1)S(1)}, u32[]{:S(2)}, u32[]{:S(2)}) collective-permute-start(bf16[1,2,128,512]{3,2,1,0:T(8,128)(2,1)} %refs_5_.1), channel_id=1, source_target_pairs={{0,4},{4,0},{1,5},{5,1},{2,6},{6,2},{3,7},{7,3},{8,12},{12,8},{9,1... | collective-permute-start | bytes 786440 | tf_op jit(solution)/shard_map/ppermute | solution.py:479
  4.0 0.1 collective-permute-start.3
  4.1 0.4 collective-permute-start
  4.5 0.1 collective-permute-start.1
  4.6 0.4 collective-permute-start.4
  5.0 1.4 %own_states.1 = (f32[2,4,128,128]{3,2,1,0:T(8,128)S(1)}, s32[1,2,128]{2,1,0:T(2,128)S(1)}) custom-call(bf16[1,2,128,512]{3,2,1,0:T(8,128)(2,1)} %refs_0_.5, bf16[1,2,128,512]{3,2,1,0:T(8,128)(2,1)} %refs_1_.6, bf16[1,2,128,512]{3,2,1,0:T(8,128)(2,1)} %refs_5_.1, bf16[1,2,128,512]{3,2,1,0:T(8,128)(2,1)} %refs_6_.1, s32[1,2,128]{2,1,0:T(2,128)} %refs_4_.2), custom_call_target="tpu_custom_call" | custom-call | flops 33554432 | bytes 1048576 | tf_op jit(solution)/shard_map/own_states/pallas_call | solution.py:67
  6.4 0.1 collective-permute-done.4.refs_15_
  6.5 0.0 collective-permute-done.kp2_ref.refs_11_.refs_4_
  6.5 0.0 copy-start.6
  6.5 0.0 collective-permute-done.1.vp2_ref.refs_12_.refs_5_
  6.5 0.0 copy-start.7
  6.5 0.5 collective-permute-start.6
  7.0 0.1 collective-permute-start.7
  7.1 0.4 collective-permute-start.5
  7.5 0.3 chip_states.1
  7.8 0.0 copy-start.8
  7.8 21.1 %all_to_all.20.x_ref = bf16[32,32,128]{2,1,0:T(8,128)(2,1)S(1)} all-to-all(bf16[32,32,128]{2,1,0:T(8,128)(2,1)S(1)} %chip_states.1), channel_id=1, replica_groups=mesh['chip'=32,'core'=2,'dp'=4] {'chip'}, dimensions={0} | all-to-all | bytes 524288 | tf_op jit(solution)/shard_map/all_to_all | solution.py:483
  28.9 0.0 copy-start.2
  28.9 0.0 copy-start.4
  28.9 14.9 %all_to_all.21 = bf16[32,32,128]{2,1,0:T(8,128)(2,1)S(1)} all-to-all(bf16[32,32,128]{2,1,0:T(8,128)(2,1)S(1)} %exclusive_prefix.1), channel_id=1, replica_groups=mesh['chip'=32,'core'=2,'dp'=4] {'chip'}, dimensions={0} | all-to-all | bytes 524288 | tf_op jit(solution)/shard_map/all_to_all | solution.py:483
  43.8 0.0 collective-permute-done.7.refs_10_
  43.8 0.0 collective-permute-done.5.refs_8_.refs_3_
  43.8 0.0 copy-start.1
  43.9 5.8 %forward_pass.1 = (bf16[2,4,512,128]{3,2,1,0:T(8,128)(2,1)}, bf16[32,24,128]{2,1,0:T(8,128)(2,1)}, f32[4,128,128]{2,1,0:T(8,128)}, bf16[2,4,128,128]{3,2,1,0:T(8,128)(2,1)}) custom-call(bf16[1,2,128,2048]{3,2,1,0:T(8,128)(2,1)S(1)} %copy-done, bf16[1,2,128,2048]{3,2,1,0:T(8,128)(2,1)S(1)} %copy-done.8, bf16[1,2,128,2048]{3,2,1,0:T(8,128)(2,1)S(1)} %copy-done.9, ...), custom_call_target="tpu_custom_call" | custom-call | flops 805306368 | bytes 8388608 | tf_op jit(solution)/shard_map/forward_pass/pallas_call | solution.py:278
  49.7 5.4 %all-to-all-start.2 = ((bf16[32,24,128]{2,1,0:T(8,128)(2,1)}), bf16[32,24,128]{2,1,0:T(8,128)(2,1)S(1)}, u32[]{:S(2)}, u32[]{:S(2)}) async-start(bf16[32,24,128]{2,1,0:T(8,128)(2,1)} %get-tuple-element.68), calls=%async_computation.2 | async-start | bytes 393216 | tf_op jit(solution)/shard_map/all_to_all | solution.py:483
  55.1 5.5 %backward_pass.1 = (bf16[128,2048]{1,0:T(8,128)(2,1)}, f32[2,128,512]{2,1,0:T(8,128)}, bf16[128,512]{1,0:T(8,128)(2,1)}, bf16[128,512]{1,0:T(8,128)(2,1)}, bf16[...) custom-call(bf16[1,2,128,2048]{3,2,1,0:T(8,128)(2,1)} %refs_0_.4, ...), custom_call_target="tpu_custom_call" | custom-call | flops 805306368 | bytes 6291456 | tf_op jit(solution)/shard_map/backward_pass/pallas_call | solution.py:371
  60.7 4.1 %all-to-all-done.2.x_ref = bf16[32,24,128]{2,1,0:T(8,128)(2,1)S(1)} async-done(((bf16[32,24,128]{2,1,0:T(8,128)(2,1)}), bf16[32,24,128]{2,1,0:T(8,128)(2,1)S(1)}, u32[]{:S(2)}, u32[]{:S(2)}) %all-to-all-start.2) | async-done | bytes 196640 | tf_op jit(solution)/shard_map/all_to_all | solution.py:483
  64.8 0.7 exclusive_suffix.1
  65.5 5.1 %all-to-all-start.3 = ((bf16[32,16,128]{2,1,0:T(8,128)(2,1)}), bf16[32,16,128]{2,1,0:T(8,128)(2,1)S(1)}, u32[]{:S(2)}, u32[]{:S(2)}) async-start(bf16[32,16,128]{2,1,0:T(8,128)(2,1)} %get-tuple-element.89), calls=%async_computation.3 | async-start | bytes 262144 | tf_op jit(solution)/shard_map/all_to_all | solution.py:483
  70.6 2.7 %collective-permute-start.12 = (f32[8,128]{1,0:T(8,128)S(1)}, f32[8,128]{1,0:T(8,128)S(1)}, u32[]{:S(2)}, u32[]{:S(2)}) collective-permute-start(f32[8,128]{1,0:T(8,128)S(1)} %get-tuple-element.95), channel_id=1, source_target_pairs={{0,4},{4,0},{1,5},{5,1},{2,6},{6,2},{3,7},{7,3},{8,12},{12,8},{9,1... | collective-permute-start | bytes 12296 | tf_op jit(solution)/shard_map/ppermute | solution.py:479
  73.3 0.1 collective-permute-start.8
  73.4 0.4 collective-permute-start.9
  73.8 0.1 collective-permute-start.10
  73.9 0.4 collective-permute-start.11
  74.3 0.0 collective-permute-done.12
  74.3 2.8 %collective-permute-start.15 = (f32[8,128]{1,0:T(8,128)S(1)}, f32[8,128]{1,0:T(8,128)S(1)}, u32[]{:S(2)}, u32[]{:S(2)}) collective-permute-start(f32[8,128]{1,0:T(8,128)S(1)} %get-tuple-element.108.refs_10_), channel_id=1, source_target_pairs={{0,3},{1,2},{2,1},{3,0},{4,7},{5,6},{6,5},{7,4},{8,11},{9,10},{10,... | collective-permute-start | bytes 12296 | tf_op jit(solution)/shard_map/ppermute | solution.py:512
  77.1 0.6 collective-permute-start.14
  77.7 0.0 collective-permute-done.9.refs_1_
  77.8 0.4 collective-permute-start.13
  78.1 0.0 collective-permute-done.10.refs_2_
  78.2 0.7 collective-permute-start.16
  78.9 0.1 collective-permute-start.17
  79.0 2.3 %scaled_queries.1 = bf16[1,2,128,2048]{3,2,1,0:T(8,128)(2,1)} custom-call(bf16[128,2048]{1,0:T(8,128)(2,1)} %get-tuple-element.90.own_hbm, bf16[128,512]{1,0:T(8,128)(2,1)S(1)} %collective-permute-done.8.refs_0_, bf16[128,512]{1,0:T(8,128)(2,1)S(1)} %collective-permute-done.9.refs_1_, bf16[128,512]{1,0:T(8,128)(2,1)S(1)} %collective-permute-done.10.refs_2_, ...), custom_call_target="tpu_custom_call" | custom-call | flops 524288 | bytes 128 | tf_op jit(solution)/shard_map/scaled_queries/pallas_call | solution.py:418
  81.3 0.5 collective-permute-start.19
  81.8 2.0 %collective-permute-start.18 = (bf16[4,128,128]{2,1,0:T(8,128)(2,1)S(1)}, bf16[4,128,128]{2,1,0:T(8,128)(2,1)S(1)}, u32[]{:S(2)}, u32[]{:S(2)}) collective-permute-start(bf16[4,128,128]{2,1,0:T(8,128)(2,1)S(1)} %bitcast.4), channel_id=1, source_target_pairs={{0,4},{4,0},{1,5},{5,1},{2,6},{6,2},{3,7},{7,3},{8,12},{12,8},{9,1... | collective-permute-start | bytes 393224 | tf_op jit(solution)/shard_map/ppermute | solution.py:479
  83.8 1.0 %collective-permute-done.18.refs_7_ = bf16[4,128,128]{2,1,0:T(8,128)(2,1)S(1)} collective-permute-done((bf16[4,128,128]{2,1,0:T(8,128)(2,1)S(1)}, bf16[4,128,128]{2,1,0:T(8,128)(2,1)S(1)}, u32[]{:S(2)}, u32[]{:S(2)}) %collective-permute-start.18) | collective-permute-done | bytes 131104 | tf_op jit(solution)/shard_map/ppermute | solution.py:479
  84.8 1.6 %final_pass.1 = (bf16[1,2,128,512]{3,2,1,0:T(8,128)(2,1)}, bf16[1,2,128,512]{3,2,1,0:T(8,128)(2,1)}, f32[1,1]{1,0:T(1,128)}) custom-call(bf16[1,2,128,512]{3,2,1,0:T(8,128)(2,1)S(1)} %copy-done.3, bf16[1,2,128,512]{3,2,1,0:T(8,128)(2,1)S(1)} %copy-done.5, f32[2,128,512]{2,1,0:T(8,128)S(1)} %copy-done.13, ...), custom_call_target="tpu_custom_call" | custom-call | flops 67108864 | bytes 3145728 | tf_op jit(solution)/shard_map/final_pass/pallas_call | solution.py:466
  (42 shorter events, 0.2 us)
Async XLA Ops:
  0.6 6.5 %copy-start = (bf16[1,2,128,2048]{3,2,1,0:T(8,128)(2,1)S(1)}, bf16[1,2,128,2048]{3,2,1,0:T(8,128)(2,1)}, u32[]{:S(2)}) copy-start(bf16[1,2,128,2048]{3,2,1,0:T(8,128)(2,1)} %refs_0_.4) | copy-start | bytes 3145732
  0.6 5.8 %collective-permute-start.2 = (bf16[1,2,128,512]{3,2,1,0:T(8,128)(2,1)}, bf16[1,2,128,512]{3,2,1,0:T(8,128)(2,1)S(1)}, u32[]{:S(2)}, u32[]{:S(2)}) collective-permute-start(bf16[1,2,128,512]{3,2,1,0:T(8,128)(2,1)} %refs_5_.1), channel_id=1, source_target_pairs={{0,4},{4,0},{1,5},{5,1},{2,6},{6,2},{3,7},{7,3},{8,12},{12,8},{9,1... | collective-permute-start | bytes 786440 | tf_op jit(solution)/shard_map/ppermute | solution.py:479
  4.0 2.5 %collective-permute-start.3 = (bf16[1,2,128,512]{3,2,1,0:T(8,128)(2,1)}, bf16[1,2,128,512]{3,2,1,0:T(8,128)(2,1)S(1)}, u32[]{:S(2)}, u32[]{:S(2)}) collective-permute-start(bf16[1,2,128,512]{3,2,1,0:T(8,128)(2,1)} %refs_6_.1), channel_id=1, source_target_pairs={{0,4},{4,0},{1,5},{5,1},{2,6},{6,2},{3,7},{7,3},{8,12},{12,8},{9,1... | collective-permute-start | bytes 786440 | tf_op jit(solution)/shard_map/ppermute | solution.py:479
  4.1 2.4 %collective-permute-start = (bf16[1,2,128,512]{3,2,1,0:T(8,128)(2,1)}, bf16[1,2,128,512]{3,2,1,0:T(8,128)(2,1)S(1)}, u32[]{:S(2)}, u32[]{:S(2)}) collective-permute-start(bf16[1,2,128,512]{3,2,1,0:T(8,128)(2,1)} %refs_0_.5), channel_id=1, source_target_pairs={{0,4},{4,0},{1,5},{5,1},{2,6},{6,2},{3,7},{7,3},{8,12},{12,8},{9,1... | collective-permute-start | bytes 786440 | tf_op jit(solution)/shard_map/ppermute | solution.py:479
  4.5 2.0 %collective-permute-start.1 = (bf16[1,2,128,512]{3,2,1,0:T(8,128)(2,1)}, bf16[1,2,128,512]{3,2,1,0:T(8,128)(2,1)S(1)}, u32[]{:S(2)}, u32[]{:S(2)}) collective-permute-start(bf16[1,2,128,512]{3,2,1,0:T(8,128)(2,1)} %refs_1_.6), channel_id=1, source_target_pairs={{0,4},{4,0},{1,5},{5,1},{2,6},{6,2},{3,7},{7,3},{8,12},{12,8},{9,1... | collective-permute-start | bytes 786440 | tf_op jit(solution)/shard_map/ppermute | solution.py:479
  4.6 1.9 %collective-permute-start.4 = (s32[1,2,128]{2,1,0:T(2,128)}, s32[1,2,128]{2,1,0:T(2,128)S(1)}, u32[]{:S(2)}, u32[]{:S(2)}) collective-permute-start(s32[1,2,128]{2,1,0:T(2,128)} %refs_4_.2), channel_id=1, source_target_pairs={{0,4},{4,0},{1,5},{5,1},{2,6},{6,2},{3,7},{7,3},{8,12},{12,8},{9,1... | collective-permute-start | bytes 3080 | tf_op jit(solution)/shard_map/ppermute | solution.py:479
  6.5 37.3 %copy-start.6 = (bf16[1,2,128,512]{3,2,1,0:T(8,128)(2,1)}, bf16[1,2,128,512]{3,2,1,0:T(8,128)(2,1)S(1)}, u32[]{:S(2)}) copy-start(bf16[1,2,128,512]{3,2,1,0:T(8,128)(2,1)S(1)} %collective-permute-done.kp2_ref.refs_11_.refs_4_) | copy-start | bytes 786436
  6.5 37.3 %copy-start.7 = (bf16[1,2,128,512]{3,2,1,0:T(8,128)(2,1)}, bf16[1,2,128,512]{3,2,1,0:T(8,128)(2,1)S(1)}, u32[]{:S(2)}) copy-start(bf16[1,2,128,512]{3,2,1,0:T(8,128)(2,1)S(1)} %collective-permute-done.1.vp2_ref.refs_12_.refs_5_) | copy-start | bytes 786436
  6.5 37.3 %collective-permute-start.6 = (bf16[1,2,128,2048]{3,2,1,0:T(8,128)(2,1)}, bf16[1,2,128,2048]{3,2,1,0:T(8,128)(2,1)S(1)}, u32[]{:S(2)}, u32[]{:S(2)}) collective-permute-start(bf16[1,2,128,2048]{3,2,1,0:T(8,128)(2,1)} %refs_1_.4), channel_id=1, source_target_pairs={{0,4},{4,0},{1,5},{5,1},{2,6},{6,2},{3,7},{7,3},{8,12},{12,8},{9,1... | collective-permute-start | bytes 3145736 | tf_op jit(solution)/shard_map/ppermute | solution.py:479
  7.0 36.8 %collective-permute-start.7 = (bf16[1,2,128,2048]{3,2,1,0:T(8,128)(2,1)}, bf16[1,2,128,2048]{3,2,1,0:T(8,128)(2,1)S(1)}, u32[]{:S(2)}, u32[]{:S(2)}) collective-permute-start(bf16[1,2,128,2048]{3,2,1,0:T(8,128)(2,1)} %refs_2_.3), channel_id=1, source_target_pairs={{0,4},{4,0},{1,5},{5,1},{2,6},{6,2},{3,7},{7,3},{8,12},{12,8},{9,1... | collective-permute-start | bytes 3145736 | tf_op jit(solution)/shard_map/ppermute | solution.py:479
  7.1 36.7 %collective-permute-start.5 = (bf16[1,2,128,2048]{3,2,1,0:T(8,128)(2,1)S(1)}, bf16[1,2,128,2048]{3,2,1,0:T(8,128)(2,1)S(1)}, u32[]{:S(2)}, u32[]{:S(2)}) collective-permute-start(bf16[1,2,128,2048]{3,2,1,0:T(8,128)(2,1)S(1)} %copy-done), channel_id=1, source_target_pairs={{0,4},{4,0},{1,5},{5,1},{2,6},{6,2},{3,7},{7,3},{8,12},{12,8},{9,1... | collective-permute-start | bytes 3145736 | tf_op jit(solution)/shard_map/ppermute | solution.py:479
  7.5 36.4 %copy-start.9 = (bf16[1,2,128,2048]{3,2,1,0:T(8,128)(2,1)S(1)}, bf16[1,2,128,2048]{3,2,1,0:T(8,128)(2,1)}, u32[]{:S(2)}) copy-start(bf16[1,2,128,2048]{3,2,1,0:T(8,128)(2,1)} %refs_2_.3) | copy-start | bytes 3145732
  7.5 36.4 %copy-start.10 = (bf16[1,2,128,512]{3,2,1,0:T(8,128)(2,1)S(1)}, bf16[1,2,128,512]{3,2,1,0:T(8,128)(2,1)}, u32[]{:S(2)}) copy-start(bf16[1,2,128,512]{3,2,1,0:T(8,128)(2,1)} %refs_5_.1) | copy-start | bytes 786436
  7.5 36.4 %copy-start.11 = (bf16[1,2,128,512]{3,2,1,0:T(8,128)(2,1)S(1)}, bf16[1,2,128,512]{3,2,1,0:T(8,128)(2,1)}, u32[]{:S(2)}) copy-start(bf16[1,2,128,512]{3,2,1,0:T(8,128)(2,1)} %refs_6_.1) | copy-start | bytes 786436
  7.8 36.1 %copy-start.8 = (bf16[1,2,128,2048]{3,2,1,0:T(8,128)(2,1)S(1)}, bf16[1,2,128,2048]{3,2,1,0:T(8,128)(2,1)}, u32[]{:S(2)}) copy-start(bf16[1,2,128,2048]{3,2,1,0:T(8,128)(2,1)} %refs_1_.4) | copy-start | bytes 3145732
  28.9 15.0 %copy-start.2 = (bf16[1,2,128,512]{3,2,1,0:T(8,128)(2,1)S(1)}, bf16[1,2,128,512]{3,2,1,0:T(8,128)(2,1)}, u32[]{:S(2)}) copy-start(bf16[1,2,128,512]{3,2,1,0:T(8,128)(2,1)} %refs_0_.5) | copy-start | bytes 786436
  28.9 15.0 %copy-start.4 = (bf16[1,2,128,512]{3,2,1,0:T(8,128)(2,1)S(1)}, bf16[1,2,128,512]{3,2,1,0:T(8,128)(2,1)}, u32[]{:S(2)}) copy-start(bf16[1,2,128,512]{3,2,1,0:T(8,128)(2,1)} %refs_1_.6) | copy-start | bytes 786436
  43.8 5.9 %copy-start.1 = (bf16[1,2,128,2048]{3,2,1,0:T(8,128)(2,1)}, bf16[1,2,128,2048]{3,2,1,0:T(8,128)(2,1)S(1)}, u32[]{:S(2)}) copy-start(bf16[1,2,128,2048]{3,2,1,0:T(8,128)(2,1)S(1)} %collective-permute-done.5.refs_8_.refs_3_) | copy-start | bytes 3145732
  49.7 5.4 %copy-start.12 = (f32[4,128,128]{2,1,0:T(8,128)S(1)}, f32[4,128,128]{2,1,0:T(8,128)}, u32[]{:S(2)}) copy-start(f32[4,128,128]{2,1,0:T(8,128)} %get-tuple-element.88.refs_8_) | copy-start | bytes 786436
  49.7 15.1 %all-to-all-start.2 = ((bf16[32,24,128]{2,1,0:T(8,128)(2,1)}), bf16[32,24,128]{2,1,0:T(8,128)(2,1)S(1)}, u32[]{:S(2)}, u32[]{:S(2)}) async-start(bf16[32,24,128]{2,1,0:T(8,128)(2,1)} %get-tuple-element.68), calls=%async_computation.2 | async-start | bytes 393216 | tf_op jit(solution)/shard_map/all_to_all | solution.py:483
  64.8 9.1 %copy-start.16 = (bf16[128,512]{1,0:T(8,128)(2,1)S(1)}, bf16[128,512]{1,0:T(8,128)(2,1)}, u32[]{:S(2)}) copy-start(bf16[128,512]{1,0:T(8,128)(2,1)} %get-tuple-element.94) | copy-start | bytes 393220
  65.5 12.7 %copy-start.15 = (bf16[128,512]{1,0:T(8,128)(2,1)S(1)}, bf16[128,512]{1,0:T(8,128)(2,1)}, u32[]{:S(2)}) copy-start(bf16[128,512]{1,0:T(8,128)(2,1)} %get-tuple-element.98) | copy-start | bytes 393220
  65.5 13.4 %copy-start.14 = (bf16[128,512]{1,0:T(8,128)(2,1)S(1)}, bf16[128,512]{1,0:T(8,128)(2,1)}, u32[]{:S(2)}) copy-start(bf16[128,512]{1,0:T(8,128)(2,1)} %get-tuple-element.99) | copy-start | bytes 393220
  65.5 16.3 %all-to-all-start.3 = ((bf16[32,16,128]{2,1,0:T(8,128)(2,1)}), bf16[32,16,128]{2,1,0:T(8,128)(2,1)S(1)}, u32[]{:S(2)}, u32[]{:S(2)}) async-start(bf16[32,16,128]{2,1,0:T(8,128)(2,1)} %get-tuple-element.89), calls=%async_computation.3 | async-start | bytes 262144 | tf_op jit(solution)/shard_map/all_to_all | solution.py:483
  70.6 3.7 %collective-permute-start.12 = (f32[8,128]{1,0:T(8,128)S(1)}, f32[8,128]{1,0:T(8,128)S(1)}, u32[]{:S(2)}, u32[]{:S(2)}) collective-permute-start(f32[8,128]{1,0:T(8,128)S(1)} %get-tuple-element.95), channel_id=1, source_target_pairs={{0,4},{4,0},{1,5},{5,1},{2,6},{6,2},{3,7},{7,3},{8,12},{12,8},{9,1... | collective-permute-start | bytes 12296 | tf_op jit(solution)/shard_map/ppermute | solution.py:479
  73.3 3.9 %collective-permute-start.8 = (bf16[128,512]{1,0:T(8,128)(2,1)}, bf16[128,512]{1,0:T(8,128)(2,1)S(1)}, u32[]{:S(2)}, u32[]{:S(2)}) collective-permute-start(bf16[128,512]{1,0:T(8,128)(2,1)} %get-tuple-element.91), channel_id=1, source_target_pairs={{0,4},{4,0},{1,5},{5,1},{2,6},{6,2},{3,7},{7,3},{8,12},{12,8},{9,1... | collective-permute-start | bytes 393224 | tf_op jit(solution)/shard_map/ppermute | solution.py:479
  73.4 4.4 %collective-permute-start.9 = (bf16[128,512]{1,0:T(8,128)(2,1)}, bf16[128,512]{1,0:T(8,128)(2,1)S(1)}, u32[]{:S(2)}, u32[]{:S(2)}) collective-permute-start(bf16[128,512]{1,0:T(8,128)(2,1)} %get-tuple-element.92), channel_id=1, source_target_pairs={{0,4},{4,0},{1,5},{5,1},{2,6},{6,2},{3,7},{7,3},{8,12},{12,8},{9,1... | collective-permute-start | bytes 393224 | tf_op jit(solution)/shard_map/ppermute | solution.py:479
  73.8 4.4 %collective-permute-start.10 = (bf16[128,512]{1,0:T(8,128)(2,1)}, bf16[128,512]{1,0:T(8,128)(2,1)S(1)}, u32[]{:S(2)}, u32[]{:S(2)}) collective-permute-start(bf16[128,512]{1,0:T(8,128)(2,1)} %get-tuple-element.93), channel_id=1, source_target_pairs={{0,4},{4,0},{1,5},{5,1},{2,6},{6,2},{3,7},{7,3},{8,12},{12,8},{9,1... | collective-permute-start | bytes 393224 | tf_op jit(solution)/shard_map/ppermute | solution.py:479
  73.9 5.0 %collective-permute-start.11 = (bf16[128,512]{1,0:T(8,128)(2,1)S(1)}, bf16[128,512]{1,0:T(8,128)(2,1)S(1)}, u32[]{:S(2)}, u32[]{:S(2)}) collective-permute-start(bf16[128,512]{1,0:T(8,128)(2,1)S(1)} %copy-done.16), channel_id=1, source_target_pairs={{0,4},{4,0},{1,5},{5,1},{2,6},{6,2},{3,7},{7,3},{8,12},{12,8},{9,1... | collective-permute-start | bytes 393224 | tf_op jit(solution)/shard_map/ppermute | solution.py:479
  74.3 7.0 %collective-permute-start.15 = (f32[8,128]{1,0:T(8,128)S(1)}, f32[8,128]{1,0:T(8,128)S(1)}, u32[]{:S(2)}, u32[]{:S(2)}) collective-permute-start(f32[8,128]{1,0:T(8,128)S(1)} %get-tuple-element.108.refs_10_), channel_id=1, source_target_pairs={{0,3},{1,2},{2,1},{3,0},{4,7},{5,6},{6,5},{7,4},{8,11},{9,10},{10,... | collective-permute-start | bytes 12296 | tf_op jit(solution)/shard_map/ppermute | solution.py:512
  77.1 4.6 %collective-permute-start.14 = (f32[8,128]{1,0:T(8,128)S(1)}, f32[8,128]{1,0:T(8,128)S(1)}, u32[]{:S(2)}, u32[]{:S(2)}) collective-permute-start(f32[8,128]{1,0:T(8,128)S(1)} %get-tuple-element.108.refs_10_), channel_id=1, source_target_pairs={{0,2},{1,3},{2,0},{3,1},{4,6},{5,7},{6,4},{7,5},{8,10},{9,11},{10,... | collective-permute-start | bytes 12296 | tf_op jit(solution)/shard_map/ppermute | solution.py:512
  77.8 4.0 %collective-permute-start.13 = (f32[8,128]{1,0:T(8,128)S(1)}, f32[8,128]{1,0:T(8,128)S(1)}, u32[]{:S(2)}, u32[]{:S(2)}) collective-permute-start(f32[8,128]{1,0:T(8,128)S(1)} %get-tuple-element.108.refs_10_), channel_id=1, source_target_pairs={{0,1},{1,0},{2,3},{3,2},{4,5},{5,4},{6,7},{7,6},{8,9},{9,8},{10,11... | collective-permute-start | bytes 12296 | tf_op jit(solution)/shard_map/ppermute | solution.py:512
  78.2 5.7 %collective-permute-start.16 = (bf16[128,512]{1,0:T(8,128)(2,1)S(1)}, bf16[128,512]{1,0:T(8,128)(2,1)S(1)}, u32[]{:S(2)}, u32[]{:S(2)}) collective-permute-start(bf16[128,512]{1,0:T(8,128)(2,1)S(1)} %copy-done.15), channel_id=1, source_target_pairs={{0,4},{4,0},{1,5},{5,1},{2,6},{6,2},{3,7},{7,3},{8,12},{12,8},{9,1... | collective-permute-start | bytes 393224 | tf_op jit(solution)/shard_map/ppermute | solution.py:479
  78.9 4.9 %collective-permute-start.17 = (bf16[128,512]{1,0:T(8,128)(2,1)S(1)}, bf16[128,512]{1,0:T(8,128)(2,1)S(1)}, u32[]{:S(2)}, u32[]{:S(2)}) collective-permute-start(bf16[128,512]{1,0:T(8,128)(2,1)S(1)} %copy-done.14), channel_id=1, source_target_pairs={{0,4},{4,0},{1,5},{5,1},{2,6},{6,2},{3,7},{7,3},{8,12},{12,8},{9,1... | collective-permute-start | bytes 393224 | tf_op jit(solution)/shard_map/ppermute | solution.py:479
  79.0 5.8 %copy-start.3 = (bf16[1,2,128,512]{3,2,1,0:T(8,128)(2,1)S(1)}, bf16[1,2,128,512]{3,2,1,0:T(8,128)(2,1)}, u32[]{:S(2)}) copy-start(bf16[1,2,128,512]{3,2,1,0:T(8,128)(2,1)} %refs_0_.5) | copy-start | bytes 786436
  79.0 5.8 %copy-start.5 = (bf16[1,2,128,512]{3,2,1,0:T(8,128)(2,1)S(1)}, bf16[1,2,128,512]{3,2,1,0:T(8,128)(2,1)}, u32[]{:S(2)}) copy-start(bf16[1,2,128,512]{3,2,1,0:T(8,128)(2,1)} %refs_1_.6) | copy-start | bytes 786436
  79.0 5.8 %copy-start.13 = (f32[2,128,512]{2,1,0:T(8,128)S(1)}, f32[2,128,512]{2,1,0:T(8,128)}, u32[]{:S(2)}) copy-start(f32[2,128,512]{2,1,0:T(8,128)} %get-tuple-element.97.refs_2_) | copy-start | bytes 1572868
  81.3 2.6 %collective-permute-start.19 = (bf16[4,128,128]{2,1,0:T(8,128)(2,1)S(1)}, bf16[4,128,128]{2,1,0:T(8,128)(2,1)S(1)}, u32[]{:S(2)}, u32[]{:S(2)}) collective-permute-start(bf16[4,128,128]{2,1,0:T(8,128)(2,1)S(1)} %convert_element_type.3), channel_id=1, source_target_pairs={{0,4},{4,0},{1,5},{5,1},{2,6},{6,2},{3,7},{7,3},{8,12},{12,8},{9,1... | collective-permute-start | bytes 393224 | tf_op jit(solution)/shard_map/ppermute | solution.py:479
  81.8 3.0 %collective-permute-start.18 = (bf16[4,128,128]{2,1,0:T(8,128)(2,1)S(1)}, bf16[4,128,128]{2,1,0:T(8,128)(2,1)S(1)}, u32[]{:S(2)}, u32[]{:S(2)}) collective-permute-start(bf16[4,128,128]{2,1,0:T(8,128)(2,1)S(1)} %bitcast.4), channel_id=1, source_target_pairs={{0,4},{4,0},{1,5},{5,1},{2,6},{6,2},{3,7},{7,3},{8,12},{12,8},{9,1... | collective-permute-start | bytes 393224 | tf_op jit(solution)/shard_map/ppermute | solution.py:479
